TPU v7x, 128 devices: a whole 4x4x4 slice. The times are simulated.
128 devices in a mesh: src: 32 (over x, z, core), tgt: 4 (over y).
Axes of the slice: x: 4, y: 4, z: 4, core: 2. Of those that a mesh axis runs over, the one named last changes fastest.
Arguments:
- features: bfloat16 [65536, 1024], P('src', 'tgt'), may hold values from -6 to 6
- cites_tiles: bfloat16 [6144, 128, 128], P('src'), may hold values from -0.0546875 to 0.0546875
- cites_targets: int32 [6144], P('src'), may hold values from 0 to 31
- cites_sources: int32 [6144], P('src'), may hold values from 0 to 15
- cites_counts: int32 [32], P('src'), may hold values from 1 to 192, 3072 in all
- writes_tiles: bfloat16 [3072, 128, 128], P('src'), may hold values from -0.078125 to 0.078125
- writes_targets: int32 [3072], P('src'), may hold values from 0 to 31
- writes_sources: int32 [3072], P('src'), may hold values from 0 to 15
- writes_counts: int32 [32], P('src'), may hold values from 1 to 96, 1536 in all
- topic_tiles: bfloat16 [1536, 128, 128], P('src'), may hold values from -0.109375 to 0.109375
- topic_targets: int32 [1536], P('src'), may hold values from 0 to 31
- topic_sources: int32 [1536], P('src'), may hold values from 0 to 15
- topic_counts: int32 [32], P('src'), may hold values from 1 to 48, 768 in all
- owner_map: int32 [32], replicated, may hold values from 0 to 31, each once
- weights: bfloat16 [3, 1024, 1024], P(None, 'tgt'), may hold values from -0.1875 to 0.1875
- bias_row: bfloat16 [1024], P('tgt'), may hold values from -3 to 3
- cotangent: bfloat16 [4096, 1024], P('src', 'tgt'), may hold values from -6 to 6
Outputs:
- mixed_out: bfloat16 [4096, 1024], P('src', 'tgt')
- grad_weight: float32 [3, 1024, 1024], P(None, 'tgt', 'src')
- grad_source: bfloat16 [65536, 1024], P('src', 'tgt')
Inputs may be any that keep to these rules, and one draw needn't show every extreme that they name: `cites_targets`: target block of a slot; only live slots are read. `cites_sources`: source block within the slot's own partition. `cites_counts`: live slots come first in each partition's 192 slots; they sum to 3072. `writes_targets`: target block of a slot; only live slots are read. `writes_sources`: source block within the slot's own partition. `writes_counts`: live slots come first in each partition's 96 slots; they sum to 1536. `topic_targets`: target block of a slot; only live slots are read. `topic_sources`: source block within the slot's own partition. `topic_counts`: live slots come first in each partition's 48 slots; they sum to 768. `owner_map`: A permutation of the target blocks.
All inputs are finite; a program needn't handle non-finite values.
Results may differ from a plain program's by a relative error of at most 0.015.
Values may be sent and summed in bfloat16 or wider, within the bound.
No kernel may reach another device: no remote copies, remote signals or barrier semaphores. Data moves between devices by JAX's collectives and lax.ppermute only.
A program may use at most 128 MiB of HBM per device.

v0:
```python
import functools

import jax
import jax.numpy as jnp
from jax import lax
from jax.experimental import pallas as pl
from jax.experimental.pallas import tpu as pltpu
from jax.sharding import PartitionSpec as P


TILE = 128
SIDE = 4
GROUP = 16
PAIRS = 16
BF16 = jnp.bfloat16
F32 = jnp.float32
MIB = 1024 * 1024
GATHER_LIMIT = 36 * MIB
SPREAD_LIMIT = 26 * MIB
barrier = lax.optimization_barrier


def spec(space):
    return pl.BlockSpec(memory_space=space)


ANY, SMEM, VMEM = pl.ANY, pltpu.SMEM, pltpu.VMEM


def here():
    s = lax.axis_index("src")
    return s >> 3, (s >> 1) & 3, s & 1


def place_of(slot, mine):
    c = slot & 1
    dx = ((slot >> 3) - mine[0]) & 3
    dz = ((slot >> 1) - mine[1]) & 3
    first = jnp.where(c == 0, dx, dz)
    second = jnp.where(c == 0, dz, dx)
    return first, second, c ^ mine[2]


def live_parts(counts):
    parts = [(count[0] + GROUP - 1) // GROUP for count in counts]
    return parts, [0, parts[0], parts[0] + parts[1], parts[0] + parts[1] + parts[2]]


def start_tiles(tiles, counts, buffer, sems):
    parts, begins = live_parts(counts)
    for number in range(3):
        def step(part, carry, number=number):
            at = begins[number] + part
            pltpu.make_async_copy(
                tiles[number].at[pl.ds(part * GROUP, GROUP)],
                buffer.at[pl.ds(at * GROUP, GROUP)],
                sems.at[at],
            ).start()
            return carry

        lax.fori_loop(0, parts[number], step, 0)
    return begins


def wait_tiles(tile, buffer, sems, waited, needed):
    def step(at, carry):
        pltpu.make_async_copy(
            tile.at[pl.ds(0, GROUP)], buffer.at[pl.ds(at * GROUP, GROUP)], sems.at[at]
        ).wait()
        return carry

    lax.fori_loop(waited, needed, step, 0)
    return jnp.maximum(waited, needed)


def clear(total, amount):
    def step(block, carry):
        total[block] = jnp.zeros(total.shape[1:], F32)
        return carry

    lax.fori_loop(0, amount, step, 0)


def gather_kernel(
    owner_map,
    targets0, targets1, targets2, sources0, sources1, sources2, counts0, counts1, counts2,
    features, tiles0, tiles1, tiles2,
    keep, send,
    buffer, held, total, staged, table, tile_sems, out_sems, feature_sem,
):
    targets, sources = (targets0, targets1, targets2), (sources0, sources1, sources2)
    counts, tiles = (counts0, counts1, counts2), (tiles0, tiles1, tiles2)
    feature_copy = pltpu.make_async_copy(features, held, feature_sem)
    feature_copy.start()
    begins = start_tiles(tiles, counts, buffer, tile_sems)
    mine = here()

    def fill(slot, carry):
        first, second, away = place_of(slot, mine)
        table[owner_map[slot]] = (away * 16 + first * SIDE + second) * 3
        for number in range(3):
            total[slot * 3 + number] = jnp.zeros(total.shape[1:], F32)
        return carry

    lax.fori_loop(0, 32, fill, 0)
    feature_copy.wait()

    for number in range(3):
        def add_group(group, carry, number=number):
            at = begins[number] + group
            wait_tiles(tiles[0], buffer, tile_sems, at, at + 1)
            products = []
            for lane in range(GROUP):
                source = sources[number][group * GROUP + lane]
                products.append(
                    jnp.dot(
                        buffer[at * GROUP + lane], held[source], preferred_element_type=F32
                    )
                )
            for lane in range(GROUP):
                j = group * GROUP + lane
                spot = jnp.where(j < counts[number][0], table[targets[number][j]] + number, 96)
                total[spot] += products[lane]
            return carry

        lax.fori_loop(0, (counts[number][0] + GROUP - 1) // GROUP, add_group, 0)

    def out_copy(where, spot):
        target = keep if where == 0 else send
        return pltpu.make_async_copy(
            staged.at[where * 16 + spot], target.at[spot], out_sems.at[where * 16 + spot]
        )

    for where in (1, 0):
        def emit(spot, carry, where=where):
            block = where * 16 + spot
            for number in range(3):
                staged[block, pl.ds(number * TILE, TILE), :] = total[block * 3 + number].astype(
                    BF16
                )
            out_copy(where, spot).start()
            return carry

        lax.fori_loop(0, 16, emit, 0)
    for where in (1, 0):
        def finish(spot, carry, where=where):
            out_copy(where, spot).wait()
            return carry

        lax.fori_loop(0, 16, finish, 0)


def in_hbm(value):
    return pltpu.with_memory_space_constraint(value, pltpu.HBM)


def flat_args(owner_map, relations):
    return (
        in_hbm(owner_map),
        *[in_hbm(relation[1]) for relation in relations],
        *[in_hbm(relation[2]) for relation in relations],
        *[relation[3] for relation in relations],
    )


def tile_args(relations):
    return [in_hbm(relation[0]) for relation in relations]


def gather_sums(owner_map, relations, features):
    width = features.shape[-1]
    slots = sum(relation[0].shape[0] for relation in relations)
    blocks = jax.ShapeDtypeStruct((16, 3 * TILE, width), BF16)
    features = features.reshape(-1, TILE, width)
    return pl.pallas_call(
        gather_kernel,
        out_shape=(blocks, blocks),
        in_specs=[spec(SMEM)] * 10 + [spec(ANY)] * 4,
        out_specs=(spec(ANY), spec(ANY)),
        scratch_shapes=[
            pltpu.VMEM((slots, TILE, TILE), BF16),
            pltpu.VMEM(features.shape, BF16),
            pltpu.VMEM((97, TILE, width), F32),
            pltpu.VMEM((32, 3 * TILE, width), BF16),
            pltpu.SMEM((32,), jnp.int32),
            pltpu.SemaphoreType.DMA((slots // GROUP,)),
            pltpu.SemaphoreType.DMA((32,)),
            pltpu.SemaphoreType.DMA(()),
        ],
        compiler_params=pltpu.CompilerParams(vmem_limit_bytes=GATHER_LIMIT),
        cost_estimate=pl.CostEstimate(
            flops=3 * 10**9, bytes_accessed=18 * 10**6, transcendentals=0
        ),
        name="gather_sums",
    )(*flat_args(owner_map, relations), in_hbm(features), *tile_args(relations))


def plan_kernel(
    owner_map,
    targets0, targets1, targets2, sources0, sources1, sources2, counts0, counts1, counts2,
    pair_a, pair_b, pair_spot, amount,
    table, pending,
    *, blank,
):
    targets, sources = (targets0, targets1, targets2), (sources0, sources1, sources2)
    counts = (counts0, counts1, counts2)
    begins = live_parts(counts)[1]
    mine = here()

    def fill(slot, carry):
        first, second, away = place_of(slot, mine)
        table[owner_map[slot]] = (away * 16 + second * SIDE + first) * 3
        return carry

    lax.fori_loop(0, 32, fill, 0)
    for spot in range(17):
        pending[spot] = -1

    def put(found, a, b, spot, yes):
        pair_a[found] = a
        pair_b[found] = b
        pair_spot[found] = spot
        return found + jnp.where(yes, 1, 0)

    found = jnp.int32(0)
    for number in range(3):
        def match(group, found, number=number):
            for lane in range(GROUP):
                j = group * GROUP + lane
                live = j < counts[number][0]
                code = begins[number] * GROUP + j + (table[targets[number][j]] + number) * 1024
                spot = jnp.where(live, sources[number][j], 16)
                waiting = pending[spot]
                hit = live & (waiting >= 0)
                found = put(found, waiting, code, spot, hit)
                pending[spot] = jnp.where(hit, -1, code)
            return found

        found = lax.fori_loop(0, (counts[number][0] + GROUP - 1) // GROUP, match, found)
    for spot in range(16):
        found = put(found, pending[spot], blank, spot, pending[spot] >= 0)
    for lane in range(PAIRS):
        put(found + lane, blank, blank, 16, False)
    amount[0] = found


def plan_spread(owner_map, relations):
    slots = sum(relation[0].shape[0] for relation in relations)
    pairs = jax.ShapeDtypeStruct((slots // 2 + 16 + 2 * PAIRS,), jnp.int32)
    return pl.pallas_call(
        functools.partial(plan_kernel, blank=slots),
        out_shape=(pairs, pairs, pairs, jax.ShapeDtypeStruct((1,), jnp.int32)),
        in_specs=[spec(SMEM)] * 10,
        out_specs=tuple([spec(SMEM)] * 4),
        scratch_shapes=[pltpu.SMEM((32,), jnp.int32), pltpu.SMEM((17,), jnp.int32)],
        compiler_params=pltpu.CompilerParams(vmem_limit_bytes=MIB),
        cost_estimate=pl.CostEstimate(flops=10**9, bytes_accessed=10**6, transcendentals=0),
        name="plan_spread",
    )(*flat_args(owner_map, relations))


PLACES = (0, 8, 12, 4, 16, 24, 28, 20)


def spread_kernel(pair_a, pair_b, pair_spot, amount, *refs):
    counts, tiles, pieces, refs = refs[:3], refs[3:6], refs[6:14], refs[14:]
    out, buffer, messages, total, tile_sems, in_sems = refs
    begins = start_tiles(tiles, counts, buffer, tile_sems)
    copies = [
        pltpu.make_async_copy(piece, messages.at[pl.ds(at * 3, 12)], in_sems.at[number])
        for number, (piece, at) in enumerate(zip(pieces, PLACES))
    ]
    for copy in copies:
        copy.start()
    blank = buffer.shape[0] - 1
    buffer[blank] = jnp.zeros((TILE, TILE), BF16)
    clear(total, 16)
    for copy in copies:
        copy.wait()

    def add_group(group, waited):
        at = group * PAIRS
        needed = jnp.minimum(((pair_b[at + PAIRS - 1] & 1023) >> 4) + 1, begins[3])
        waited = wait_tiles(tiles[0], buffer, tile_sems, waited, needed)
        products = []
        for lane in range(PAIRS):
            marks = (pair_a[at + lane], pair_b[at + lane])
            tile = jnp.concatenate([buffer[mark & 1023] for mark in marks], axis=0)
            block = jnp.concatenate([messages[mark >> 10] for mark in marks], axis=0)
            products.append(
                lax.dot_general(
                    tile, block, (((0,), (0,)), ((), ())), preferred_element_type=F32
                )
            )
        for lane in range(PAIRS):
            total[pair_spot[at + lane]] += products[lane]
        return waited

    waited = lax.fori_loop(0, (amount[0] + PAIRS - 1) // PAIRS, add_group, jnp.int32(0))
    wait_tiles(tiles[0], buffer, tile_sems, waited, begins[3])

    def emit(block, carry):
        out[block] = total[block].astype(out.dtype)
        return carry

    lax.fori_loop(0, 16, emit, 0)


def spread_sums(plan, relations, pieces):
    width = pieces[0].shape[-1]
    slots = sum(relation[0].shape[0] for relation in relations)
    return pl.pallas_call(
        spread_kernel,
        out_shape=jax.ShapeDtypeStruct((16, TILE, width), BF16),
        in_specs=[spec(SMEM)] * 7 + [spec(ANY)] * 11,
        out_specs=spec(VMEM),
        scratch_shapes=[
            pltpu.VMEM((slots + 1, TILE, TILE), BF16),
            pltpu.VMEM((96, TILE, width), BF16),
            pltpu.VMEM((17, TILE, width), F32),
            pltpu.SemaphoreType.DMA((slots // GROUP,)),
            pltpu.SemaphoreType.DMA((8,)),
        ],
        compiler_params=pltpu.CompilerParams(vmem_limit_bytes=SPREAD_LIMIT),
        cost_estimate=pl.CostEstimate(
            flops=3 * 10**9, bytes_accessed=18 * 10**6, transcendentals=0
        ),
        name="spread_sums",
    )(
        *plan,
        *[relation[3] for relation in relations],
        *tile_args(relations),
        *pieces,
    )


def columns_at(step, width):
    column = (lax.axis_index("tgt") + step) % SIDE
    return pl.ds(pl.multiple_of(column * width, width), width)


def hidden_kernel(part0, part1, part2, part3, weights, rounded, terms0, terms1, terms2, terms3):
    width = part0.shape[1]
    whole = part0[...].astype(F32)
    for part in (part1, part2, part3):
        whole = whole + part[...].astype(F32)
    whole = whole.astype(BF16)
    rounded[...] = whole
    for step, terms in ((2, terms2), (1, terms1), (3, terms3), (0, terms0)):
        value = jnp.zeros(terms.shape, F32)
        for number in range(3):
            value += jnp.dot(
                whole[number * TILE:(number + 1) * TILE],
                weights[number, :, columns_at(step, width)],
                preferred_element_type=F32,
            )
        terms[...] = value.astype(terms.dtype)


def hidden_terms(parts, weights):
    width = parts[0].shape[1]
    return pl.pallas_call(
        hidden_kernel,
        out_shape=(
            jax.ShapeDtypeStruct((3 * TILE, width), BF16),
            jax.ShapeDtypeStruct((TILE, width), F32),
            jax.ShapeDtypeStruct((TILE, width), BF16),
            jax.ShapeDtypeStruct((TILE, width), BF16),
            jax.ShapeDtypeStruct((TILE, width), BF16),
        ),
        in_specs=[spec(VMEM)] * 5,
        out_specs=tuple([spec(VMEM)] * 5),
        compiler_params=pltpu.CompilerParams(vmem_limit_bytes=8 * MIB),
        name="hidden_terms",
    )(*parts, weights)


def message_kernel(grad0, grad1, grad2, grad3, weights, messages):
    width = grad0.shape[1]
    for number in range(3):
        value = jnp.zeros((TILE, width), F32)
        for step, grad in enumerate((grad0, grad1, grad2, grad3)):
            value += lax.dot_general(
                grad[...],
                weights[number, :, columns_at(step, width)],
                (((1,), (1,)), ((), ())),
                preferred_element_type=F32,
            )
        messages[number] = value.astype(BF16)


def form_messages(grads, weights):
    width = grads[0].shape[1]
    return pl.pallas_call(
        message_kernel,
        out_shape=jax.ShapeDtypeStruct((3, TILE, width), BF16),
        in_specs=[spec(VMEM)] * 5,
        out_specs=spec(VMEM),
        compiler_params=pltpu.CompilerParams(vmem_limit_bytes=8 * MIB),
        name="form_messages",
    )(*grads, weights)


def weight_kernel(grad0, grad1, grad2, grad3, rounded, keep, send, staged, sems):
    mine = here()
    block0 = lax.axis_index("tgt")
    values = jnp.concatenate(
        [rounded[number * TILE:(number + 1) * TILE, :] for number in range(3)], axis=1
    )
    for step, grad in enumerate((grad0, grad1, grad2, grad3)):
        turned = grad[...].astype(F32).T.astype(BF16)
        block = (block0 + step) % SIDE
        for part in range(8):
            first, second, away = place_of(block * 8 + part, mine)
            spot = away * 16 + second * SIDE + first
            value = jnp.dot(
                turned[part * 32:(part + 1) * 32], values, preferred_element_type=F32
            ).astype(BF16)
            for column in range(values.shape[1] // TILE):
                staged[spot, pl.ds(column * 32, 32), :] = value[
                    :, column * TILE:(column + 1) * TILE
                ]
    copies = [
        pltpu.make_async_copy(staged.at[pl.ds(16, 16)], send, sems.at[0]),
        pltpu.make_async_copy(staged.at[pl.ds(0, 16)], keep, sems.at[1]),
    ]
    for copy in copies:
        copy.start()
    for copy in copies:
        copy.wait()


def weight_terms(grads, rounded):
    width = grads[0].shape[1]
    rows = 32 * 3 * width // TILE
    blocks = jax.ShapeDtypeStruct((16, rows, TILE), BF16)
    return pl.pallas_call(
        weight_kernel,
        out_shape=(blocks, blocks),
        in_specs=[spec(VMEM)] * 5,
        out_specs=(spec(ANY), spec(ANY)),
        scratch_shapes=[
            pltpu.VMEM((32, rows, TILE), BF16),
            pltpu.SemaphoreType.DMA((2,)),
        ],
        compiler_params=pltpu.CompilerParams(vmem_limit_bytes=8 * MIB),
        cost_estimate=pl.CostEstimate(flops=10**9, bytes_accessed=3 * 10**6, transcendentals=0),
        name="weight_terms",
    )(*grads, rounded)


def shift_pairs(step, second):
    pairs = []
    for s in range(32):
        x, z, c = s // 8, (s // 2) % 4, s % 2
        if (c == 0) != second:
            x = (x + step) % SIDE
        else:
            z = (z + step) % SIDE
        pairs.append((s, (x * SIDE + z) * 2 + c))
    return pairs


def shift(value, step, second=False):
    return lax.ppermute(value, "src", shift_pairs(step, second))


def swap(value):
    return lax.ppermute(value, "src", [(s, s ^ 1) for s in range(32)])


def add(*values):
    total = values[0].astype(F32)
    for value in values[1:]:
        total = total + value.astype(F32)
    return total.astype(BF16)


def three_starts(values, second=False):
    arrived = []
    for k in (2, 1, 3):
        arrived.append(shift(values[k], k if k < 3 else -1, second))
    return tuple(arrived)


def three_ways(values, second=False):
    return barrier(three_starts(values, second))


def turn(value, step):
    return lax.ppermute(value, "tgt", [(t, (t + step) % SIDE) for t in range(SIDE)])


def shards(
    features,
    cites_tiles,
    cites_targets,
    cites_sources,
    cites_counts,
    writes_tiles,
    writes_targets,
    writes_sources,
    writes_counts,
    topic_tiles,
    topic_targets,
    topic_sources,
    topic_counts,
    owner_map,
    weights,
    bias_row,
    cotangent,
):
    width = features.shape[1]
    relations = (
        (cites_tiles, cites_targets, cites_sources, cites_counts),
        (writes_tiles, writes_targets, writes_sources, writes_counts),
        (topic_tiles, topic_targets, topic_sources, topic_counts),
    )
    keep, send = gather_sums(owner_map, relations, features)
    got = swap(send)
    quarters = [add(keep[4 * k:4 * k + 4], got[4 * k:4 * k + 4]) for k in range(4)]
    owner_map, *quarters = barrier((owner_map, *quarters))
    arrived = three_ways(quarters)
    plan = plan_spread(owner_map, relations)
    *plan, a0, a1, a2 = barrier((*plan, *arrived))
    line = [add(quarters[0][k], *[part[k] for part in (a0, a1, a2)]) for k in range(4)]
    parts = (line[0], *three_ways(line, True))

    rounded, terms0, terms1, terms2, terms3 = hidden_terms(parts, weights)
    turned = barrier((turn(terms2, 2), turn(terms1, 1), turn(terms3, 3)))
    hidden = terms0 + bias_row.astype(F32)[None, :]
    for part in turned:
        hidden = hidden + part.astype(F32)
    mixed_out, pullback = jax.vjp(functools.partial(jax.nn.gelu, approximate=True), hidden)
    grad_hidden = pullback(cotangent.astype(F32))[0].astype(BF16)
    two, one, three = barrier(
        (turn(grad_hidden, -2), turn(grad_hidden, -1), turn(grad_hidden, -3))
    )
    grads = [grad_hidden, one, two, three]

    own = form_messages(grads, weights)
    own, *grads = barrier((own, *grads))
    two, three, one = barrier(three_starts((own,) * 4))
    weight_keep, weight_send = weight_terms(grads, rounded)
    weight_got = swap(weight_send)
    quarters = [
        add(weight_keep[4 * k:4 * k + 4], weight_got[4 * k:4 * k + 4]) for k in range(4)
    ]
    arrived = barrier(three_starts(quarters, True))
    whole = jnp.concatenate([own, one, two, three])
    spread_out = three_starts((whole,) * 4, True)
    beside = swap(whole)
    line = [add(quarters[0][k], *[part[k] for part in arrived]) for k in range(4)]
    weight_parts = three_ways(line)
    *spread_out, beside, l0, w0, w1, w2 = barrier((*spread_out, beside, line[0], *weight_parts))
    weight_parts = (w0, w1, w2)
    siblings = [swap(piece) for piece in spread_out]
    grad_source = spread_sums(plan, relations, [whole, *spread_out, beside, *siblings])
    weight_sum = l0.astype(F32)
    for part in weight_parts:
        weight_sum = weight_sum + part.astype(F32)
    grad_weight = weight_sum.reshape(3 * width // TILE, 32, TILE).transpose(0, 2, 1)
    return (
        mixed_out.astype(BF16),
        grad_weight.reshape(3, width, 32),
        grad_source.reshape(-1, width),
    )


def solution(mesh):
    in_specs = (
        P("src", "tgt"),
        P("src", None, None),
        P("src"),
        P("src"),
        P("src"),
        P("src", None, None),
        P("src"),
        P("src"),
        P("src"),
        P("src", None, None),
        P("src"),
        P("src"),
        P("src"),
        P(),
        P(None, "tgt", None),
        P("tgt"),
        P("src", "tgt"),
    )
    out_specs = (P("src", "tgt"), P(None, "tgt", "src"), P("src", "tgt"))

    return jax.shard_map(shards, mesh=mesh, in_specs=in_specs, out_specs=out_specs, check_vma=False)
```

profile of v0, /device:TPU:7, one launch (start us, length us, event | category | flops | bytes accessed | tf_op | source)
XLA Modules:
  0.0 160.4 jit_solution(14405887984621972250)
XLA Ops:
  2.6 21.1 %gather_sums.1 = (bf16[16,384,256]{2,1,0:T(8,128)(2,1)S(1)}, bf16[16,384,256]{2,1,0:T(8,128)(2,1)S(1)}) custom-call(s32[32]{0:T(128)} %owner_map.2, s32[192]{0:T(256)} %targets0.3, s32[96]{0:T(128)} %targets1.3, s32[48]{0:T(128)} %targets2.3, s32[192]{0:T(256)} %sources0.3, s32[96]{0:T(128)} %sources1.3, s32[48]{0:T(128)} %sources2.3, ...), custom_call_target="tpu_custom_call" | custom-call | flops 3000000000 | bytes 18000000 | tf_op jit(solution)/shard_map/gather_sums/pallas_call | solution.py:175
  23.7 5.6 %collective-permute-done = bf16[16,384,256]{2,1,0:T(8,128)(2,1)S(1)} collective-permute-done((bf16[16,384,256]{2,1,0:T(8,128)(2,1)S(1)}, bf16[16,384,256]{2,1,0:T(8,128)(2,1)S(1)}, u32[]{:S(2)}, u32[]{:S(2)}) %collective-permute-start) | collective-permute-done | bytes 3145760 | tf_op jit(solution)/shard_map/ppermute | solution.py:469
  29.4 0.9 add_convert_fusion
  30.4 0.9 collective-permute-start.1
  31.2 3.5 %collective-permute-start.2 = (bf16[4,384,256]{2,1,0:T(8,128)(2,1)S(1)}, bf16[4,384,256]{2,1,0:T(8,128)(2,1)S(1)}, u32[]{:S(2)}, u32[]{:S(2)}) collective-permute-start(bf16[4,384,256]{2,1,0:T(8,128)(2,1)S(1)} %get-tuple-element.71), channel_id=1, source_target_pairs={{0,32},{4,12},{8,40},{12,20},{16,48},{20,28},{24,56},{28,4},{32,64... | collective-permute-start | bytes 2359304 | tf_op jit(solution)/shard_map/ppermute | solution.py:465
  34.8 4.2 %plan_spread.1 = (s32[216]{0:T(256)S(1)}, s32[216]{0:T(256)S(1)}, s32[216]{0:T(256)S(1)}, s32[1]{0:T(128)}) custom-call(s32[32]{0:T(128)} %owner_map.2, s32[192]{0:T(256)} %targets0.3, s32[96]{0:T(128)} %targets1.3, s32[48]{0:T(128)} %targets2.3, s32[192]{0:T(256)} %sources0.3, s32[96]{0:T(128)} %sources1.3, s32[48]{0:T(128)} %sources2.3, ...), custom_call_target="tpu_custom_call" | custom-call | flops 1000000000 | bytes 1000000 | tf_op jit(solution)/shard_map/plan_spread/pallas_call | solution.py:250
  39.0 4.1 %collective-permute-done.1 = bf16[4,384,256]{2,1,0:T(8,128)(2,1)S(1)} collective-permute-done((bf16[4,384,256]{2,1,0:T(8,128)(2,1)S(1)}, bf16[4,384,256]{2,1,0:T(8,128)(2,1)S(1)}, u32[]{:S(2)}, u32[]{:S(2)}) %collective-permute-start.1) | collective-permute-done | bytes 786464 | tf_op jit(solution)/shard_map/ppermute | solution.py:465
  43.1 8.4 %collective-permute-done.2 = bf16[4,384,256]{2,1,0:T(8,128)(2,1)S(1)} collective-permute-done((bf16[4,384,256]{2,1,0:T(8,128)(2,1)S(1)}, bf16[4,384,256]{2,1,0:T(8,128)(2,1)S(1)}, u32[]{:S(2)}, u32[]{:S(2)}) %collective-permute-start.2) | collective-permute-done | bytes 786464 | tf_op jit(solution)/shard_map/ppermute | solution.py:465
  51.5 1.1 collective-permute-done.3
  53.0 0.6 collective-permute-start.4
  53.7 1.5 collective-permute-start.6
  55.1 4.4 %collective-permute-done.4.part1 = bf16[384,256]{1,0:T(8,128)(2,1)S(1)} collective-permute-done((bf16[384,256]{1,0:T(8,128)(2,1)S(1)}, bf16[384,256]{1,0:T(8,128)(2,1)S(1)}, u32[]{:S(2)}, u32[]{:S(2)}) %collective-permute-start.4) | collective-permute-done | bytes 196640 | tf_op jit(solution)/shard_map/ppermute | solution.py:465
  59.5 2.1 %collective-permute-done.6.part3 = bf16[384,256]{1,0:T(8,128)(2,1)S(1)} collective-permute-done((bf16[384,256]{1,0:T(8,128)(2,1)S(1)}, bf16[384,256]{1,0:T(8,128)(2,1)S(1)}, u32[]{:S(2)}, u32[]{:S(2)}) %collective-permute-start.6) | collective-permute-done | bytes 196640 | tf_op jit(solution)/shard_map/ppermute | solution.py:465
  62.0 3.0 %collective-permute-start.7 = (bf16[128,256]{1,0:T(8,128)(2,1)S(1)}, bf16[128,256]{1,0:T(8,128)(2,1)S(1)}, u32[]{:S(2)}, u32[]{:S(2)}) collective-permute-start(bf16[128,256]{1,0:T(8,128)(2,1)S(1)} %get-tuple-element.83), channel_id=1, source_target_pairs={{0,2},{1,3},{2,0},{3,1},{4,6},{5,7},{6,4},{7,5},{8,10},{9,11},{10,... | collective-permute-start | bytes 196616 | tf_op jit(solution)/shard_map/ppermute | solution.py:491
  65.4 2.3 %collective-permute-start.9 = (bf16[128,256]{1,0:T(8,128)(2,1)S(1)}, bf16[128,256]{1,0:T(8,128)(2,1)S(1)}, u32[]{:S(2)}, u32[]{:S(2)}) collective-permute-start(bf16[128,256]{1,0:T(8,128)(2,1)S(1)} %get-tuple-element.85), channel_id=1, source_target_pairs={{0,3},{1,0},{2,1},{3,2},{4,7},{5,4},{6,5},{7,6},{8,11},{9,8},{10,9... | collective-permute-start | bytes 196616 | tf_op jit(solution)/shard_map/ppermute | solution.py:491
  67.7 2.3 %collective-permute-done.8 = bf16[128,256]{1,0:T(8,128)(2,1)S(1)} collective-permute-done((bf16[128,256]{1,0:T(8,128)(2,1)S(1)}, bf16[128,256]{1,0:T(8,128)(2,1)S(1)}, u32[]{:S(2)}, u32[]{:S(2)}) %collective-permute-start.8) | collective-permute-done | bytes 65568 | tf_op jit(solution)/shard_map/ppermute | solution.py:491
  70.0 0.8 fusion.6
  71.3 2.2 %collective-permute-start.11 = (bf16[128,256]{1,0:T(8,128)(2,1)S(1)}, bf16[128,256]{1,0:T(8,128)(2,1)S(1)}, u32[]{:S(2)}, u32[]{:S(2)}) collective-permute-start(bf16[128,256]{1,0:T(8,128)(2,1)S(1)} %get-tuple-element.96.grad0), channel_id=1, source_target_pairs={{0,3},{1,0},{2,1},{3,2},{4,7},{5,4},{6,5},{7,6},{8,11},{9,8},{10,9... | collective-permute-start | bytes 196616 | tf_op jit(solution)/shard_map/ppermute | solution.py:491
  73.5 0.6 collective-permute-start.12
  74.0 1.3 collective-permute-done.10.grad2
  75.4 1.0 collective-permute-done.11.grad1
  76.4 1.4 collective-permute-done.12.grad3
  77.8 0.6 form_messages.1
  78.4 1.1 weight_terms.1
  79.6 4.6 %collective-permute-start.20 = (bf16[16,192,128]{2,1,0:T(8,128)(2,1)S(1)}, bf16[16,192,128]{2,1,0:T(8,128)(2,1)S(1)}, u32[]{:S(2)}, u32[]{:S(2)}) collective-permute-start(bf16[16,192,128]{2,1,0:T(8,128)(2,1)S(1)} %get-tuple-element.102), channel_id=1, source_target_pairs={{0,4},{4,0},{8,12},{12,8},{16,20},{20,16},{24,28},{28,24},{32,36},... | collective-permute-start | bytes 2359304 | tf_op jit(solution)/shard_map/ppermute | solution.py:469
  84.6 2.6 %collective-permute-start.14 = (bf16[3,128,256]{2,1,0:T(8,128)(2,1)S(1)}, bf16[3,128,256]{2,1,0:T(8,128)(2,1)S(1)}, u32[]{:S(2)}, u32[]{:S(2)}) collective-permute-start(bf16[3,128,256]{2,1,0:T(8,128)(2,1)S(1)} %form_messages.1), channel_id=1, source_target_pairs={{0,32},{4,12},{8,40},{12,20},{16,48},{20,28},{24,56},{28,4},{32,64... | collective-permute-start | bytes 589832 | tf_op jit(solution)/shard_map/ppermute | solution.py:465
  87.2 3.3 %collective-permute-done.13 = bf16[3,128,256]{2,1,0:T(8,128)(2,1)S(1)} collective-permute-done((bf16[3,128,256]{2,1,0:T(8,128)(2,1)S(1)}, bf16[3,128,256]{2,1,0:T(8,128)(2,1)S(1)}, u32[]{:S(2)}, u32[]{:S(2)}) %collective-permute-start.13) | collective-permute-done | bytes 196640 | tf_op jit(solution)/shard_map/ppermute | solution.py:465
  90.6 2.1 %collective-permute-done.14 = bf16[3,128,256]{2,1,0:T(8,128)(2,1)S(1)} collective-permute-done((bf16[3,128,256]{2,1,0:T(8,128)(2,1)S(1)}, bf16[3,128,256]{2,1,0:T(8,128)(2,1)S(1)}, u32[]{:S(2)}, u32[]{:S(2)}) %collective-permute-start.14) | collective-permute-done | bytes 196640 | tf_op jit(solution)/shard_map/ppermute | solution.py:465
  92.9 0.8 collective-permute-start.21
  93.8 2.3 %collective-permute-start.16 = (bf16[12,128,256]{2,1,0:T(8,128)(2,1)S(1)}, bf16[12,128,256]{2,1,0:T(8,128)(2,1)S(1)}, u32[]{:S(2)}, u32[]{:S(2)}) collective-permute-start(bf16[12,128,256]{2,1,0:T(8,128)(2,1)S(1)} %constant_dynamic-update-slice_fusion.refs_6_), channel_id=1, source_target_pairs={{0,16},{4,68},{8,24},{12,76},{16,0},{20,84},{24,8},{28,92},{32,48}... | collective-permute-start | bytes 2359304 | tf_op jit(solution)/shard_map/ppermute | solution.py:465
  96.4 1.1 collective-permute-start.18
  97.6 3.2 %collective-permute-start.19 = (bf16[12,128,256]{2,1,0:T(8,128)(2,1)S(1)}, bf16[12,128,256]{2,1,0:T(8,128)(2,1)S(1)}, u32[]{:S(2)}, u32[]{:S(2)}) collective-permute-start(bf16[12,128,256]{2,1,0:T(8,128)(2,1)S(1)} %constant_dynamic-update-slice_fusion.refs_6_), channel_id=1, source_target_pairs={{0,4},{4,0},{8,12},{12,8},{16,20},{20,16},{24,28},{28,24},{32,36},... | collective-permute-start | bytes 2359304 | tf_op jit(solution)/shard_map/ppermute | solution.py:469
  101.2 15.1 %collective-permute-done.22 = bf16[4,192,128]{2,1,0:T(8,128)(2,1)S(1)} collective-permute-done((bf16[4,192,128]{2,1,0:T(8,128)(2,1)S(1)}, bf16[4,192,128]{2,1,0:T(8,128)(2,1)S(1)}, u32[]{:S(2)}, u32[]{:S(2)}) %collective-permute-start.22) | collective-permute-done | bytes 196640 | tf_op jit(solution)/shard_map/ppermute | solution.py:465
  116.3 1.3 collective-permute-start.23
  117.6 4.4 %collective-permute-done.23 = bf16[4,192,128]{2,1,0:T(8,128)(2,1)S(1)} collective-permute-done((bf16[4,192,128]{2,1,0:T(8,128)(2,1)S(1)}, bf16[4,192,128]{2,1,0:T(8,128)(2,1)S(1)}, u32[]{:S(2)}, u32[]{:S(2)}) %collective-permute-start.23) | collective-permute-done | bytes 196640 | tf_op jit(solution)/shard_map/ppermute | solution.py:465
  122.1 0.7 collective-permute-start.24
  122.8 3.9 %collective-permute-done.24 = bf16[192,128]{1,0:T(8,128)(2,1)S(1)} collective-permute-done((bf16[192,128]{1,0:T(8,128)(2,1)S(1)}, bf16[192,128]{1,0:T(8,128)(2,1)S(1)}, u32[]{:S(2)}, u32[]{:S(2)}) %collective-permute-start.24) | collective-permute-done | bytes 49184 | tf_op jit(solution)/shard_map/ppermute | solution.py:465
  126.6 4.4 %collective-permute-done.25 = bf16[192,128]{1,0:T(8,128)(2,1)S(1)} collective-permute-done((bf16[192,128]{1,0:T(8,128)(2,1)S(1)}, bf16[192,128]{1,0:T(8,128)(2,1)S(1)}, u32[]{:S(2)}, u32[]{:S(2)}) %collective-permute-start.25) | collective-permute-done | bytes 49184 | tf_op jit(solution)/shard_map/ppermute | solution.py:465
  131.1 1.1 collective-permute-start.26
  132.2 1.8 %collective-permute-done.26 = bf16[192,128]{1,0:T(8,128)(2,1)S(1)} collective-permute-done((bf16[192,128]{1,0:T(8,128)(2,1)S(1)}, bf16[192,128]{1,0:T(8,128)(2,1)S(1)}, u32[]{:S(2)}, u32[]{:S(2)}) %collective-permute-start.26) | collective-permute-done | bytes 49184 | tf_op jit(solution)/shard_map/ppermute | solution.py:465
  134.1 0.9 copy-done.1
  134.9 6.9 %collective-permute-start.27 = (bf16[12,128,256]{2,1,0:T(8,128)(2,1)S(1)}, bf16[12,128,256]{2,1,0:T(8,128)(2,1)}, u32[]{:S(2)}, u32[]{:S(2)}) collective-permute-start(bf16[12,128,256]{2,1,0:T(8,128)(2,1)S(1)} %collective-permute-done.16.refs_7_), channel_id=1, source_target_pairs={{0,4},{4,0},{8,12},{12,8},{16,20},{20,16},{24,28},{28,24},{32,36},... | collective-permute-start | bytes 2359304 | tf_op jit(solution)/shard_map/ppermute | solution.py:469
  142.5 0.7 copy.21
  143.2 0.7 collective-permute-done.27.refs_11_
  143.9 1.1 collective-permute-done.28.refs_12_
  145.0 1.1 collective-permute-done.29.refs_13_
  146.1 1.1 copy-done.2
  147.2 13.0 %spread_sums.1 = bf16[16,128,256]{2,1,0:T(8,128)(2,1)} custom-call(s32[216]{0:T(256)S(1)} %get-tuple-element.113.pair_a, s32[216]{0:T(256)S(1)} %get-tuple-element.114.pair_b, s32[216]{0:T(256)S(1)} %get-tuple-element.115.pair_spot, s32[1]{0:T(128)} %get-tuple-element.116.amount, s32[1]{0:T(128)S(6)} %copy.27.counts0.refs_0_, s32[1]{0:T(128)S(6)} %copy.28.counts1.refs_1_, ...), custom_call_target="tpu_custom_call" | custom-call | flops 3000000000 | bytes 18000000 | tf_op jit(solution)/shard_map/spread_sums/pallas_call | solution.py:312
  (42 shorter events, 4.1 us)
Async XLA Ops:
  23.7 5.7 %collective-permute-start = (bf16[16,384,256]{2,1,0:T(8,128)(2,1)S(1)}, bf16[16,384,256]{2,1,0:T(8,128)(2,1)S(1)}, u32[]{:S(2)}, u32[]{:S(2)}) collective-permute-start(bf16[16,384,256]{2,1,0:T(8,128)(2,1)S(1)} %get-tuple-element.63), channel_id=1, source_target_pairs={{0,4},{4,0},{8,12},{12,8},{16,20},{20,16},{24,28},{28,24},{32,36},... | collective-permute-start | bytes 9437192 | tf_op jit(solution)/shard_map/ppermute | solution.py:469
  30.4 12.8 %collective-permute-start.1 = (bf16[4,384,256]{2,1,0:T(8,128)(2,1)S(1)}, bf16[4,384,256]{2,1,0:T(8,128)(2,1)S(1)}, u32[]{:S(2)}, u32[]{:S(2)}) collective-permute-start(bf16[4,384,256]{2,1,0:T(8,128)(2,1)S(1)} %get-tuple-element.70), channel_id=1, source_target_pairs={{0,64},{4,20},{8,72},{12,28},{16,80},{20,4},{24,88},{28,12},{32,96... | collective-permute-start | bytes 2359304 | tf_op jit(solution)/shard_map/ppermute | solution.py:465
  31.2 20.3 %collective-permute-start.2 = (bf16[4,384,256]{2,1,0:T(8,128)(2,1)S(1)}, bf16[4,384,256]{2,1,0:T(8,128)(2,1)S(1)}, u32[]{:S(2)}, u32[]{:S(2)}) collective-permute-start(bf16[4,384,256]{2,1,0:T(8,128)(2,1)S(1)} %get-tuple-element.71), channel_id=1, source_target_pairs={{0,32},{4,12},{8,40},{12,20},{16,48},{20,28},{24,56},{28,4},{32,64... | collective-permute-start | bytes 2359304 | tf_op jit(solution)/shard_map/ppermute | solution.py:465
  34.8 17.8 %collective-permute-start.3 = (bf16[4,384,256]{2,1,0:T(8,128)(2,1)S(1)}, bf16[4,384,256]{2,1,0:T(8,128)(2,1)S(1)}, u32[]{:S(2)}, u32[]{:S(2)}) collective-permute-start(bf16[4,384,256]{2,1,0:T(8,128)(2,1)S(1)} %get-tuple-element.72), channel_id=1, source_target_pairs={{0,96},{4,28},{8,104},{12,4},{16,112},{20,12},{24,120},{28,20},{32... | collective-permute-start | bytes 2359304 | tf_op jit(solution)/shard_map/ppermute | solution.py:465
  52.6 8.9 %copy-start = (bf16[3,256,1024]{2,1,0:T(8,128)(2,1)S(1)}, bf16[3,256,1024]{2,1,0:T(8,128)(2,1)}, u32[]{:S(2)}) copy-start(bf16[3,256,1024]{2,1,0:T(8,128)(2,1)} %weights.3) | copy-start | bytes 4718596
  53.0 14.6 %copy-start.4 = (bf16[256]{0:T(256)(128)(2,1)S(1)}, bf16[256]{0:T(256)(128)(2,1)}, u32[]{:S(2)}) copy-start(bf16[256]{0:T(256)(128)(2,1)} %param.32) | copy-start | bytes 1540
  53.0 17.0 %copy-start.3 = (bf16[128,256]{1,0:T(8,128)(2,1)S(1)}, bf16[128,256]{1,0:T(8,128)(2,1)}, u32[]{:S(2)}) copy-start(bf16[128,256]{1,0:T(8,128)(2,1)} %param.33) | copy-start | bytes 196612
  53.0 6.4 %collective-permute-start.4 = (bf16[384,256]{1,0:T(8,128)(2,1)S(1)}, bf16[384,256]{1,0:T(8,128)(2,1)S(1)}, u32[]{:S(2)}, u32[]{:S(2)}) collective-permute-start(bf16[384,256]{1,0:T(8,128)(2,1)S(1)} %get-tuple-element.130), channel_id=1, source_target_pairs={{0,16},{4,68},{8,24},{12,76},{16,0},{20,84},{24,8},{28,92},{32,48}... | collective-permute-start | bytes 589832 | tf_op jit(solution)/shard_map/ppermute | solution.py:465
  53.7 5.8 %collective-permute-start.5 = (bf16[384,256]{1,0:T(8,128)(2,1)S(1)}, bf16[384,256]{1,0:T(8,128)(2,1)S(1)}, u32[]{:S(2)}, u32[]{:S(2)}) collective-permute-start(bf16[384,256]{1,0:T(8,128)(2,1)S(1)} %get-tuple-element.129), channel_id=1, source_target_pairs={{0,8},{4,36},{8,16},{12,44},{16,24},{20,52},{24,0},{28,60},{32,40}... | collective-permute-start | bytes 589832 | tf_op jit(solution)/shard_map/ppermute | solution.py:465
  53.7 7.9 %collective-permute-start.6 = (bf16[384,256]{1,0:T(8,128)(2,1)S(1)}, bf16[384,256]{1,0:T(8,128)(2,1)S(1)}, u32[]{:S(2)}, u32[]{:S(2)}) collective-permute-start(bf16[384,256]{1,0:T(8,128)(2,1)S(1)} %get-tuple-element.128), channel_id=1, source_target_pairs={{0,24},{4,100},{8,0},{12,108},{16,8},{20,116},{24,16},{28,124},{32... | collective-permute-start | bytes 589832 | tf_op jit(solution)/shard_map/ppermute | solution.py:465
  62.0 5.7 %collective-permute-start.7 = (bf16[128,256]{1,0:T(8,128)(2,1)S(1)}, bf16[128,256]{1,0:T(8,128)(2,1)S(1)}, u32[]{:S(2)}, u32[]{:S(2)}) collective-permute-start(bf16[128,256]{1,0:T(8,128)(2,1)S(1)} %get-tuple-element.83), channel_id=1, source_target_pairs={{0,2},{1,3},{2,0},{3,1},{4,6},{5,7},{6,4},{7,5},{8,10},{9,11},{10,... | collective-permute-start | bytes 196616 | tf_op jit(solution)/shard_map/ppermute | solution.py:491
  65.0 5.0 %collective-permute-start.8 = (bf16[128,256]{1,0:T(8,128)(2,1)S(1)}, bf16[128,256]{1,0:T(8,128)(2,1)S(1)}, u32[]{:S(2)}, u32[]{:S(2)}) collective-permute-start(bf16[128,256]{1,0:T(8,128)(2,1)S(1)} %get-tuple-element.84), channel_id=1, source_target_pairs={{0,1},{1,2},{2,3},{3,0},{4,5},{5,6},{6,7},{7,4},{8,9},{9,10},{10,1... | collective-permute-start | bytes 196616 | tf_op jit(solution)/shard_map/ppermute | solution.py:491
  65.4 4.6 %collective-permute-start.9 = (bf16[128,256]{1,0:T(8,128)(2,1)S(1)}, bf16[128,256]{1,0:T(8,128)(2,1)S(1)}, u32[]{:S(2)}, u32[]{:S(2)}) collective-permute-start(bf16[128,256]{1,0:T(8,128)(2,1)S(1)} %get-tuple-element.85), channel_id=1, source_target_pairs={{0,3},{1,0},{2,1},{3,2},{4,7},{5,4},{6,5},{7,6},{8,11},{9,8},{10,9... | collective-permute-start | bytes 196616 | tf_op jit(solution)/shard_map/ppermute | solution.py:491
  70.8 4.6 %collective-permute-start.10 = (bf16[128,256]{1,0:T(8,128)(2,1)S(1)}, bf16[128,256]{1,0:T(8,128)(2,1)S(1)}, u32[]{:S(2)}, u32[]{:S(2)}) collective-permute-start(bf16[128,256]{1,0:T(8,128)(2,1)S(1)} %get-tuple-element.96.grad0), channel_id=1, source_target_pairs={{0,2},{1,3},{2,0},{3,1},{4,6},{5,7},{6,4},{7,5},{8,10},{9,11},{10,... | collective-permute-start | bytes 196616 | tf_op jit(solution)/shard_map/ppermute | solution.py:491
  71.3 5.1 %collective-permute-start.11 = (bf16[128,256]{1,0:T(8,128)(2,1)S(1)}, bf16[128,256]{1,0:T(8,128)(2,1)S(1)}, u32[]{:S(2)}, u32[]{:S(2)}) collective-permute-start(bf16[128,256]{1,0:T(8,128)(2,1)S(1)} %get-tuple-element.96.grad0), channel_id=1, source_target_pairs={{0,3},{1,0},{2,1},{3,2},{4,7},{5,4},{6,5},{7,6},{8,11},{9,8},{10,9... | collective-permute-start | bytes 196616 | tf_op jit(solution)/shard_map/ppermute | solution.py:491
  73.5 4.3 %collective-permute-start.12 = (bf16[128,256]{1,0:T(8,128)(2,1)S(1)}, bf16[128,256]{1,0:T(8,128)(2,1)S(1)}, u32[]{:S(2)}, u32[]{:S(2)}) collective-permute-start(bf16[128,256]{1,0:T(8,128)(2,1)S(1)} %get-tuple-element.96.grad0), channel_id=1, source_target_pairs={{0,1},{1,2},{2,3},{3,0},{4,5},{5,6},{6,7},{7,4},{8,9},{9,10},{10,1... | collective-permute-start | bytes 196616 | tf_op jit(solution)/shard_map/ppermute | solution.py:491
  79.6 13.1 %collective-permute-start.20 = (bf16[16,192,128]{2,1,0:T(8,128)(2,1)S(1)}, bf16[16,192,128]{2,1,0:T(8,128)(2,1)S(1)}, u32[]{:S(2)}, u32[]{:S(2)}) collective-permute-start(bf16[16,192,128]{2,1,0:T(8,128)(2,1)S(1)} %get-tuple-element.102), channel_id=1, source_target_pairs={{0,4},{4,0},{8,12},{12,8},{16,20},{20,16},{24,28},{28,24},{32,36},... | collective-permute-start | bytes 2359304 | tf_op jit(solution)/shard_map/ppermute | solution.py:469
  84.2 6.4 %collective-permute-start.13 = (bf16[3,128,256]{2,1,0:T(8,128)(2,1)S(1)}, bf16[3,128,256]{2,1,0:T(8,128)(2,1)S(1)}, u32[]{:S(2)}, u32[]{:S(2)}) collective-permute-start(bf16[3,128,256]{2,1,0:T(8,128)(2,1)S(1)} %form_messages.1), channel_id=1, source_target_pairs={{0,64},{4,20},{8,72},{12,28},{16,80},{20,4},{24,88},{28,12},{32,96... | collective-permute-start | bytes 589832 | tf_op jit(solution)/shard_map/ppermute | solution.py:465
  84.6 8.1 %collective-permute-start.14 = (bf16[3,128,256]{2,1,0:T(8,128)(2,1)S(1)}, bf16[3,128,256]{2,1,0:T(8,128)(2,1)S(1)}, u32[]{:S(2)}, u32[]{:S(2)}) collective-permute-start(bf16[3,128,256]{2,1,0:T(8,128)(2,1)S(1)} %form_messages.1), channel_id=1, source_target_pairs={{0,32},{4,12},{8,40},{12,20},{16,48},{20,28},{24,56},{28,4},{32,64... | collective-permute-start | bytes 589832 | tf_op jit(solution)/shard_map/ppermute | solution.py:465
  87.2 5.5 %collective-permute-start.15 = (bf16[3,128,256]{2,1,0:T(8,128)(2,1)S(1)}, bf16[3,128,256]{2,1,0:T(8,128)(2,1)S(1)}, u32[]{:S(2)}, u32[]{:S(2)}) collective-permute-start(bf16[3,128,256]{2,1,0:T(8,128)(2,1)S(1)} %form_messages.1), channel_id=1, source_target_pairs={{0,96},{4,28},{8,104},{12,4},{16,112},{20,12},{24,120},{28,20},{32... | collective-permute-start | bytes 589832 | tf_op jit(solution)/shard_map/ppermute | solution.py:465
  92.9 7.9 %collective-permute-start.21 = (bf16[4,192,128]{2,1,0:T(8,128)(2,1)S(1)}, bf16[4,192,128]{2,1,0:T(8,128)(2,1)S(1)}, u32[]{:S(2)}, u32[]{:S(2)}) collective-permute-start(bf16[4,192,128]{2,1,0:T(8,128)(2,1)S(1)} %get-tuple-element.134), channel_id=1, source_target_pairs={{0,16},{4,68},{8,24},{12,76},{16,0},{20,84},{24,8},{28,92},{32,48}... | collective-permute-start | bytes 589832 | tf_op jit(solution)/shard_map/ppermute | solution.py:465
  93.8 40.2 %collective-permute-start.16 = (bf16[12,128,256]{2,1,0:T(8,128)(2,1)S(1)}, bf16[12,128,256]{2,1,0:T(8,128)(2,1)S(1)}, u32[]{:S(2)}, u32[]{:S(2)}) collective-permute-start(bf16[12,128,256]{2,1,0:T(8,128)(2,1)S(1)} %constant_dynamic-update-slice_fusion.refs_6_), channel_id=1, source_target_pairs={{0,16},{4,68},{8,24},{12,76},{16,0},{20,84},{24,8},{28,92},{32,48}... | collective-permute-start | bytes 2359304 | tf_op jit(solution)/shard_map/ppermute | solution.py:465
  96.1 37.9 %collective-permute-start.17 = (bf16[12,128,256]{2,1,0:T(8,128)(2,1)S(1)}, bf16[12,128,256]{2,1,0:T(8,128)(2,1)S(1)}, u32[]{:S(2)}, u32[]{:S(2)}) collective-permute-start(bf16[12,128,256]{2,1,0:T(8,128)(2,1)S(1)} %constant_dynamic-update-slice_fusion.refs_6_), channel_id=1, source_target_pairs={{0,8},{4,36},{8,16},{12,44},{16,24},{20,52},{24,0},{28,60},{32,40}... | collective-permute-start | bytes 2359304 | tf_op jit(solution)/shard_map/ppermute | solution.py:465
  96.4 37.6 %collective-permute-start.18 = (bf16[12,128,256]{2,1,0:T(8,128)(2,1)S(1)}, bf16[12,128,256]{2,1,0:T(8,128)(2,1)S(1)}, u32[]{:S(2)}, u32[]{:S(2)}) collective-permute-start(bf16[12,128,256]{2,1,0:T(8,128)(2,1)S(1)} %constant_dynamic-update-slice_fusion.refs_6_), channel_id=1, source_target_pairs={{0,24},{4,100},{8,0},{12,108},{16,8},{20,116},{24,16},{28,124},{32... | collective-permute-start | bytes 2359304 | tf_op jit(solution)/shard_map/ppermute | solution.py:465
  97.6 36.5 %collective-permute-start.19 = (bf16[12,128,256]{2,1,0:T(8,128)(2,1)S(1)}, bf16[12,128,256]{2,1,0:T(8,128)(2,1)S(1)}, u32[]{:S(2)}, u32[]{:S(2)}) collective-permute-start(bf16[12,128,256]{2,1,0:T(8,128)(2,1)S(1)} %constant_dynamic-update-slice_fusion.refs_6_), channel_id=1, source_target_pairs={{0,4},{4,0},{8,12},{12,8},{16,20},{20,16},{24,28},{28,24},{32,36},... | collective-permute-start | bytes 2359304 | tf_op jit(solution)/shard_map/ppermute | solution.py:469
  100.8 15.4 %collective-permute-start.22 = (bf16[4,192,128]{2,1,0:T(8,128)(2,1)S(1)}, bf16[4,192,128]{2,1,0:T(8,128)(2,1)S(1)}, u32[]{:S(2)}, u32[]{:S(2)}) collective-permute-start(bf16[4,192,128]{2,1,0:T(8,128)(2,1)S(1)} %get-tuple-element.133), channel_id=1, source_target_pairs={{0,8},{4,36},{8,16},{12,44},{16,24},{20,52},{24,0},{28,60},{32,40}... | collective-permute-start | bytes 589832 | tf_op jit(solution)/shard_map/ppermute | solution.py:465
  116.3 5.7 %collective-permute-start.23 = (bf16[4,192,128]{2,1,0:T(8,128)(2,1)S(1)}, bf16[4,192,128]{2,1,0:T(8,128)(2,1)S(1)}, u32[]{:S(2)}, u32[]{:S(2)}) collective-permute-start(bf16[4,192,128]{2,1,0:T(8,128)(2,1)S(1)} %get-tuple-element.132), channel_id=1, source_target_pairs={{0,24},{4,100},{8,0},{12,108},{16,8},{20,116},{24,16},{28,124},{32... | collective-permute-start | bytes 589832 | tf_op jit(solution)/shard_map/ppermute | solution.py:465
  122.1 4.5 %collective-permute-start.24 = (bf16[192,128]{1,0:T(8,128)(2,1)S(1)}, bf16[192,128]{1,0:T(8,128)(2,1)S(1)}, u32[]{:S(2)}, u32[]{:S(2)}) collective-permute-start(bf16[192,128]{1,0:T(8,128)(2,1)S(1)} %get-tuple-element.138), channel_id=1, source_target_pairs={{0,64},{4,20},{8,72},{12,28},{16,80},{20,4},{24,88},{28,12},{32,96... | collective-permute-start | bytes 147464 | tf_op jit(solution)/shard_map/ppermute | solution.py:465
  126.6 4.4 %collective-permute-start.25 = (bf16[192,128]{1,0:T(8,128)(2,1)S(1)}, bf16[192,128]{1,0:T(8,128)(2,1)S(1)}, u32[]{:S(2)}, u32[]{:S(2)}) collective-permute-start(bf16[192,128]{1,0:T(8,128)(2,1)S(1)} %get-tuple-element.137), channel_id=1, source_target_pairs={{0,32},{4,12},{8,40},{12,20},{16,48},{20,28},{24,56},{28,4},{32,64... | collective-permute-start | bytes 147464 | tf_op jit(solution)/shard_map/ppermute | solution.py:465
  131.1 2.9 %collective-permute-start.26 = (bf16[192,128]{1,0:T(8,128)(2,1)S(1)}, bf16[192,128]{1,0:T(8,128)(2,1)S(1)}, u32[]{:S(2)}, u32[]{:S(2)}) collective-permute-start(bf16[192,128]{1,0:T(8,128)(2,1)S(1)} %get-tuple-element.136), channel_id=1, source_target_pairs={{0,96},{4,28},{8,104},{12,4},{16,112},{20,12},{24,120},{28,20},{32... | collective-permute-start | bytes 147464 | tf_op jit(solution)/shard_map/ppermute | solution.py:465
  134.0 0.9 copy-start.1
  134.9 8.9 %collective-permute-start.27 = (bf16[12,128,256]{2,1,0:T(8,128)(2,1)S(1)}, bf16[12,128,256]{2,1,0:T(8,128)(2,1)}, u32[]{:S(2)}, u32[]{:S(2)}) collective-permute-start(bf16[12,128,256]{2,1,0:T(8,128)(2,1)S(1)} %collective-permute-done.16.refs_7_), channel_id=1, source_target_pairs={{0,4},{4,0},{8,12},{12,8},{16,20},{20,16},{24,28},{28,24},{32,36},... | collective-permute-start | bytes 2359304 | tf_op jit(solution)/shard_map/ppermute | solution.py:469
  141.8 3.2 %collective-permute-start.28 = (bf16[12,128,256]{2,1,0:T(8,128)(2,1)S(1)}, bf16[12,128,256]{2,1,0:T(8,128)(2,1)}, u32[]{:S(2)}, u32[]{:S(2)}) collective-permute-start(bf16[12,128,256]{2,1,0:T(8,128)(2,1)S(1)} %collective-permute-done.17.refs_8_), channel_id=1, source_target_pairs={{0,4},{4,0},{8,12},{12,8},{16,20},{20,16},{24,28},{28,24},{32,36},... | collective-permute-start | bytes 2359304 | tf_op jit(solution)/shard_map/ppermute | solution.py:469
  141.8 4.3 %collective-permute-start.29 = (bf16[12,128,256]{2,1,0:T(8,128)(2,1)S(1)}, bf16[12,128,256]{2,1,0:T(8,128)(2,1)}, u32[]{:S(2)}, u32[]{:S(2)}) collective-permute-start(bf16[12,128,256]{2,1,0:T(8,128)(2,1)S(1)} %collective-permute-done.18.refs_9_), channel_id=1, source_target_pairs={{0,4},{4,0},{8,12},{12,8},{16,20},{20,16},{24,28},{28,24},{32,36},... | collective-permute-start | bytes 2359304 | tf_op jit(solution)/shard_map/ppermute | solution.py:469
  146.1 1.1 copy-start.2
where the time goes:
time: 161 us; the launch traced here: 160 us
  waiting for transfers between devices  69.8 us (43%)
  starting transfers between devices  41.9 us (26%)
  Pallas kernels  40.5 us (25%)
  between operations  2.91 us (2%)
  local copies, waits for them, and re-layouts  2.86 us (2%)
  other arithmetic  2.48 us (2%)
    ppermute x18, waiting for transfers between devices, shift(): return lax.ppermute(value, 'src', shift_pairs(step, second))  55.1 us
    pallas_call x1, Pallas kernels, gather_sums(): pl.pallas_call(gather_kernel, out_shape=(blocks, blocks), in_specs=[spec(...  21.1 us
    ppermute x18, starting transfers between devices, shift(): return lax.ppermute(value, 'src', shift_pairs(step, second))  17.6 us
    ppermute x6, starting transfers between devices, swap(): return lax.ppermute(value, 'src', [(s, s ^ 1) for s in range(32)])  15.3 us
    pallas_call x1, Pallas kernels, spread_sums(): pl.pallas_call(spread_kernel, out_shape=jax.ShapeDtypeStruct((16, TILE, w...  13 us
    ppermute x6, starting transfers between devices, turn(): lax.ppermute(value, 'tgt', [(t, (t + step) % SIDE) for t in range(SIDE)])  8.94 us
    ppermute x6, waiting for transfers between devices, swap(): return lax.ppermute(value, 'src', [(s, s ^ 1) for s in range(32)])  8.61 us
    ppermute x6, waiting for transfers between devices, turn(): lax.ppermute(value, 'tgt', [(t, (t + step) % SIDE) for t in range(SIDE)])  6.07 us
  transfers between devices with their start and end apart: 30, of which 20 were waited for; matrix products, arithmetic and copies ran while one was open for 1% of the time, Pallas kernels for 3%

commit v1 on v0

--- a/solution.py
+++ b/solution.py
@@ -16,7 +16,7 @@
 F32 = jnp.float32
 MIB = 1024 * 1024
 GATHER_LIMIT = 36 * MIB
-SPREAD_LIMIT = 26 * MIB
+SPREAD_LIMIT = 28 * MIB
 barrier = lax.optimization_barrier
 
 
@@ -86,7 +86,7 @@
     targets0, targets1, targets2, sources0, sources1, sources2, counts0, counts1, counts2,
     features, tiles0, tiles1, tiles2,
     keep, send,
-    buffer, held, total, staged, table, tile_sems, out_sems, feature_sem,
+    buffer, held, total, table, tile_sems, feature_sem,
 ):
     targets, sources = (targets0, targets1, targets2), (sources0, sources1, sources2)
     counts, tiles = (counts0, counts1, counts2), (tiles0, tiles1, tiles2)
@@ -125,29 +125,15 @@
 
         lax.fori_loop(0, (counts[number][0] + GROUP - 1) // GROUP, add_group, 0)
 
-    def out_copy(where, spot):
-        target = keep if where == 0 else send
-        return pltpu.make_async_copy(
-            staged.at[where * 16 + spot], target.at[spot], out_sems.at[where * 16 + spot]
-        )
-
-    for where in (1, 0):
-        def emit(spot, carry, where=where):
-            block = where * 16 + spot
+    for where, target in ((16, send), (0, keep)):
+        def emit(spot, carry, where=where, target=target):
             for number in range(3):
-                staged[block, pl.ds(number * TILE, TILE), :] = total[block * 3 + number].astype(
-                    BF16
-                )
-            out_copy(where, spot).start()
+                target[spot, pl.ds(number * TILE, TILE), :] = total[
+                    (where + spot) * 3 + number
+                ].astype(BF16)
             return carry
 
         lax.fori_loop(0, 16, emit, 0)
-    for where in (1, 0):
-        def finish(spot, carry, where=where):
-            out_copy(where, spot).wait()
-            return carry
-
-        lax.fori_loop(0, 16, finish, 0)
 
 
 def in_hbm(value):
@@ -176,15 +162,13 @@
         gather_kernel,
         out_shape=(blocks, blocks),
         in_specs=[spec(SMEM)] * 10 + [spec(ANY)] * 4,
-        out_specs=(spec(ANY), spec(ANY)),
+        out_specs=(spec(VMEM), spec(VMEM)),
         scratch_shapes=[
             pltpu.VMEM((slots, TILE, TILE), BF16),
             pltpu.VMEM(features.shape, BF16),
             pltpu.VMEM((97, TILE, width), F32),
-            pltpu.VMEM((32, 3 * TILE, width), BF16),
             pltpu.SMEM((32,), jnp.int32),
             pltpu.SemaphoreType.DMA((slots // GROUP,)),
-            pltpu.SemaphoreType.DMA((32,)),
             pltpu.SemaphoreType.DMA(()),
         ],
         compiler_params=pltpu.CompilerParams(vmem_limit_bytes=GATHER_LIMIT),
@@ -260,18 +244,29 @@
 
 
 PLACES = (0, 8, 12, 4, 16, 24, 28, 20)
+FAR = (3, 5, 6, 7)
 
 
 def spread_kernel(pair_a, pair_b, pair_spot, amount, *refs):
     counts, tiles, pieces, refs = refs[:3], refs[3:6], refs[6:14], refs[14:]
-    out, buffer, messages, total, tile_sems, in_sems = refs
-    begins = start_tiles(tiles, counts, buffer, tile_sems)
+    out, buffer, messages, total, tile_sems, piece_sems = refs
     copies = [
-        pltpu.make_async_copy(piece, messages.at[pl.ds(at * 3, 12)], in_sems.at[number])
-        for number, (piece, at) in enumerate(zip(pieces, PLACES))
+        pltpu.make_async_copy(
+            pieces[number], messages.at[pl.ds(PLACES[number] * 3, 12)], piece_sems.at[sem]
+        )
+        for sem, number in enumerate(FAR)
     ]
     for copy in copies:
         copy.start()
+    begins = start_tiles(tiles, counts, buffer, tile_sems)
+
+    def place(block, carry):
+        for number, (piece, at) in enumerate(zip(pieces, PLACES)):
+            if number not in FAR:
+                messages[at * 3 + block] = piece[block]
+        return carry
+
+    lax.fori_loop(0, 12, place, 0)
     blank = buffer.shape[0] - 1
     buffer[blank] = jnp.zeros((TILE, TILE), BF16)
     clear(total, 16)
@@ -312,14 +307,16 @@
     return pl.pallas_call(
         spread_kernel,
         out_shape=jax.ShapeDtypeStruct((16, TILE, width), BF16),
-        in_specs=[spec(SMEM)] * 7 + [spec(ANY)] * 11,
+        in_specs=[spec(SMEM)] * 7
+        + [spec(ANY)] * 3
+        + [spec(ANY if number in FAR else VMEM) for number in range(8)],
         out_specs=spec(VMEM),
         scratch_shapes=[
             pltpu.VMEM((slots + 1, TILE, TILE), BF16),
             pltpu.VMEM((96, TILE, width), BF16),
             pltpu.VMEM((17, TILE, width), F32),
             pltpu.SemaphoreType.DMA((slots // GROUP,)),
-            pltpu.SemaphoreType.DMA((8,)),
+            pltpu.SemaphoreType.DMA((len(FAR),)),
         ],
         compiler_params=pltpu.CompilerParams(vmem_limit_bytes=SPREAD_LIMIT),
         cost_estimate=pl.CostEstimate(
@@ -330,7 +327,7 @@
         *plan,
         *[relation[3] for relation in relations],
         *tile_args(relations),
-        *pieces,
+        *[in_hbm(piece) if number in FAR else piece for number, piece in enumerate(pieces)],
     )
 
 

time: 161 us -> 147 us (0.913)
  the two profiles are of different devices: /device:TPU:7 before, /device:TPU:1 now
where the time goes in v1:
time: 147 us; the launch traced here: 145 us
  waiting for transfers between devices  72 us (49%)
  starting transfers between devices  48.4 us (33%)
  Pallas kernels  18.1 us (12%)
  between operations  2.89 us (2%)
  other arithmetic  2.48 us (2%)
    ppermute x18, waiting for transfers between devices, shift(): return lax.ppermute(value, 'src', shift_pairs(step, second))  57.4 us
    ppermute x18, starting transfers between devices, shift(): return lax.ppermute(value, 'src', shift_pairs(step, second))  25.7 us
    ppermute x6, starting transfers between devices, swap(): return lax.ppermute(value, 'src', [(s, s ^ 1) for s in range(32)])  13.8 us
    ppermute x6, starting transfers between devices, turn(): lax.ppermute(value, 'tgt', [(t, (t + step) % SIDE) for t in range(SIDE)])  8.93 us
    ppermute x6, waiting for transfers between devices, swap(): return lax.ppermute(value, 'src', [(s, s ^ 1) for s in range(32)])  8.57 us
    pallas_call x1, Pallas kernels, spread_sums(): pl.pallas_call(spread_kernel, out_shape=jax.ShapeDtypeStruct((16, TILE, w...  7.11 us
    pallas_call x1, Pallas kernels, gather_sums(): pl.pallas_call(gather_kernel, out_shape=(blocks, blocks), in_specs=[spec(...  6.14 us
    ppermute x6, waiting for transfers between devices, turn(): lax.ppermute(value, 'tgt', [(t, (t + step) % SIDE) for t in range(SIDE)])  6.07 us
  transfers between devices with their start and end apart: 30, of which 21 were waited for; matrix products, arithmetic and copies ran while one was open for 1% of the time, Pallas kernels for 2%

profile of v1, /device:TPU:1, one launch (start us, length us, event | category | flops | bytes accessed | tf_op | source)
XLA Modules:
  0.0 144.8 jit_solution(10733237347150848695)
XLA Ops:
  2.6 6.1 %gather_sums.1 = (bf16[16,384,256]{2,1,0:T(8,128)(2,1)S(1)}, bf16[16,384,256]{2,1,0:T(8,128)(2,1)S(1)}) custom-call(s32[32]{0:T(128)} %owner_map.2, s32[192]{0:T(256)} %targets0.3, s32[96]{0:T(128)} %targets1.3, s32[48]{0:T(128)} %targets2.3, s32[192]{0:T(256)} %sources0.3, s32[96]{0:T(128)} %sources1.3, s32[48]{0:T(128)} %sources2.3, ...), custom_call_target="tpu_custom_call" | custom-call | flops 3000000000 | bytes 18000000 | tf_op jit(solution)/shard_map/gather_sums/pallas_call | solution.py:161
  8.9 5.6 %collective-permute-done = bf16[16,384,256]{2,1,0:T(8,128)(2,1)S(1)} collective-permute-done((bf16[16,384,256]{2,1,0:T(8,128)(2,1)S(1)}, bf16[16,384,256]{2,1,0:T(8,128)(2,1)S(1)}, u32[]{:S(2)}, u32[]{:S(2)}) %collective-permute-start) | collective-permute-done | bytes 3145760 | tf_op jit(solution)/shard_map/ppermute | solution.py:466
  14.5 0.9 add_convert_fusion
  15.4 5.8 %collective-permute-start.1 = (bf16[4,384,256]{2,1,0:T(8,128)(2,1)S(1)}, bf16[4,384,256]{2,1,0:T(8,128)(2,1)S(1)}, u32[]{:S(2)}, u32[]{:S(2)}) collective-permute-start(bf16[4,384,256]{2,1,0:T(8,128)(2,1)S(1)} %get-tuple-element.70), channel_id=1, source_target_pairs={{0,64},{4,20},{8,72},{12,28},{16,80},{20,4},{24,88},{28,12},{32,96... | collective-permute-start | bytes 2359304 | tf_op jit(solution)/shard_map/ppermute | solution.py:462
  21.2 4.7 %collective-permute-start.2 = (bf16[4,384,256]{2,1,0:T(8,128)(2,1)S(1)}, bf16[4,384,256]{2,1,0:T(8,128)(2,1)S(1)}, u32[]{:S(2)}, u32[]{:S(2)}) collective-permute-start(bf16[4,384,256]{2,1,0:T(8,128)(2,1)S(1)} %get-tuple-element.71), channel_id=1, source_target_pairs={{0,32},{4,12},{8,40},{12,20},{16,48},{20,28},{24,56},{28,4},{32,64... | collective-permute-start | bytes 2359304 | tf_op jit(solution)/shard_map/ppermute | solution.py:462
  26.0 2.6 %plan_spread.1 = (s32[216]{0:T(256)S(1)}, s32[216]{0:T(256)S(1)}, s32[216]{0:T(256)S(1)}, s32[1]{0:T(128)}) custom-call(s32[32]{0:T(128)} %owner_map.2, s32[192]{0:T(256)} %targets0.3, s32[96]{0:T(128)} %targets1.3, s32[48]{0:T(128)} %targets2.3, s32[192]{0:T(256)} %sources0.3, s32[96]{0:T(128)} %sources1.3, s32[48]{0:T(128)} %sources2.3, ...), custom_call_target="tpu_custom_call" | custom-call | flops 1000000000 | bytes 1000000 | tf_op jit(solution)/shard_map/plan_spread/pallas_call | solution.py:234
  28.6 2.4 %collective-permute-done.1 = bf16[4,384,256]{2,1,0:T(8,128)(2,1)S(1)} collective-permute-done((bf16[4,384,256]{2,1,0:T(8,128)(2,1)S(1)}, bf16[4,384,256]{2,1,0:T(8,128)(2,1)S(1)}, u32[]{:S(2)}, u32[]{:S(2)}) %collective-permute-start.1) | collective-permute-done | bytes 786464 | tf_op jit(solution)/shard_map/ppermute | solution.py:462
  31.0 8.4 %collective-permute-done.2 = bf16[4,384,256]{2,1,0:T(8,128)(2,1)S(1)} collective-permute-done((bf16[4,384,256]{2,1,0:T(8,128)(2,1)S(1)}, bf16[4,384,256]{2,1,0:T(8,128)(2,1)S(1)}, u32[]{:S(2)}, u32[]{:S(2)}) %collective-permute-start.2) | collective-permute-done | bytes 786464 | tf_op jit(solution)/shard_map/ppermute | solution.py:462
  39.3 4.8 %collective-permute-done.3 = bf16[4,384,256]{2,1,0:T(8,128)(2,1)S(1)} collective-permute-done((bf16[4,384,256]{2,1,0:T(8,128)(2,1)S(1)}, bf16[4,384,256]{2,1,0:T(8,128)(2,1)S(1)}, u32[]{:S(2)}, u32[]{:S(2)}) %collective-permute-start.3) | collective-permute-done | bytes 786464 | tf_op jit(solution)/shard_map/ppermute | solution.py:462
  44.5 0.6 collective-permute-start.4
  45.1 3.1 %collective-permute-start.5 = (bf16[384,256]{1,0:T(8,128)(2,1)S(1)}, bf16[384,256]{1,0:T(8,128)(2,1)S(1)}, u32[]{:S(2)}, u32[]{:S(2)}) collective-permute-start(bf16[384,256]{1,0:T(8,128)(2,1)S(1)} %get-tuple-element.129), channel_id=1, source_target_pairs={{0,8},{4,36},{8,16},{12,44},{16,24},{20,52},{24,0},{28,60},{32,40}... | collective-permute-start | bytes 589832 | tf_op jit(solution)/shard_map/ppermute | solution.py:462
  48.3 2.7 %collective-permute-done.4.part1 = bf16[384,256]{1,0:T(8,128)(2,1)S(1)} collective-permute-done((bf16[384,256]{1,0:T(8,128)(2,1)S(1)}, bf16[384,256]{1,0:T(8,128)(2,1)S(1)}, u32[]{:S(2)}, u32[]{:S(2)}) %collective-permute-start.4) | collective-permute-done | bytes 196640 | tf_op jit(solution)/shard_map/ppermute | solution.py:462
  50.9 2.1 %collective-permute-done.5.part2 = bf16[384,256]{1,0:T(8,128)(2,1)S(1)} collective-permute-done((bf16[384,256]{1,0:T(8,128)(2,1)S(1)}, bf16[384,256]{1,0:T(8,128)(2,1)S(1)}, u32[]{:S(2)}, u32[]{:S(2)}) %collective-permute-start.5) | collective-permute-done | bytes 196640 | tf_op jit(solution)/shard_map/ppermute | solution.py:462
  53.0 0.7 collective-permute-done.6.part3
  54.2 3.0 %collective-permute-start.7 = (bf16[128,256]{1,0:T(8,128)(2,1)S(1)}, bf16[128,256]{1,0:T(8,128)(2,1)S(1)}, u32[]{:S(2)}, u32[]{:S(2)}) collective-permute-start(bf16[128,256]{1,0:T(8,128)(2,1)S(1)} %get-tuple-element.83), channel_id=1, source_target_pairs={{0,2},{1,3},{2,0},{3,1},{4,6},{5,7},{6,4},{7,5},{8,10},{9,11},{10,... | collective-permute-start | bytes 196616 | tf_op jit(solution)/shard_map/ppermute | solution.py:488
  57.6 2.3 %collective-permute-start.9 = (bf16[128,256]{1,0:T(8,128)(2,1)S(1)}, bf16[128,256]{1,0:T(8,128)(2,1)S(1)}, u32[]{:S(2)}, u32[]{:S(2)}) collective-permute-start(bf16[128,256]{1,0:T(8,128)(2,1)S(1)} %get-tuple-element.85), channel_id=1, source_target_pairs={{0,3},{1,0},{2,1},{3,2},{4,7},{5,4},{6,5},{7,6},{8,11},{9,8},{10,9... | collective-permute-start | bytes 196616 | tf_op jit(solution)/shard_map/ppermute | solution.py:488
  59.9 2.3 %collective-permute-done.8 = bf16[128,256]{1,0:T(8,128)(2,1)S(1)} collective-permute-done((bf16[128,256]{1,0:T(8,128)(2,1)S(1)}, bf16[128,256]{1,0:T(8,128)(2,1)S(1)}, u32[]{:S(2)}, u32[]{:S(2)}) %collective-permute-start.8) | collective-permute-done | bytes 65568 | tf_op jit(solution)/shard_map/ppermute | solution.py:488
  62.2 0.8 fusion.6
  63.0 0.5 collective-permute-start.10
  63.5 2.2 %collective-permute-start.11 = (bf16[128,256]{1,0:T(8,128)(2,1)S(1)}, bf16[128,256]{1,0:T(8,128)(2,1)S(1)}, u32[]{:S(2)}, u32[]{:S(2)}) collective-permute-start(bf16[128,256]{1,0:T(8,128)(2,1)S(1)} %get-tuple-element.96.grad0), channel_id=1, source_target_pairs={{0,3},{1,0},{2,1},{3,2},{4,7},{5,4},{6,5},{7,6},{8,11},{9,8},{10,9... | collective-permute-start | bytes 196616 | tf_op jit(solution)/shard_map/ppermute | solution.py:488
  65.7 0.6 collective-permute-start.12
  66.2 1.3 collective-permute-done.10.grad2
  67.6 1.0 collective-permute-done.11.grad1
  68.6 1.4 collective-permute-done.12.grad3
  70.0 0.6 form_messages.1
  70.6 1.1 weight_terms.1
  71.8 4.6 %collective-permute-start.20 = (bf16[16,192,128]{2,1,0:T(8,128)(2,1)S(1)}, bf16[16,192,128]{2,1,0:T(8,128)(2,1)S(1)}, u32[]{:S(2)}, u32[]{:S(2)}) collective-permute-start(bf16[16,192,128]{2,1,0:T(8,128)(2,1)S(1)} %get-tuple-element.102), channel_id=1, source_target_pairs={{0,4},{4,0},{8,12},{12,8},{16,20},{20,16},{24,28},{28,24},{32,36},... | collective-permute-start | bytes 2359304 | tf_op jit(solution)/shard_map/ppermute | solution.py:466
  76.7 2.6 %collective-permute-start.14 = (bf16[3,128,256]{2,1,0:T(8,128)(2,1)S(1)}, bf16[3,128,256]{2,1,0:T(8,128)(2,1)S(1)}, u32[]{:S(2)}, u32[]{:S(2)}) collective-permute-start(bf16[3,128,256]{2,1,0:T(8,128)(2,1)S(1)} %form_messages.1), channel_id=1, source_target_pairs={{0,32},{4,12},{8,40},{12,20},{16,48},{20,28},{24,56},{28,4},{32,64... | collective-permute-start | bytes 589832 | tf_op jit(solution)/shard_map/ppermute | solution.py:462
  79.4 3.3 %collective-permute-done.13 = bf16[3,128,256]{2,1,0:T(8,128)(2,1)S(1)} collective-permute-done((bf16[3,128,256]{2,1,0:T(8,128)(2,1)S(1)}, bf16[3,128,256]{2,1,0:T(8,128)(2,1)S(1)}, u32[]{:S(2)}, u32[]{:S(2)}) %collective-permute-start.13) | collective-permute-done | bytes 196640 | tf_op jit(solution)/shard_map/ppermute | solution.py:462
  82.8 2.1 %collective-permute-done.14 = bf16[3,128,256]{2,1,0:T(8,128)(2,1)S(1)} collective-permute-done((bf16[3,128,256]{2,1,0:T(8,128)(2,1)S(1)}, bf16[3,128,256]{2,1,0:T(8,128)(2,1)S(1)}, u32[]{:S(2)}, u32[]{:S(2)}) %collective-permute-start.14) | collective-permute-done | bytes 196640 | tf_op jit(solution)/shard_map/ppermute | solution.py:462
  85.1 1.5 %collective-permute-start.21 = (bf16[4,192,128]{2,1,0:T(8,128)(2,1)S(1)}, bf16[4,192,128]{2,1,0:T(8,128)(2,1)S(1)}, u32[]{:S(2)}, u32[]{:S(2)}) collective-permute-start(bf16[4,192,128]{2,1,0:T(8,128)(2,1)S(1)} %get-tuple-element.134), channel_id=1, source_target_pairs={{0,16},{4,68},{8,24},{12,76},{16,0},{20,84},{24,8},{28,92},{32,48}... | collective-permute-start | bytes 589832 | tf_op jit(solution)/shard_map/ppermute | solution.py:462
  86.6 1.7 %collective-permute-start.16 = (bf16[12,128,256]{2,1,0:T(8,128)(2,1)S(1)}, bf16[12,128,256]{2,1,0:T(8,128)(2,1)S(1)}, u32[]{:S(2)}, u32[]{:S(2)}) collective-permute-start(bf16[12,128,256]{2,1,0:T(8,128)(2,1)S(1)} %constant_dynamic-update-slice_fusion.refs_6_), channel_id=1, source_target_pairs={{0,16},{4,68},{8,24},{12,76},{16,0},{20,84},{24,8},{28,92},{32,48}... | collective-permute-start | bytes 2359304 | tf_op jit(solution)/shard_map/ppermute | solution.py:462
  88.3 0.7 collective-permute-start.17
  89.0 1.9 %collective-permute-start.18 = (bf16[12,128,256]{2,1,0:T(8,128)(2,1)S(1)}, bf16[12,128,256]{2,1,0:T(8,128)(2,1)}, u32[]{:S(2)}, u32[]{:S(2)}) collective-permute-start(bf16[12,128,256]{2,1,0:T(8,128)(2,1)S(1)} %constant_dynamic-update-slice_fusion.refs_6_), channel_id=1, source_target_pairs={{0,24},{4,100},{8,0},{12,108},{16,8},{20,116},{24,16},{28,124},{32... | collective-permute-start | bytes 2359304 | tf_op jit(solution)/shard_map/ppermute | solution.py:462
  91.0 2.0 %collective-permute-start.19 = (bf16[12,128,256]{2,1,0:T(8,128)(2,1)S(1)}, bf16[12,128,256]{2,1,0:T(8,128)(2,1)S(1)}, u32[]{:S(2)}, u32[]{:S(2)}) collective-permute-start(bf16[12,128,256]{2,1,0:T(8,128)(2,1)S(1)} %constant_dynamic-update-slice_fusion.refs_6_), channel_id=1, source_target_pairs={{0,4},{4,0},{8,12},{12,8},{16,20},{20,16},{24,28},{28,24},{32,36},... | collective-permute-start | bytes 2359304 | tf_op jit(solution)/shard_map/ppermute | solution.py:466
  93.0 0.7 collective-permute-start.22
  93.8 16.7 %collective-permute-done.22 = bf16[4,192,128]{2,1,0:T(8,128)(2,1)S(1)} collective-permute-done((bf16[4,192,128]{2,1,0:T(8,128)(2,1)S(1)}, bf16[4,192,128]{2,1,0:T(8,128)(2,1)S(1)}, u32[]{:S(2)}, u32[]{:S(2)}) %collective-permute-start.22) | collective-permute-done | bytes 196640 | tf_op jit(solution)/shard_map/ppermute | solution.py:462
  110.9 4.1 %collective-permute-done.23 = bf16[4,192,128]{2,1,0:T(8,128)(2,1)S(1)} collective-permute-done((bf16[4,192,128]{2,1,0:T(8,128)(2,1)S(1)}, bf16[4,192,128]{2,1,0:T(8,128)(2,1)S(1)}, u32[]{:S(2)}, u32[]{:S(2)}) %collective-permute-start.23) | collective-permute-done | bytes 196640 | tf_op jit(solution)/shard_map/ppermute | solution.py:462
  115.5 4.2 %collective-permute-done.24 = bf16[192,128]{1,0:T(8,128)(2,1)S(1)} collective-permute-done((bf16[192,128]{1,0:T(8,128)(2,1)S(1)}, bf16[192,128]{1,0:T(8,128)(2,1)S(1)}, u32[]{:S(2)}, u32[]{:S(2)}) %collective-permute-start.24) | collective-permute-done | bytes 49184 | tf_op jit(solution)/shard_map/ppermute | solution.py:462
  119.7 4.1 %collective-permute-done.25 = bf16[192,128]{1,0:T(8,128)(2,1)S(1)} collective-permute-done((bf16[192,128]{1,0:T(8,128)(2,1)S(1)}, bf16[192,128]{1,0:T(8,128)(2,1)S(1)}, u32[]{:S(2)}, u32[]{:S(2)}) %collective-permute-start.25) | collective-permute-done | bytes 49184 | tf_op jit(solution)/shard_map/ppermute | solution.py:462
  123.8 1.1 collective-permute-start.26
  125.0 1.8 %collective-permute-done.26 = bf16[192,128]{1,0:T(8,128)(2,1)S(1)} collective-permute-done((bf16[192,128]{1,0:T(8,128)(2,1)S(1)}, bf16[192,128]{1,0:T(8,128)(2,1)S(1)}, u32[]{:S(2)}, u32[]{:S(2)}) %collective-permute-start.26) | collective-permute-done | bytes 49184 | tf_op jit(solution)/shard_map/ppermute | solution.py:462
  126.8 6.5 %collective-permute-start.27 = (bf16[12,128,256]{2,1,0:T(8,128)(2,1)S(1)}, bf16[12,128,256]{2,1,0:T(8,128)(2,1)}, u32[]{:S(2)}, u32[]{:S(2)}) collective-permute-start(bf16[12,128,256]{2,1,0:T(8,128)(2,1)S(1)} %collective-permute-done.16.refs_7_), channel_id=1, source_target_pairs={{0,4},{4,0},{8,12},{12,8},{16,20},{20,16},{24,28},{28,24},{32,36},... | collective-permute-start | bytes 2359304 | tf_op jit(solution)/shard_map/ppermute | solution.py:466
  133.9 0.7 copy.21
  134.6 0.7 collective-permute-done.27.refs_11_
  135.3 1.1 collective-permute-done.28.refs_12_
  136.4 1.1 collective-permute-done.29.refs_13_
  137.5 7.1 %spread_sums.1 = bf16[16,128,256]{2,1,0:T(8,128)(2,1)} custom-call(s32[216]{0:T(256)S(1)} %get-tuple-element.113.pair_a, s32[216]{0:T(256)S(1)} %get-tuple-element.114.pair_b, s32[216]{0:T(256)S(1)} %get-tuple-element.115.pair_spot, s32[1]{0:T(128)} %get-tuple-element.116.amount, s32[1]{0:T(128)S(6)} %copy.27.counts0.refs_0_, s32[1]{0:T(128)S(6)} %copy.28.counts1.refs_1_, ...), custom_call_target="tpu_custom_call" | custom-call | flops 3000000000 | bytes 18000000 | tf_op jit(solution)/shard_map/spread_sums/pallas_call | solution.py:307
  (38 shorter events, 3.7 us)
Async XLA Ops:
  8.7 5.7 %collective-permute-start = (bf16[16,384,256]{2,1,0:T(8,128)(2,1)S(1)}, bf16[16,384,256]{2,1,0:T(8,128)(2,1)S(1)}, u32[]{:S(2)}, u32[]{:S(2)}) collective-permute-start(bf16[16,384,256]{2,1,0:T(8,128)(2,1)S(1)} %get-tuple-element.63), channel_id=1, source_target_pairs={{0,4},{4,0},{8,12},{12,8},{16,20},{20,16},{24,28},{28,24},{32,36},... | collective-permute-start | bytes 9437192 | tf_op jit(solution)/shard_map/ppermute | solution.py:466
  15.4 15.5 %collective-permute-start.1 = (bf16[4,384,256]{2,1,0:T(8,128)(2,1)S(1)}, bf16[4,384,256]{2,1,0:T(8,128)(2,1)S(1)}, u32[]{:S(2)}, u32[]{:S(2)}) collective-permute-start(bf16[4,384,256]{2,1,0:T(8,128)(2,1)S(1)} %get-tuple-element.70), channel_id=1, source_target_pairs={{0,64},{4,20},{8,72},{12,28},{16,80},{20,4},{24,88},{28,12},{32,96... | collective-permute-start | bytes 2359304 | tf_op jit(solution)/shard_map/ppermute | solution.py:462
  21.2 18.1 %collective-permute-start.2 = (bf16[4,384,256]{2,1,0:T(8,128)(2,1)S(1)}, bf16[4,384,256]{2,1,0:T(8,128)(2,1)S(1)}, u32[]{:S(2)}, u32[]{:S(2)}) collective-permute-start(bf16[4,384,256]{2,1,0:T(8,128)(2,1)S(1)} %get-tuple-element.71), channel_id=1, source_target_pairs={{0,32},{4,12},{8,40},{12,20},{16,48},{20,28},{24,56},{28,4},{32,64... | collective-permute-start | bytes 2359304 | tf_op jit(solution)/shard_map/ppermute | solution.py:462
  25.9 18.1 %collective-permute-start.3 = (bf16[4,384,256]{2,1,0:T(8,128)(2,1)S(1)}, bf16[4,384,256]{2,1,0:T(8,128)(2,1)S(1)}, u32[]{:S(2)}, u32[]{:S(2)}) collective-permute-start(bf16[4,384,256]{2,1,0:T(8,128)(2,1)S(1)} %get-tuple-element.72), channel_id=1, source_target_pairs={{0,96},{4,28},{8,104},{12,4},{16,112},{20,12},{24,120},{28,20},{32... | collective-permute-start | bytes 2359304 | tf_op jit(solution)/shard_map/ppermute | solution.py:462
  44.1 9.7 %copy-start = (bf16[3,256,1024]{2,1,0:T(8,128)(2,1)S(1)}, bf16[3,256,1024]{2,1,0:T(8,128)(2,1)}, u32[]{:S(2)}) copy-start(bf16[3,256,1024]{2,1,0:T(8,128)(2,1)} %weights.3) | copy-start | bytes 4718596
  44.5 15.4 %copy-start.2 = (bf16[256]{0:T(256)(128)(2,1)S(1)}, bf16[256]{0:T(256)(128)(2,1)}, u32[]{:S(2)}) copy-start(bf16[256]{0:T(256)(128)(2,1)} %param.32) | copy-start | bytes 1540
  44.5 17.7 %copy-start.1 = (bf16[128,256]{1,0:T(8,128)(2,1)S(1)}, bf16[128,256]{1,0:T(8,128)(2,1)}, u32[]{:S(2)}) copy-start(bf16[128,256]{1,0:T(8,128)(2,1)} %param.33) | copy-start | bytes 196612
  44.5 6.4 %collective-permute-start.4 = (bf16[384,256]{1,0:T(8,128)(2,1)S(1)}, bf16[384,256]{1,0:T(8,128)(2,1)S(1)}, u32[]{:S(2)}, u32[]{:S(2)}) collective-permute-start(bf16[384,256]{1,0:T(8,128)(2,1)S(1)} %get-tuple-element.130), channel_id=1, source_target_pairs={{0,16},{4,68},{8,24},{12,76},{16,0},{20,84},{24,8},{28,92},{32,48}... | collective-permute-start | bytes 589832 | tf_op jit(solution)/shard_map/ppermute | solution.py:462
  45.1 7.9 %collective-permute-start.5 = (bf16[384,256]{1,0:T(8,128)(2,1)S(1)}, bf16[384,256]{1,0:T(8,128)(2,1)S(1)}, u32[]{:S(2)}, u32[]{:S(2)}) collective-permute-start(bf16[384,256]{1,0:T(8,128)(2,1)S(1)} %get-tuple-element.129), channel_id=1, source_target_pairs={{0,8},{4,36},{8,16},{12,44},{16,24},{20,52},{24,0},{28,60},{32,40}... | collective-permute-start | bytes 589832 | tf_op jit(solution)/shard_map/ppermute | solution.py:462
  48.3 5.5 %collective-permute-start.6 = (bf16[384,256]{1,0:T(8,128)(2,1)S(1)}, bf16[384,256]{1,0:T(8,128)(2,1)S(1)}, u32[]{:S(2)}, u32[]{:S(2)}) collective-permute-start(bf16[384,256]{1,0:T(8,128)(2,1)S(1)} %get-tuple-element.128), channel_id=1, source_target_pairs={{0,24},{4,100},{8,0},{12,108},{16,8},{20,116},{24,16},{28,124},{32... | collective-permute-start | bytes 589832 | tf_op jit(solution)/shard_map/ppermute | solution.py:462
  54.2 5.7 %collective-permute-start.7 = (bf16[128,256]{1,0:T(8,128)(2,1)S(1)}, bf16[128,256]{1,0:T(8,128)(2,1)S(1)}, u32[]{:S(2)}, u32[]{:S(2)}) collective-permute-start(bf16[128,256]{1,0:T(8,128)(2,1)S(1)} %get-tuple-element.83), channel_id=1, source_target_pairs={{0,2},{1,3},{2,0},{3,1},{4,6},{5,7},{6,4},{7,5},{8,10},{9,11},{10,... | collective-permute-start | bytes 196616 | tf_op jit(solution)/shard_map/ppermute | solution.py:488
  57.2 5.0 %collective-permute-start.8 = (bf16[128,256]{1,0:T(8,128)(2,1)S(1)}, bf16[128,256]{1,0:T(8,128)(2,1)S(1)}, u32[]{:S(2)}, u32[]{:S(2)}) collective-permute-start(bf16[128,256]{1,0:T(8,128)(2,1)S(1)} %get-tuple-element.84), channel_id=1, source_target_pairs={{0,1},{1,2},{2,3},{3,0},{4,5},{5,6},{6,7},{7,4},{8,9},{9,10},{10,1... | collective-permute-start | bytes 196616 | tf_op jit(solution)/shard_map/ppermute | solution.py:488
  57.6 4.6 %collective-permute-start.9 = (bf16[128,256]{1,0:T(8,128)(2,1)S(1)}, bf16[128,256]{1,0:T(8,128)(2,1)S(1)}, u32[]{:S(2)}, u32[]{:S(2)}) collective-permute-start(bf16[128,256]{1,0:T(8,128)(2,1)S(1)} %get-tuple-element.85), channel_id=1, source_target_pairs={{0,3},{1,0},{2,1},{3,2},{4,7},{5,4},{6,5},{7,6},{8,11},{9,8},{10,9... | collective-permute-start | bytes 196616 | tf_op jit(solution)/shard_map/ppermute | solution.py:488
  63.0 4.6 %collective-permute-start.10 = (bf16[128,256]{1,0:T(8,128)(2,1)S(1)}, bf16[128,256]{1,0:T(8,128)(2,1)S(1)}, u32[]{:S(2)}, u32[]{:S(2)}) collective-permute-start(bf16[128,256]{1,0:T(8,128)(2,1)S(1)} %get-tuple-element.96.grad0), channel_id=1, source_target_pairs={{0,2},{1,3},{2,0},{3,1},{4,6},{5,7},{6,4},{7,5},{8,10},{9,11},{10,... | collective-permute-start | bytes 196616 | tf_op jit(solution)/shard_map/ppermute | solution.py:488
  63.5 5.1 %collective-permute-start.11 = (bf16[128,256]{1,0:T(8,128)(2,1)S(1)}, bf16[128,256]{1,0:T(8,128)(2,1)S(1)}, u32[]{:S(2)}, u32[]{:S(2)}) collective-permute-start(bf16[128,256]{1,0:T(8,128)(2,1)S(1)} %get-tuple-element.96.grad0), channel_id=1, source_target_pairs={{0,3},{1,0},{2,1},{3,2},{4,7},{5,4},{6,5},{7,6},{8,11},{9,8},{10,9... | collective-permute-start | bytes 196616 | tf_op jit(solution)/shard_map/ppermute | solution.py:488
  65.7 4.3 %collective-permute-start.12 = (bf16[128,256]{1,0:T(8,128)(2,1)S(1)}, bf16[128,256]{1,0:T(8,128)(2,1)S(1)}, u32[]{:S(2)}, u32[]{:S(2)}) collective-permute-start(bf16[128,256]{1,0:T(8,128)(2,1)S(1)} %get-tuple-element.96.grad0), channel_id=1, source_target_pairs={{0,1},{1,2},{2,3},{3,0},{4,5},{5,6},{6,7},{7,4},{8,9},{9,10},{10,1... | collective-permute-start | bytes 196616 | tf_op jit(solution)/shard_map/ppermute | solution.py:488
  71.8 13.1 %collective-permute-start.20 = (bf16[16,192,128]{2,1,0:T(8,128)(2,1)S(1)}, bf16[16,192,128]{2,1,0:T(8,128)(2,1)S(1)}, u32[]{:S(2)}, u32[]{:S(2)}) collective-permute-start(bf16[16,192,128]{2,1,0:T(8,128)(2,1)S(1)} %get-tuple-element.102), channel_id=1, source_target_pairs={{0,4},{4,0},{8,12},{12,8},{16,20},{20,16},{24,28},{28,24},{32,36},... | collective-permute-start | bytes 2359304 | tf_op jit(solution)/shard_map/ppermute | solution.py:466
  76.4 6.4 %collective-permute-start.13 = (bf16[3,128,256]{2,1,0:T(8,128)(2,1)S(1)}, bf16[3,128,256]{2,1,0:T(8,128)(2,1)S(1)}, u32[]{:S(2)}, u32[]{:S(2)}) collective-permute-start(bf16[3,128,256]{2,1,0:T(8,128)(2,1)S(1)} %form_messages.1), channel_id=1, source_target_pairs={{0,64},{4,20},{8,72},{12,28},{16,80},{20,4},{24,88},{28,12},{32,96... | collective-permute-start | bytes 589832 | tf_op jit(solution)/shard_map/ppermute | solution.py:462
  76.7 8.1 %collective-permute-start.14 = (bf16[3,128,256]{2,1,0:T(8,128)(2,1)S(1)}, bf16[3,128,256]{2,1,0:T(8,128)(2,1)S(1)}, u32[]{:S(2)}, u32[]{:S(2)}) collective-permute-start(bf16[3,128,256]{2,1,0:T(8,128)(2,1)S(1)} %form_messages.1), channel_id=1, source_target_pairs={{0,32},{4,12},{8,40},{12,20},{16,48},{20,28},{24,56},{28,4},{32,64... | collective-permute-start | bytes 589832 | tf_op jit(solution)/shard_map/ppermute | solution.py:462
  79.4 5.5 %collective-permute-start.15 = (bf16[3,128,256]{2,1,0:T(8,128)(2,1)S(1)}, bf16[3,128,256]{2,1,0:T(8,128)(2,1)S(1)}, u32[]{:S(2)}, u32[]{:S(2)}) collective-permute-start(bf16[3,128,256]{2,1,0:T(8,128)(2,1)S(1)} %form_messages.1), channel_id=1, source_target_pairs={{0,96},{4,28},{8,104},{12,4},{16,112},{20,12},{24,120},{28,20},{32... | collective-permute-start | bytes 589832 | tf_op jit(solution)/shard_map/ppermute | solution.py:462
  85.1 7.9 %collective-permute-start.21 = (bf16[4,192,128]{2,1,0:T(8,128)(2,1)S(1)}, bf16[4,192,128]{2,1,0:T(8,128)(2,1)S(1)}, u32[]{:S(2)}, u32[]{:S(2)}) collective-permute-start(bf16[4,192,128]{2,1,0:T(8,128)(2,1)S(1)} %get-tuple-element.134), channel_id=1, source_target_pairs={{0,16},{4,68},{8,24},{12,76},{16,0},{20,84},{24,8},{28,92},{32,48}... | collective-permute-start | bytes 589832 | tf_op jit(solution)/shard_map/ppermute | solution.py:462
  86.6 40.1 %collective-permute-start.16 = (bf16[12,128,256]{2,1,0:T(8,128)(2,1)S(1)}, bf16[12,128,256]{2,1,0:T(8,128)(2,1)S(1)}, u32[]{:S(2)}, u32[]{:S(2)}) collective-permute-start(bf16[12,128,256]{2,1,0:T(8,128)(2,1)S(1)} %constant_dynamic-update-slice_fusion.refs_6_), channel_id=1, source_target_pairs={{0,16},{4,68},{8,24},{12,76},{16,0},{20,84},{24,8},{28,92},{32,48}... | collective-permute-start | bytes 2359304 | tf_op jit(solution)/shard_map/ppermute | solution.py:462
  88.3 38.4 %collective-permute-start.17 = (bf16[12,128,256]{2,1,0:T(8,128)(2,1)S(1)}, bf16[12,128,256]{2,1,0:T(8,128)(2,1)S(1)}, u32[]{:S(2)}, u32[]{:S(2)}) collective-permute-start(bf16[12,128,256]{2,1,0:T(8,128)(2,1)S(1)} %constant_dynamic-update-slice_fusion.refs_6_), channel_id=1, source_target_pairs={{0,8},{4,36},{8,16},{12,44},{16,24},{20,52},{24,0},{28,60},{32,40}... | collective-permute-start | bytes 2359304 | tf_op jit(solution)/shard_map/ppermute | solution.py:462
  89.0 37.7 %collective-permute-start.18 = (bf16[12,128,256]{2,1,0:T(8,128)(2,1)S(1)}, bf16[12,128,256]{2,1,0:T(8,128)(2,1)}, u32[]{:S(2)}, u32[]{:S(2)}) collective-permute-start(bf16[12,128,256]{2,1,0:T(8,128)(2,1)S(1)} %constant_dynamic-update-slice_fusion.refs_6_), channel_id=1, source_target_pairs={{0,24},{4,100},{8,0},{12,108},{16,8},{20,116},{24,16},{28,124},{32... | collective-permute-start | bytes 2359304 | tf_op jit(solution)/shard_map/ppermute | solution.py:462
  91.0 35.8 %collective-permute-start.19 = (bf16[12,128,256]{2,1,0:T(8,128)(2,1)S(1)}, bf16[12,128,256]{2,1,0:T(8,128)(2,1)S(1)}, u32[]{:S(2)}, u32[]{:S(2)}) collective-permute-start(bf16[12,128,256]{2,1,0:T(8,128)(2,1)S(1)} %constant_dynamic-update-slice_fusion.refs_6_), channel_id=1, source_target_pairs={{0,4},{4,0},{8,12},{12,8},{16,20},{20,16},{24,28},{28,24},{32,36},... | collective-permute-start | bytes 2359304 | tf_op jit(solution)/shard_map/ppermute | solution.py:466
  93.0 17.5 %collective-permute-start.22 = (bf16[4,192,128]{2,1,0:T(8,128)(2,1)S(1)}, bf16[4,192,128]{2,1,0:T(8,128)(2,1)S(1)}, u32[]{:S(2)}, u32[]{:S(2)}) collective-permute-start(bf16[4,192,128]{2,1,0:T(8,128)(2,1)S(1)} %get-tuple-element.133), channel_id=1, source_target_pairs={{0,8},{4,36},{8,16},{12,44},{16,24},{20,52},{24,0},{28,60},{32,40}... | collective-permute-start | bytes 589832 | tf_op jit(solution)/shard_map/ppermute | solution.py:462
  110.5 4.5 %collective-permute-start.23 = (bf16[4,192,128]{2,1,0:T(8,128)(2,1)S(1)}, bf16[4,192,128]{2,1,0:T(8,128)(2,1)S(1)}, u32[]{:S(2)}, u32[]{:S(2)}) collective-permute-start(bf16[4,192,128]{2,1,0:T(8,128)(2,1)S(1)} %get-tuple-element.132), channel_id=1, source_target_pairs={{0,24},{4,100},{8,0},{12,108},{16,8},{20,116},{24,16},{28,124},{32... | collective-permute-start | bytes 589832 | tf_op jit(solution)/shard_map/ppermute | solution.py:462
  115.1 4.5 %collective-permute-start.24 = (bf16[192,128]{1,0:T(8,128)(2,1)S(1)}, bf16[192,128]{1,0:T(8,128)(2,1)S(1)}, u32[]{:S(2)}, u32[]{:S(2)}) collective-permute-start(bf16[192,128]{1,0:T(8,128)(2,1)S(1)} %get-tuple-element.138), channel_id=1, source_target_pairs={{0,64},{4,20},{8,72},{12,28},{16,80},{20,4},{24,88},{28,12},{32,96... | collective-permute-start | bytes 147464 | tf_op jit(solution)/shard_map/ppermute | solution.py:462
  119.7 4.2 %collective-permute-start.25 = (bf16[192,128]{1,0:T(8,128)(2,1)S(1)}, bf16[192,128]{1,0:T(8,128)(2,1)S(1)}, u32[]{:S(2)}, u32[]{:S(2)}) collective-permute-start(bf16[192,128]{1,0:T(8,128)(2,1)S(1)} %get-tuple-element.137), channel_id=1, source_target_pairs={{0,32},{4,12},{8,40},{12,20},{16,48},{20,28},{24,56},{28,4},{32,64... | collective-permute-start | bytes 147464 | tf_op jit(solution)/shard_map/ppermute | solution.py:462
  123.8 2.9 %collective-permute-start.26 = (bf16[192,128]{1,0:T(8,128)(2,1)S(1)}, bf16[192,128]{1,0:T(8,128)(2,1)S(1)}, u32[]{:S(2)}, u32[]{:S(2)}) collective-permute-start(bf16[192,128]{1,0:T(8,128)(2,1)S(1)} %get-tuple-element.136), channel_id=1, source_target_pairs={{0,96},{4,28},{8,104},{12,4},{16,112},{20,12},{24,120},{28,20},{32... | collective-permute-start | bytes 147464 | tf_op jit(solution)/shard_map/ppermute | solution.py:462
  126.8 8.5 %collective-permute-start.27 = (bf16[12,128,256]{2,1,0:T(8,128)(2,1)S(1)}, bf16[12,128,256]{2,1,0:T(8,128)(2,1)}, u32[]{:S(2)}, u32[]{:S(2)}) collective-permute-start(bf16[12,128,256]{2,1,0:T(8,128)(2,1)S(1)} %collective-permute-done.16.refs_7_), channel_id=1, source_target_pairs={{0,4},{4,0},{8,12},{12,8},{16,20},{20,16},{24,28},{28,24},{32,36},... | collective-permute-start | bytes 2359304 | tf_op jit(solution)/shard_map/ppermute | solution.py:466
  133.2 3.2 %collective-permute-start.28 = (bf16[12,128,256]{2,1,0:T(8,128)(2,1)S(1)}, bf16[12,128,256]{2,1,0:T(8,128)(2,1)}, u32[]{:S(2)}, u32[]{:S(2)}) collective-permute-start(bf16[12,128,256]{2,1,0:T(8,128)(2,1)S(1)} %collective-permute-done.17.refs_8_), channel_id=1, source_target_pairs={{0,4},{4,0},{8,12},{12,8},{16,20},{20,16},{24,28},{28,24},{32,36},... | collective-permute-start | bytes 2359304 | tf_op jit(solution)/shard_map/ppermute | solution.py:466
  133.3 4.2 %collective-permute-start.29 = (bf16[12,128,256]{2,1,0:T(8,128)(2,1)}, bf16[12,128,256]{2,1,0:T(8,128)(2,1)}, u32[]{:S(2)}, u32[]{:S(2)}) collective-permute-start(bf16[12,128,256]{2,1,0:T(8,128)(2,1)} %collective-permute-done.18.refs_9_), channel_id=1, source_target_pairs={{0,4},{4,0},{8,12},{12,8},{16,20},{20,16},{24,28},{28,24},{32,36},... | collective-permute-start | bytes 2359304 | tf_op jit(solution)/shard_map/ppermute | solution.py:466

commit v2 on v1

--- a/solution.py
+++ b/solution.py
@@ -73,20 +73,46 @@
     return jnp.maximum(waited, needed)
 
 
-def clear(total, amount):
+def clear(total, amount, begin=0):
     def step(block, carry):
         total[block] = jnp.zeros(total.shape[1:], F32)
         return carry
 
-    lax.fori_loop(0, amount, step, 0)
-
-
-def gather_kernel(
+    lax.fori_loop(begin, amount, step, 0)
+
+
+def gather_list(codes, amount, features, buffer, total, ready):
+    def add_group(group, waited):
+        waited = ready(waited, codes[jnp.minimum(group * GROUP + GROUP, amount) - 1] & 1023)
+        marks = [codes[group * GROUP + lane] for lane in range(GROUP)]
+        products = [
+            jnp.dot(
+                buffer[mark & 1023], features[(mark >> 10) & 15], preferred_element_type=F32
+            )
+            for mark in marks
+        ]
+        for mark, product in zip(marks, products):
+            total[mark >> 14] += product
+        return waited
+
+    return lax.fori_loop(0, (amount + GROUP - 1) // GROUP, add_group, jnp.int32(0))
+
+
+def emit_blocks(total, target):
+    def emit(spot, carry):
+        for number in range(3):
+            target[spot, pl.ds(number * TILE, TILE), :] = total[spot * 3 + number].astype(BF16)
+        return carry
+
+    lax.fori_loop(0, 16, emit, 0)
+
+
+def gather_send_kernel(
     owner_map,
     targets0, targets1, targets2, sources0, sources1, sources2, counts0, counts1, counts2,
     features, tiles0, tiles1, tiles2,
-    keep, send,
-    buffer, held, total, table, tile_sems, feature_sem,
+    send, keep_codes, keep_amount, buffer, held,
+    total, table, send_codes, tile_sems, feature_sem,
 ):
     targets, sources = (targets0, targets1, targets2), (sources0, sources1, sources2)
     counts, tiles = (counts0, counts1, counts2), (tiles0, tiles1, tiles2)
@@ -97,43 +123,53 @@
 
     def fill(slot, carry):
         first, second, away = place_of(slot, mine)
-        table[owner_map[slot]] = (away * 16 + first * SIDE + second) * 3
-        for number in range(3):
-            total[slot * 3 + number] = jnp.zeros(total.shape[1:], F32)
+        table[owner_map[slot]] = (first * SIDE + second) * 3 + away * 128
+        total[slot] = jnp.zeros(total.shape[1:], F32)
         return carry
 
     lax.fori_loop(0, 32, fill, 0)
-    feature_copy.wait()
-
+    clear(total, 48, 32)
+
+    sent, kept = jnp.int32(0), jnp.int32(0)
     for number in range(3):
-        def add_group(group, carry, number=number):
-            at = begins[number] + group
-            wait_tiles(tiles[0], buffer, tile_sems, at, at + 1)
-            products = []
-            for lane in range(GROUP):
-                source = sources[number][group * GROUP + lane]
-                products.append(
-                    jnp.dot(
-                        buffer[at * GROUP + lane], held[source], preferred_element_type=F32
-                    )
-                )
+        def sort(group, carry, number=number):
+            sent, kept = carry
             for lane in range(GROUP):
                 j = group * GROUP + lane
-                spot = jnp.where(j < counts[number][0], table[targets[number][j]] + number, 96)
-                total[spot] += products[lane]
-            return carry
-
-        lax.fori_loop(0, (counts[number][0] + GROUP - 1) // GROUP, add_group, 0)
-
-    for where, target in ((16, send), (0, keep)):
-        def emit(spot, carry, where=where, target=target):
-            for number in range(3):
-                target[spot, pl.ds(number * TILE, TILE), :] = total[
-                    (where + spot) * 3 + number
-                ].astype(BF16)
-            return carry
-
-        lax.fori_loop(0, 16, emit, 0)
+                spot = table[targets[number][j]]
+                code = (
+                    (begins[number] * GROUP + j)
+                    + sources[number][j] * 1024
+                    + ((spot & 127) + number) * 16384
+                )
+                send_codes[sent] = code
+                keep_codes[kept] = code
+                live = jnp.where(j < counts[number][0], 1, 0)
+                away = live & (spot >> 7)
+                sent, kept = sent + away, kept + (live - away)
+            return sent, kept
+
+        sent, kept = lax.fori_loop(
+            0, (counts[number][0] + GROUP - 1) // GROUP, sort, (sent, kept)
+        )
+    for lane in range(GROUP):
+        send_codes[sent + lane] = 48 * 16384
+        keep_codes[kept + lane] = 48 * 16384
+    keep_amount[0] = kept
+    feature_copy.wait()
+
+    def ready(waited, last):
+        return wait_tiles(tiles[0], buffer, tile_sems, waited, (last >> 4) + 1)
+
+    waited = gather_list(send_codes, sent, held, buffer, total, ready)
+    wait_tiles(tiles[0], buffer, tile_sems, waited, begins[3])
+    emit_blocks(total, send)
+
+
+def gather_keep_kernel(codes, amount, buffer, held, keep, total):
+    clear(total, 48)
+    gather_list(codes, amount[0], held, buffer, total, lambda waited, last: waited)
+    emit_blocks(total, keep)
 
 
 def in_hbm(value):
@@ -158,25 +194,44 @@
     slots = sum(relation[0].shape[0] for relation in relations)
     blocks = jax.ShapeDtypeStruct((16, 3 * TILE, width), BF16)
     features = features.reshape(-1, TILE, width)
-    return pl.pallas_call(
-        gather_kernel,
-        out_shape=(blocks, blocks),
+    total = pltpu.VMEM((49, TILE, width), F32)
+    common = dict(
+        compiler_params=pltpu.CompilerParams(vmem_limit_bytes=GATHER_LIMIT),
+        cost_estimate=pl.CostEstimate(
+            flops=2 * 10**9, bytes_accessed=12 * 10**6, transcendentals=0
+        ),
+    )
+    send, codes, amount, buffer, held = pl.pallas_call(
+        gather_send_kernel,
+        out_shape=(
+            blocks,
+            jax.ShapeDtypeStruct((slots + GROUP,), jnp.int32),
+            jax.ShapeDtypeStruct((1,), jnp.int32),
+            jax.ShapeDtypeStruct((slots, TILE, TILE), BF16),
+            jax.ShapeDtypeStruct(features.shape, BF16),
+        ),
         in_specs=[spec(SMEM)] * 10 + [spec(ANY)] * 4,
-        out_specs=(spec(VMEM), spec(VMEM)),
+        out_specs=(spec(VMEM), spec(SMEM), spec(SMEM), spec(VMEM), spec(VMEM)),
         scratch_shapes=[
-            pltpu.VMEM((slots, TILE, TILE), BF16),
-            pltpu.VMEM(features.shape, BF16),
-            pltpu.VMEM((97, TILE, width), F32),
+            total,
             pltpu.SMEM((32,), jnp.int32),
+            pltpu.SMEM((slots + GROUP,), jnp.int32),
             pltpu.SemaphoreType.DMA((slots // GROUP,)),
             pltpu.SemaphoreType.DMA(()),
         ],
-        compiler_params=pltpu.CompilerParams(vmem_limit_bytes=GATHER_LIMIT),
-        cost_estimate=pl.CostEstimate(
-            flops=3 * 10**9, bytes_accessed=18 * 10**6, transcendentals=0
-        ),
-        name="gather_sums",
+        name="gather_send",
+        **common,
     )(*flat_args(owner_map, relations), in_hbm(features), *tile_args(relations))
+    keep = pl.pallas_call(
+        gather_keep_kernel,
+        out_shape=blocks,
+        in_specs=[spec(SMEM)] * 2 + [spec(VMEM)] * 2,
+        out_specs=spec(VMEM),
+        scratch_shapes=[total],
+        name="gather_keep",
+        **common,
+    )(codes, amount, buffer, held)
+    return keep, send
 
 
 def plan_kernel(
@@ -537,9 +592,9 @@
 
     own = form_messages(grads, weights)
     own, *grads = barrier((own, *grads))
-    two, three, one = barrier(three_starts((own,) * 4))
     weight_keep, weight_send = weight_terms(grads, rounded)
     weight_got = swap(weight_send)
+    two, three, one = barrier(three_starts((own,) * 4))
     quarters = [
         add(weight_keep[4 * k:4 * k + 4], weight_got[4 * k:4 * k + 4]) for k in range(4)
     ]

time: 147 us -> 146 us (level)
  the two profiles are of different devices: /device:TPU:1 before, /device:TPU:7 now
where the time goes in v2:
time: 146 us
  waiting for transfers between devices  63.6 us (44%)
  starting transfers between devices  42.5 us (29%)
  Pallas kernels  33.2 us (23%)
  between operations  2.93 us (2%)
  other arithmetic  2.56 us (2%)
    ppermute x18, waiting for transfers between devices, shift(): return lax.ppermute(value, 'src', shift_pairs(step, second))  54.6 us
    ppermute x18, starting transfers between devices, shift(): return lax.ppermute(value, 'src', shift_pairs(step, second))  17.8 us
    ppermute x6, starting transfers between devices, swap(): return lax.ppermute(value, 'src', [(s, s ^ 1) for s in range(32)])  15.6 us
    pallas_call x1, Pallas kernels, spread_sums(): pl.pallas_call(spread_kernel, out_shape=jax.ShapeDtypeStruct((16, TILE, w...  10.5 us
    pallas_call x1, Pallas kernels, gather_sums(): pl.pallas_call(gather_send_kernel, out_shape=(blocks, jax.ShapeDtypeStruc...  9.24 us
    ppermute x6, starting transfers between devices, turn(): lax.ppermute(value, 'tgt', [(t, (t + step) % SIDE) for t in range(SIDE)])  9.06 us
    pallas_call x1, Pallas kernels, gather_sums(): pl.pallas_call(gather_keep_kernel, out_shape=blocks, in_specs=[spec(SMEM)...  7.02 us
    ppermute x6, waiting for transfers between devices, turn(): lax.ppermute(value, 'tgt', [(t, (t + step) % SIDE) for t in range(SIDE)])  6.09 us
  transfers between devices with their start and end apart: 30, of which 19 were waited for; matrix products, arithmetic and copies ran while one was open for 1% of the time, Pallas kernels for 8%

profile of v2, /device:TPU:7, one launch (start us, length us, event | category | flops | bytes accessed | tf_op | source)
XLA Modules:
  0.0 145.6 jit_solution(7625767829454345307)
XLA Ops:
  2.6 9.2 %gather_send.1 = (bf16[16,384,256]{2,1,0:T(8,128)(2,1)S(1)}, s32[352]{0:T(512)S(1)}, s32[1]{0:T(128)}, bf16[336,128,128]{2,1,0:T(8,128)(2,1)S(1)}, bf16[16,128,256]{2,1,0:T(8,128)(2,1)S(1)}) custom-call(s32[32]{0:T(128)} %owner_map.2, s32[192]{0:T(256)} %targets0.3, s32[96]{0:T(128)} %targets1.3, s32[48]{0:T(128)} %targets2.3, s32[192]{0:T(256)} %sources0.3, ...), custom_call_target="tpu_custom_call" | custom-call | flops 2000000000 | bytes 12000000 | tf_op jit(solution)/shard_map/gather_send/pallas_call | solution.py:204
  11.9 7.0 %gather_keep.1 = bf16[16,384,256]{2,1,0:T(8,128)(2,1)S(1)} custom-call(s32[352]{0:T(512)S(1)} %get-tuple-element.65.codes, s32[1]{0:T(128)} %get-tuple-element.66.amount, bf16[336,128,128]{2,1,0:T(8,128)(2,1)S(1)} %get-tuple-element.67.buffer, bf16[16,128,256]{2,1,0:T(8,128)(2,1)S(1)} %get-tuple-element.68.held), custom_call_target="tpu_custom_call" | custom-call | flops 2000000000 | bytes 12000000 | tf_op jit(solution)/shard_map/gather_keep/pallas_call | solution.py:225
  19.0 1.0 add_convert_fusion
  20.0 1.3 collective-permute-start.1
  21.3 3.6 %collective-permute-start.2 = (bf16[4,384,256]{2,1,0:T(8,128)(2,1)S(1)}, bf16[4,384,256]{2,1,0:T(8,128)(2,1)S(1)}, u32[]{:S(2)}, u32[]{:S(2)}) collective-permute-start(bf16[4,384,256]{2,1,0:T(8,128)(2,1)S(1)} %get-tuple-element.77), channel_id=1, source_target_pairs={{0,32},{4,12},{8,40},{12,20},{16,48},{20,28},{24,56},{28,4},{32,64... | collective-permute-start | bytes 2359304 | tf_op jit(solution)/shard_map/ppermute | solution.py:517
  24.8 4.2 %plan_spread.1 = (s32[216]{0:T(256)S(1)}, s32[216]{0:T(256)S(1)}, s32[216]{0:T(256)S(1)}, s32[1]{0:T(128)}) custom-call(s32[32]{0:T(128)} %owner_map.2, s32[192]{0:T(256)} %targets0.3, s32[96]{0:T(128)} %targets1.3, s32[48]{0:T(128)} %targets2.3, s32[192]{0:T(256)} %sources0.3, s32[96]{0:T(128)} %sources1.3, s32[48]{0:T(128)} %sources2.3, ...), custom_call_target="tpu_custom_call" | custom-call | flops 1000000000 | bytes 1000000 | tf_op jit(solution)/shard_map/plan_spread/pallas_call | solution.py:289
  29.1 3.4 %collective-permute-done.1 = bf16[4,384,256]{2,1,0:T(8,128)(2,1)S(1)} collective-permute-done((bf16[4,384,256]{2,1,0:T(8,128)(2,1)S(1)}, bf16[4,384,256]{2,1,0:T(8,128)(2,1)S(1)}, u32[]{:S(2)}, u32[]{:S(2)}) %collective-permute-start.1) | collective-permute-done | bytes 786464 | tf_op jit(solution)/shard_map/ppermute | solution.py:517
  32.5 8.3 %collective-permute-done.2 = bf16[4,384,256]{2,1,0:T(8,128)(2,1)S(1)} collective-permute-done((bf16[4,384,256]{2,1,0:T(8,128)(2,1)S(1)}, bf16[4,384,256]{2,1,0:T(8,128)(2,1)S(1)}, u32[]{:S(2)}, u32[]{:S(2)}) %collective-permute-start.2) | collective-permute-done | bytes 786464 | tf_op jit(solution)/shard_map/ppermute | solution.py:517
  40.8 1.9 %collective-permute-done.3 = bf16[4,384,256]{2,1,0:T(8,128)(2,1)S(1)} collective-permute-done((bf16[4,384,256]{2,1,0:T(8,128)(2,1)S(1)}, bf16[4,384,256]{2,1,0:T(8,128)(2,1)S(1)}, u32[]{:S(2)}, u32[]{:S(2)}) %collective-permute-start.3) | collective-permute-done | bytes 786464 | tf_op jit(solution)/shard_map/ppermute | solution.py:517
  43.3 1.5 collective-permute-start.6
  44.8 4.6 %collective-permute-done.4.part1 = bf16[384,256]{1,0:T(8,128)(2,1)S(1)} collective-permute-done((bf16[384,256]{1,0:T(8,128)(2,1)S(1)}, bf16[384,256]{1,0:T(8,128)(2,1)S(1)}, u32[]{:S(2)}, u32[]{:S(2)}) %collective-permute-start.4) | collective-permute-done | bytes 196640 | tf_op jit(solution)/shard_map/ppermute | solution.py:517
  49.4 2.0 %collective-permute-done.6.part3 = bf16[384,256]{1,0:T(8,128)(2,1)S(1)} collective-permute-done((bf16[384,256]{1,0:T(8,128)(2,1)S(1)}, bf16[384,256]{1,0:T(8,128)(2,1)S(1)}, u32[]{:S(2)}, u32[]{:S(2)}) %collective-permute-start.6) | collective-permute-done | bytes 196640 | tf_op jit(solution)/shard_map/ppermute | solution.py:517
  51.8 3.0 %collective-permute-start.7 = (bf16[128,256]{1,0:T(8,128)(2,1)S(1)}, bf16[128,256]{1,0:T(8,128)(2,1)S(1)}, u32[]{:S(2)}, u32[]{:S(2)}) collective-permute-start(bf16[128,256]{1,0:T(8,128)(2,1)S(1)} %get-tuple-element.89), channel_id=1, source_target_pairs={{0,2},{1,3},{2,0},{3,1},{4,6},{5,7},{6,4},{7,5},{8,10},{9,11},{10,... | collective-permute-start | bytes 196616 | tf_op jit(solution)/shard_map/ppermute | solution.py:543
  55.2 2.3 %collective-permute-start.9 = (bf16[128,256]{1,0:T(8,128)(2,1)S(1)}, bf16[128,256]{1,0:T(8,128)(2,1)S(1)}, u32[]{:S(2)}, u32[]{:S(2)}) collective-permute-start(bf16[128,256]{1,0:T(8,128)(2,1)S(1)} %get-tuple-element.91), channel_id=1, source_target_pairs={{0,3},{1,0},{2,1},{3,2},{4,7},{5,4},{6,5},{7,6},{8,11},{9,8},{10,9... | collective-permute-start | bytes 196616 | tf_op jit(solution)/shard_map/ppermute | solution.py:543
  57.5 1.6 %collective-permute-done.8 = bf16[128,256]{1,0:T(8,128)(2,1)S(1)} collective-permute-done((bf16[128,256]{1,0:T(8,128)(2,1)S(1)}, bf16[128,256]{1,0:T(8,128)(2,1)S(1)}, u32[]{:S(2)}, u32[]{:S(2)}) %collective-permute-start.8) | collective-permute-done | bytes 65568 | tf_op jit(solution)/shard_map/ppermute | solution.py:543
  59.1 0.8 fusion.6
  59.9 1.7 %collective-permute-start.10 = (bf16[128,256]{1,0:T(8,128)(2,1)S(1)}, bf16[128,256]{1,0:T(8,128)(2,1)S(1)}, u32[]{:S(2)}, u32[]{:S(2)}) collective-permute-start(bf16[128,256]{1,0:T(8,128)(2,1)S(1)} %get-tuple-element.102.grad0), channel_id=1, source_target_pairs={{0,2},{1,3},{2,0},{3,1},{4,6},{5,7},{6,4},{7,5},{8,10},{9,11},{10,... | collective-permute-start | bytes 196616 | tf_op jit(solution)/shard_map/ppermute | solution.py:543
  61.6 1.1 collective-permute-start.11
  62.7 0.6 collective-permute-start.12
  63.3 1.2 collective-permute-done.10.grad2
  64.5 1.1 collective-permute-done.11.grad1
  65.6 2.1 %collective-permute-done.12.grad3 = bf16[128,256]{1,0:T(8,128)(2,1)S(1)} collective-permute-done((bf16[128,256]{1,0:T(8,128)(2,1)S(1)}, bf16[128,256]{1,0:T(8,128)(2,1)S(1)}, u32[]{:S(2)}, u32[]{:S(2)}) %collective-permute-start.12) | collective-permute-done | bytes 65568 | tf_op jit(solution)/shard_map/ppermute | solution.py:543
  67.7 0.7 form_messages.1
  68.4 1.1 weight_terms.1
  69.6 3.4 %collective-permute-start.20 = (bf16[16,192,128]{2,1,0:T(8,128)(2,1)S(1)}, bf16[16,192,128]{2,1,0:T(8,128)(2,1)S(1)}, u32[]{:S(2)}, u32[]{:S(2)}) collective-permute-start(bf16[16,192,128]{2,1,0:T(8,128)(2,1)S(1)} %get-tuple-element.108), channel_id=1, source_target_pairs={{0,4},{4,0},{8,12},{12,8},{16,20},{20,16},{24,28},{28,24},{32,36},... | collective-permute-start | bytes 2359304 | tf_op jit(solution)/shard_map/ppermute | solution.py:521
  72.9 1.0 collective-permute-start.13
  73.9 1.9 %collective-permute-start.14 = (bf16[3,128,256]{2,1,0:T(8,128)(2,1)S(1)}, bf16[3,128,256]{2,1,0:T(8,128)(2,1)S(1)}, u32[]{:S(2)}, u32[]{:S(2)}) collective-permute-start(bf16[3,128,256]{2,1,0:T(8,128)(2,1)S(1)} %form_messages.1), channel_id=1, source_target_pairs={{0,32},{4,12},{8,40},{12,20},{16,48},{20,28},{24,56},{28,4},{32,64... | collective-permute-start | bytes 589832 | tf_op jit(solution)/shard_map/ppermute | solution.py:517
  75.9 0.7 collective-permute-start.15
  76.6 2.6 %collective-permute-done.13 = bf16[3,128,256]{2,1,0:T(8,128)(2,1)S(1)} collective-permute-done((bf16[3,128,256]{2,1,0:T(8,128)(2,1)S(1)}, bf16[3,128,256]{2,1,0:T(8,128)(2,1)S(1)}, u32[]{:S(2)}, u32[]{:S(2)}) %collective-permute-start.13) | collective-permute-done | bytes 196640 | tf_op jit(solution)/shard_map/ppermute | solution.py:517
  79.2 2.1 %collective-permute-done.14 = bf16[3,128,256]{2,1,0:T(8,128)(2,1)S(1)} collective-permute-done((bf16[3,128,256]{2,1,0:T(8,128)(2,1)S(1)}, bf16[3,128,256]{2,1,0:T(8,128)(2,1)S(1)}, u32[]{:S(2)}, u32[]{:S(2)}) %collective-permute-start.14) | collective-permute-done | bytes 196640 | tf_op jit(solution)/shard_map/ppermute | solution.py:517
  81.6 2.0 %collective-permute-start.21 = (bf16[4,192,128]{2,1,0:T(8,128)(2,1)S(1)}, bf16[4,192,128]{2,1,0:T(8,128)(2,1)S(1)}, u32[]{:S(2)}, u32[]{:S(2)}) collective-permute-start(bf16[4,192,128]{2,1,0:T(8,128)(2,1)S(1)} %get-tuple-element.140), channel_id=1, source_target_pairs={{0,16},{4,68},{8,24},{12,76},{16,0},{20,84},{24,8},{28,92},{32,48}... | collective-permute-start | bytes 589832 | tf_op jit(solution)/shard_map/ppermute | solution.py:517
  83.7 1.1 collective-permute-start.16
  85.1 1.1 collective-permute-start.18
  86.2 4.3 %collective-permute-start.19 = (bf16[12,128,256]{2,1,0:T(8,128)(2,1)S(1)}, bf16[12,128,256]{2,1,0:T(8,128)(2,1)S(1)}, u32[]{:S(2)}, u32[]{:S(2)}) collective-permute-start(bf16[12,128,256]{2,1,0:T(8,128)(2,1)S(1)} %constant_dynamic-update-slice_fusion.refs_6_), channel_id=1, source_target_pairs={{0,4},{4,0},{8,12},{12,8},{16,20},{20,16},{24,28},{28,24},{32,36},... | collective-permute-start | bytes 2359304 | tf_op jit(solution)/shard_map/ppermute | solution.py:521
  90.5 15.1 %collective-permute-done.22 = bf16[4,192,128]{2,1,0:T(8,128)(2,1)S(1)} collective-permute-done((bf16[4,192,128]{2,1,0:T(8,128)(2,1)S(1)}, bf16[4,192,128]{2,1,0:T(8,128)(2,1)S(1)}, u32[]{:S(2)}, u32[]{:S(2)}) %collective-permute-start.22) | collective-permute-done | bytes 196640 | tf_op jit(solution)/shard_map/ppermute | solution.py:517
  105.6 1.8 %collective-permute-start.23 = (bf16[4,192,128]{2,1,0:T(8,128)(2,1)S(1)}, bf16[4,192,128]{2,1,0:T(8,128)(2,1)S(1)}, u32[]{:S(2)}, u32[]{:S(2)}) collective-permute-start(bf16[4,192,128]{2,1,0:T(8,128)(2,1)S(1)} %get-tuple-element.138), channel_id=1, source_target_pairs={{0,24},{4,100},{8,0},{12,108},{16,8},{20,116},{24,16},{28,124},{32... | collective-permute-start | bytes 589832 | tf_op jit(solution)/shard_map/ppermute | solution.py:517
  107.4 3.9 %collective-permute-done.23 = bf16[4,192,128]{2,1,0:T(8,128)(2,1)S(1)} collective-permute-done((bf16[4,192,128]{2,1,0:T(8,128)(2,1)S(1)}, bf16[4,192,128]{2,1,0:T(8,128)(2,1)S(1)}, u32[]{:S(2)}, u32[]{:S(2)}) %collective-permute-start.23) | collective-permute-done | bytes 196640 | tf_op jit(solution)/shard_map/ppermute | solution.py:517
  111.4 0.7 collective-permute-start.24
  112.1 3.9 %collective-permute-done.24 = bf16[192,128]{1,0:T(8,128)(2,1)S(1)} collective-permute-done((bf16[192,128]{1,0:T(8,128)(2,1)S(1)}, bf16[192,128]{1,0:T(8,128)(2,1)S(1)}, u32[]{:S(2)}, u32[]{:S(2)}) %collective-permute-start.24) | collective-permute-done | bytes 49184 | tf_op jit(solution)/shard_map/ppermute | solution.py:517
  116.0 4.4 %collective-permute-done.25 = bf16[192,128]{1,0:T(8,128)(2,1)S(1)} collective-permute-done((bf16[192,128]{1,0:T(8,128)(2,1)S(1)}, bf16[192,128]{1,0:T(8,128)(2,1)S(1)}, u32[]{:S(2)}, u32[]{:S(2)}) %collective-permute-start.25) | collective-permute-done | bytes 49184 | tf_op jit(solution)/shard_map/ppermute | solution.py:517
  120.4 0.6 collective-permute-start.26
  121.0 2.4 %collective-permute-done.26 = bf16[192,128]{1,0:T(8,128)(2,1)S(1)} collective-permute-done((bf16[192,128]{1,0:T(8,128)(2,1)S(1)}, bf16[192,128]{1,0:T(8,128)(2,1)S(1)}, u32[]{:S(2)}, u32[]{:S(2)}) %collective-permute-start.26) | collective-permute-done | bytes 49184 | tf_op jit(solution)/shard_map/ppermute | solution.py:517
  123.4 7.3 %collective-permute-start.27 = (bf16[12,128,256]{2,1,0:T(8,128)(2,1)S(1)}, bf16[12,128,256]{2,1,0:T(8,128)(2,1)}, u32[]{:S(2)}, u32[]{:S(2)}) collective-permute-start(bf16[12,128,256]{2,1,0:T(8,128)(2,1)S(1)} %collective-permute-done.16.refs_7_), channel_id=1, source_target_pairs={{0,4},{4,0},{8,12},{12,8},{16,20},{20,16},{24,28},{28,24},{32,36},... | collective-permute-start | bytes 2359304 | tf_op jit(solution)/shard_map/ppermute | solution.py:521
  131.4 0.7 copy.21
  132.0 0.7 collective-permute-done.27.refs_11_
  132.8 1.1 collective-permute-done.28.refs_12_
  133.9 1.1 collective-permute-done.29.refs_13_
  135.0 10.5 %spread_sums.1 = bf16[16,128,256]{2,1,0:T(8,128)(2,1)} custom-call(s32[216]{0:T(256)S(1)} %get-tuple-element.119.pair_a, s32[216]{0:T(256)S(1)} %get-tuple-element.120.pair_b, s32[216]{0:T(256)S(1)} %get-tuple-element.121.pair_spot, s32[1]{0:T(128)} %get-tuple-element.122.amount, s32[1]{0:T(128)S(6)} %copy.27.counts0.refs_0_, s32[1]{0:T(128)S(6)} %copy.28.counts1.refs_1_, ...), custom_call_target="tpu_custom_call" | custom-call | flops 3000000000 | bytes 18000000 | tf_op jit(solution)/shard_map/spread_sums/pallas_call | solution.py:362
  (39 shorter events, 3.0 us)
Async XLA Ops:
  11.8 7.1 %collective-permute-start = (bf16[16,384,256]{2,1,0:T(8,128)(2,1)S(1)}, bf16[16,384,256]{2,1,0:T(8,128)(2,1)S(1)}, u32[]{:S(2)}, u32[]{:S(2)}) collective-permute-start(bf16[16,384,256]{2,1,0:T(8,128)(2,1)S(1)} %get-tuple-element.69), channel_id=1, source_target_pairs={{0,4},{4,0},{8,12},{12,8},{16,20},{20,16},{24,28},{28,24},{32,36},... | collective-permute-start | bytes 9437192 | tf_op jit(solution)/shard_map/ppermute | solution.py:521
  20.0 12.5 %collective-permute-start.1 = (bf16[4,384,256]{2,1,0:T(8,128)(2,1)S(1)}, bf16[4,384,256]{2,1,0:T(8,128)(2,1)S(1)}, u32[]{:S(2)}, u32[]{:S(2)}) collective-permute-start(bf16[4,384,256]{2,1,0:T(8,128)(2,1)S(1)} %get-tuple-element.76), channel_id=1, source_target_pairs={{0,64},{4,20},{8,72},{12,28},{16,80},{20,4},{24,88},{28,12},{32,96... | collective-permute-start | bytes 2359304 | tf_op jit(solution)/shard_map/ppermute | solution.py:517
  21.3 19.6 %collective-permute-start.2 = (bf16[4,384,256]{2,1,0:T(8,128)(2,1)S(1)}, bf16[4,384,256]{2,1,0:T(8,128)(2,1)S(1)}, u32[]{:S(2)}, u32[]{:S(2)}) collective-permute-start(bf16[4,384,256]{2,1,0:T(8,128)(2,1)S(1)} %get-tuple-element.77), channel_id=1, source_target_pairs={{0,32},{4,12},{8,40},{12,20},{16,48},{20,28},{24,56},{28,4},{32,64... | collective-permute-start | bytes 2359304 | tf_op jit(solution)/shard_map/ppermute | solution.py:517
  24.8 17.8 %collective-permute-start.3 = (bf16[4,384,256]{2,1,0:T(8,128)(2,1)S(1)}, bf16[4,384,256]{2,1,0:T(8,128)(2,1)S(1)}, u32[]{:S(2)}, u32[]{:S(2)}) collective-permute-start(bf16[4,384,256]{2,1,0:T(8,128)(2,1)S(1)} %get-tuple-element.78), channel_id=1, source_target_pairs={{0,96},{4,28},{8,104},{12,4},{16,112},{20,12},{24,120},{28,20},{32... | collective-permute-start | bytes 2359304 | tf_op jit(solution)/shard_map/ppermute | solution.py:517
  42.7 8.7 %copy-start = (bf16[3,256,1024]{2,1,0:T(8,128)(2,1)S(1)}, bf16[3,256,1024]{2,1,0:T(8,128)(2,1)}, u32[]{:S(2)}) copy-start(bf16[3,256,1024]{2,1,0:T(8,128)(2,1)} %weights.3) | copy-start | bytes 4718596
  43.1 14.4 %copy-start.2 = (bf16[256]{0:T(256)(128)(2,1)S(1)}, bf16[256]{0:T(256)(128)(2,1)}, u32[]{:S(2)}) copy-start(bf16[256]{0:T(256)(128)(2,1)} %param.32) | copy-start | bytes 1540
  43.1 16.0 %copy-start.1 = (bf16[128,256]{1,0:T(8,128)(2,1)S(1)}, bf16[128,256]{1,0:T(8,128)(2,1)}, u32[]{:S(2)}) copy-start(bf16[128,256]{1,0:T(8,128)(2,1)} %param.33) | copy-start | bytes 196612
  43.1 6.2 %collective-permute-start.4 = (bf16[384,256]{1,0:T(8,128)(2,1)S(1)}, bf16[384,256]{1,0:T(8,128)(2,1)S(1)}, u32[]{:S(2)}, u32[]{:S(2)}) collective-permute-start(bf16[384,256]{1,0:T(8,128)(2,1)S(1)} %get-tuple-element.136), channel_id=1, source_target_pairs={{0,16},{4,68},{8,24},{12,76},{16,0},{20,84},{24,8},{28,92},{32,48}... | collective-permute-start | bytes 589832 | tf_op jit(solution)/shard_map/ppermute | solution.py:517
  43.2 6.1 %collective-permute-start.5 = (bf16[384,256]{1,0:T(8,128)(2,1)S(1)}, bf16[384,256]{1,0:T(8,128)(2,1)S(1)}, u32[]{:S(2)}, u32[]{:S(2)}) collective-permute-start(bf16[384,256]{1,0:T(8,128)(2,1)S(1)} %get-tuple-element.135), channel_id=1, source_target_pairs={{0,8},{4,36},{8,16},{12,44},{16,24},{20,52},{24,0},{28,60},{32,40}... | collective-permute-start | bytes 589832 | tf_op jit(solution)/shard_map/ppermute | solution.py:517
  43.3 8.0 %collective-permute-start.6 = (bf16[384,256]{1,0:T(8,128)(2,1)S(1)}, bf16[384,256]{1,0:T(8,128)(2,1)S(1)}, u32[]{:S(2)}, u32[]{:S(2)}) collective-permute-start(bf16[384,256]{1,0:T(8,128)(2,1)S(1)} %get-tuple-element.134), channel_id=1, source_target_pairs={{0,24},{4,100},{8,0},{12,108},{16,8},{20,116},{24,16},{28,124},{32... | collective-permute-start | bytes 589832 | tf_op jit(solution)/shard_map/ppermute | solution.py:517
  51.8 5.7 %collective-permute-start.7 = (bf16[128,256]{1,0:T(8,128)(2,1)S(1)}, bf16[128,256]{1,0:T(8,128)(2,1)S(1)}, u32[]{:S(2)}, u32[]{:S(2)}) collective-permute-start(bf16[128,256]{1,0:T(8,128)(2,1)S(1)} %get-tuple-element.89), channel_id=1, source_target_pairs={{0,2},{1,3},{2,0},{3,1},{4,6},{5,7},{6,4},{7,5},{8,10},{9,11},{10,... | collective-permute-start | bytes 196616 | tf_op jit(solution)/shard_map/ppermute | solution.py:543
  54.8 4.3 %collective-permute-start.8 = (bf16[128,256]{1,0:T(8,128)(2,1)S(1)}, bf16[128,256]{1,0:T(8,128)(2,1)S(1)}, u32[]{:S(2)}, u32[]{:S(2)}) collective-permute-start(bf16[128,256]{1,0:T(8,128)(2,1)S(1)} %get-tuple-element.90), channel_id=1, source_target_pairs={{0,1},{1,2},{2,3},{3,0},{4,5},{5,6},{6,7},{7,4},{8,9},{9,10},{10,1... | collective-permute-start | bytes 196616 | tf_op jit(solution)/shard_map/ppermute | solution.py:543
  55.2 3.9 %collective-permute-start.9 = (bf16[128,256]{1,0:T(8,128)(2,1)S(1)}, bf16[128,256]{1,0:T(8,128)(2,1)S(1)}, u32[]{:S(2)}, u32[]{:S(2)}) collective-permute-start(bf16[128,256]{1,0:T(8,128)(2,1)S(1)} %get-tuple-element.91), channel_id=1, source_target_pairs={{0,3},{1,0},{2,1},{3,2},{4,7},{5,4},{6,5},{7,6},{8,11},{9,8},{10,9... | collective-permute-start | bytes 196616 | tf_op jit(solution)/shard_map/ppermute | solution.py:543
  59.9 4.6 %collective-permute-start.10 = (bf16[128,256]{1,0:T(8,128)(2,1)S(1)}, bf16[128,256]{1,0:T(8,128)(2,1)S(1)}, u32[]{:S(2)}, u32[]{:S(2)}) collective-permute-start(bf16[128,256]{1,0:T(8,128)(2,1)S(1)} %get-tuple-element.102.grad0), channel_id=1, source_target_pairs={{0,2},{1,3},{2,0},{3,1},{4,6},{5,7},{6,4},{7,5},{8,10},{9,11},{10,... | collective-permute-start | bytes 196616 | tf_op jit(solution)/shard_map/ppermute | solution.py:543
  61.6 4.0 %collective-permute-start.11 = (bf16[128,256]{1,0:T(8,128)(2,1)S(1)}, bf16[128,256]{1,0:T(8,128)(2,1)S(1)}, u32[]{:S(2)}, u32[]{:S(2)}) collective-permute-start(bf16[128,256]{1,0:T(8,128)(2,1)S(1)} %get-tuple-element.102.grad0), channel_id=1, source_target_pairs={{0,3},{1,0},{2,1},{3,2},{4,7},{5,4},{6,5},{7,6},{8,11},{9,8},{10,9... | collective-permute-start | bytes 196616 | tf_op jit(solution)/shard_map/ppermute | solution.py:543
  62.7 5.0 %collective-permute-start.12 = (bf16[128,256]{1,0:T(8,128)(2,1)S(1)}, bf16[128,256]{1,0:T(8,128)(2,1)S(1)}, u32[]{:S(2)}, u32[]{:S(2)}) collective-permute-start(bf16[128,256]{1,0:T(8,128)(2,1)S(1)} %get-tuple-element.102.grad0), channel_id=1, source_target_pairs={{0,1},{1,2},{2,3},{3,0},{4,5},{5,6},{6,7},{7,4},{8,9},{9,10},{10,1... | collective-permute-start | bytes 196616 | tf_op jit(solution)/shard_map/ppermute | solution.py:543
  69.6 11.8 %collective-permute-start.20 = (bf16[16,192,128]{2,1,0:T(8,128)(2,1)S(1)}, bf16[16,192,128]{2,1,0:T(8,128)(2,1)S(1)}, u32[]{:S(2)}, u32[]{:S(2)}) collective-permute-start(bf16[16,192,128]{2,1,0:T(8,128)(2,1)S(1)} %get-tuple-element.108), channel_id=1, source_target_pairs={{0,4},{4,0},{8,12},{12,8},{16,20},{20,16},{24,28},{28,24},{32,36},... | collective-permute-start | bytes 2359304 | tf_op jit(solution)/shard_map/ppermute | solution.py:521
  72.9 6.3 %collective-permute-start.13 = (bf16[3,128,256]{2,1,0:T(8,128)(2,1)S(1)}, bf16[3,128,256]{2,1,0:T(8,128)(2,1)S(1)}, u32[]{:S(2)}, u32[]{:S(2)}) collective-permute-start(bf16[3,128,256]{2,1,0:T(8,128)(2,1)S(1)} %form_messages.1), channel_id=1, source_target_pairs={{0,64},{4,20},{8,72},{12,28},{16,80},{20,4},{24,88},{28,12},{32,96... | collective-permute-start | bytes 589832 | tf_op jit(solution)/shard_map/ppermute | solution.py:517
  73.9 7.4 %collective-permute-start.14 = (bf16[3,128,256]{2,1,0:T(8,128)(2,1)S(1)}, bf16[3,128,256]{2,1,0:T(8,128)(2,1)S(1)}, u32[]{:S(2)}, u32[]{:S(2)}) collective-permute-start(bf16[3,128,256]{2,1,0:T(8,128)(2,1)S(1)} %form_messages.1), channel_id=1, source_target_pairs={{0,32},{4,12},{8,40},{12,20},{16,48},{20,28},{24,56},{28,4},{32,64... | collective-permute-start | bytes 589832 | tf_op jit(solution)/shard_map/ppermute | solution.py:517
  75.9 5.5 %collective-permute-start.15 = (bf16[3,128,256]{2,1,0:T(8,128)(2,1)S(1)}, bf16[3,128,256]{2,1,0:T(8,128)(2,1)S(1)}, u32[]{:S(2)}, u32[]{:S(2)}) collective-permute-start(bf16[3,128,256]{2,1,0:T(8,128)(2,1)S(1)} %form_messages.1), channel_id=1, source_target_pairs={{0,96},{4,28},{8,104},{12,4},{16,112},{20,12},{24,120},{28,20},{32... | collective-permute-start | bytes 589832 | tf_op jit(solution)/shard_map/ppermute | solution.py:517
  81.6 8.9 %collective-permute-start.21 = (bf16[4,192,128]{2,1,0:T(8,128)(2,1)S(1)}, bf16[4,192,128]{2,1,0:T(8,128)(2,1)S(1)}, u32[]{:S(2)}, u32[]{:S(2)}) collective-permute-start(bf16[4,192,128]{2,1,0:T(8,128)(2,1)S(1)} %get-tuple-element.140), channel_id=1, source_target_pairs={{0,16},{4,68},{8,24},{12,76},{16,0},{20,84},{24,8},{28,92},{32,48}... | collective-permute-start | bytes 589832 | tf_op jit(solution)/shard_map/ppermute | solution.py:517
  83.7 39.7 %collective-permute-start.16 = (bf16[12,128,256]{2,1,0:T(8,128)(2,1)S(1)}, bf16[12,128,256]{2,1,0:T(8,128)(2,1)S(1)}, u32[]{:S(2)}, u32[]{:S(2)}) collective-permute-start(bf16[12,128,256]{2,1,0:T(8,128)(2,1)S(1)} %constant_dynamic-update-slice_fusion.refs_6_), channel_id=1, source_target_pairs={{0,16},{4,68},{8,24},{12,76},{16,0},{20,84},{24,8},{28,92},{32,48}... | collective-permute-start | bytes 2359304 | tf_op jit(solution)/shard_map/ppermute | solution.py:517
  84.8 38.6 %collective-permute-start.17 = (bf16[12,128,256]{2,1,0:T(8,128)(2,1)S(1)}, bf16[12,128,256]{2,1,0:T(8,128)(2,1)S(1)}, u32[]{:S(2)}, u32[]{:S(2)}) collective-permute-start(bf16[12,128,256]{2,1,0:T(8,128)(2,1)S(1)} %constant_dynamic-update-slice_fusion.refs_6_), channel_id=1, source_target_pairs={{0,8},{4,36},{8,16},{12,44},{16,24},{20,52},{24,0},{28,60},{32,40}... | collective-permute-start | bytes 2359304 | tf_op jit(solution)/shard_map/ppermute | solution.py:517
  85.1 38.3 %collective-permute-start.18 = (bf16[12,128,256]{2,1,0:T(8,128)(2,1)S(1)}, bf16[12,128,256]{2,1,0:T(8,128)(2,1)}, u32[]{:S(2)}, u32[]{:S(2)}) collective-permute-start(bf16[12,128,256]{2,1,0:T(8,128)(2,1)S(1)} %constant_dynamic-update-slice_fusion.refs_6_), channel_id=1, source_target_pairs={{0,24},{4,100},{8,0},{12,108},{16,8},{20,116},{24,16},{28,124},{32... | collective-permute-start | bytes 2359304 | tf_op jit(solution)/shard_map/ppermute | solution.py:517
  86.2 37.1 %collective-permute-start.19 = (bf16[12,128,256]{2,1,0:T(8,128)(2,1)S(1)}, bf16[12,128,256]{2,1,0:T(8,128)(2,1)S(1)}, u32[]{:S(2)}, u32[]{:S(2)}) collective-permute-start(bf16[12,128,256]{2,1,0:T(8,128)(2,1)S(1)} %constant_dynamic-update-slice_fusion.refs_6_), channel_id=1, source_target_pairs={{0,4},{4,0},{8,12},{12,8},{16,20},{20,16},{24,28},{28,24},{32,36},... | collective-permute-start | bytes 2359304 | tf_op jit(solution)/shard_map/ppermute | solution.py:521
  90.5 15.1 %collective-permute-start.22 = (bf16[4,192,128]{2,1,0:T(8,128)(2,1)S(1)}, bf16[4,192,128]{2,1,0:T(8,128)(2,1)S(1)}, u32[]{:S(2)}, u32[]{:S(2)}) collective-permute-start(bf16[4,192,128]{2,1,0:T(8,128)(2,1)S(1)} %get-tuple-element.139), channel_id=1, source_target_pairs={{0,8},{4,36},{8,16},{12,44},{16,24},{20,52},{24,0},{28,60},{32,40}... | collective-permute-start | bytes 589832 | tf_op jit(solution)/shard_map/ppermute | solution.py:517
  105.6 5.7 %collective-permute-start.23 = (bf16[4,192,128]{2,1,0:T(8,128)(2,1)S(1)}, bf16[4,192,128]{2,1,0:T(8,128)(2,1)S(1)}, u32[]{:S(2)}, u32[]{:S(2)}) collective-permute-start(bf16[4,192,128]{2,1,0:T(8,128)(2,1)S(1)} %get-tuple-element.138), channel_id=1, source_target_pairs={{0,24},{4,100},{8,0},{12,108},{16,8},{20,116},{24,16},{28,124},{32... | collective-permute-start | bytes 589832 | tf_op jit(solution)/shard_map/ppermute | solution.py:517
  111.4 4.5 %collective-permute-start.24 = (bf16[192,128]{1,0:T(8,128)(2,1)S(1)}, bf16[192,128]{1,0:T(8,128)(2,1)S(1)}, u32[]{:S(2)}, u32[]{:S(2)}) collective-permute-start(bf16[192,128]{1,0:T(8,128)(2,1)S(1)} %get-tuple-element.144), channel_id=1, source_target_pairs={{0,64},{4,20},{8,72},{12,28},{16,80},{20,4},{24,88},{28,12},{32,96... | collective-permute-start | bytes 147464 | tf_op jit(solution)/shard_map/ppermute | solution.py:517
  116.0 4.4 %collective-permute-start.25 = (bf16[192,128]{1,0:T(8,128)(2,1)S(1)}, bf16[192,128]{1,0:T(8,128)(2,1)S(1)}, u32[]{:S(2)}, u32[]{:S(2)}) collective-permute-start(bf16[192,128]{1,0:T(8,128)(2,1)S(1)} %get-tuple-element.143), channel_id=1, source_target_pairs={{0,32},{4,12},{8,40},{12,20},{16,48},{20,28},{24,56},{28,4},{32,64... | collective-permute-start | bytes 147464 | tf_op jit(solution)/shard_map/ppermute | solution.py:517
  120.4 2.9 %collective-permute-start.26 = (bf16[192,128]{1,0:T(8,128)(2,1)S(1)}, bf16[192,128]{1,0:T(8,128)(2,1)S(1)}, u32[]{:S(2)}, u32[]{:S(2)}) collective-permute-start(bf16[192,128]{1,0:T(8,128)(2,1)S(1)} %get-tuple-element.142), channel_id=1, source_target_pairs={{0,96},{4,28},{8,104},{12,4},{16,112},{20,12},{24,120},{28,20},{32... | collective-permute-start | bytes 147464 | tf_op jit(solution)/shard_map/ppermute | solution.py:517
  123.4 9.4 %collective-permute-start.27 = (bf16[12,128,256]{2,1,0:T(8,128)(2,1)S(1)}, bf16[12,128,256]{2,1,0:T(8,128)(2,1)}, u32[]{:S(2)}, u32[]{:S(2)}) collective-permute-start(bf16[12,128,256]{2,1,0:T(8,128)(2,1)S(1)} %collective-permute-done.16.refs_7_), channel_id=1, source_target_pairs={{0,4},{4,0},{8,12},{12,8},{16,20},{20,16},{24,28},{28,24},{32,36},... | collective-permute-start | bytes 2359304 | tf_op jit(solution)/shard_map/ppermute | solution.py:521
  130.7 3.2 %collective-permute-start.28 = (bf16[12,128,256]{2,1,0:T(8,128)(2,1)S(1)}, bf16[12,128,256]{2,1,0:T(8,128)(2,1)}, u32[]{:S(2)}, u32[]{:S(2)}) collective-permute-start(bf16[12,128,256]{2,1,0:T(8,128)(2,1)S(1)} %collective-permute-done.17.refs_8_), channel_id=1, source_target_pairs={{0,4},{4,0},{8,12},{12,8},{16,20},{20,16},{24,28},{28,24},{32,36},... | collective-permute-start | bytes 2359304 | tf_op jit(solution)/shard_map/ppermute | solution.py:521
  130.8 4.2 %collective-permute-start.29 = (bf16[12,128,256]{2,1,0:T(8,128)(2,1)}, bf16[12,128,256]{2,1,0:T(8,128)(2,1)}, u32[]{:S(2)}, u32[]{:S(2)}) collective-permute-start(bf16[12,128,256]{2,1,0:T(8,128)(2,1)} %collective-permute-done.18.refs_9_), channel_id=1, source_target_pairs={{0,4},{4,0},{8,12},{12,8},{16,20},{20,16},{24,28},{28,24},{32,36},... | collective-permute-start | bytes 2359304 | tf_op jit(solution)/shard_map/ppermute | solution.py:521

commit v3 on v2

--- a/solution.py
+++ b/solution.py
@@ -453,6 +453,38 @@
     )(*grads, weights)
 
 
+def add_kernel(left, right, out):
+    out[...] = (left[...].astype(F32) + right[...].astype(F32)).astype(BF16)
+
+
+def add_blocks(left, right):
+    return pl.pallas_call(
+        add_kernel,
+        out_shape=jax.ShapeDtypeStruct(left.shape, BF16),
+        in_specs=[spec(VMEM)] * 2,
+        out_specs=spec(VMEM),
+        compiler_params=pltpu.CompilerParams(vmem_limit_bytes=8 * MIB),
+        name="add_blocks",
+    )(left, right)
+
+
+def join_kernel(*refs):
+    for number, ref in enumerate(refs[:-1]):
+        refs[-1][pl.ds(number * ref.shape[0], ref.shape[0])] = ref[...]
+
+
+def join(blocks):
+    shape = (sum(block.shape[0] for block in blocks), *blocks[0].shape[1:])
+    return pl.pallas_call(
+        join_kernel,
+        out_shape=jax.ShapeDtypeStruct(shape, BF16),
+        in_specs=[spec(VMEM)] * len(blocks),
+        out_specs=spec(VMEM),
+        compiler_params=pltpu.CompilerParams(vmem_limit_bytes=8 * MIB),
+        name="join_blocks",
+    )(*blocks)
+
+
 def weight_kernel(grad0, grad1, grad2, grad3, rounded, keep, send, staged, sems):
     mine = here()
     block0 = lax.axis_index("tgt")
@@ -596,10 +628,11 @@
     weight_got = swap(weight_send)
     two, three, one = barrier(three_starts((own,) * 4))
     quarters = [
-        add(weight_keep[4 * k:4 * k + 4], weight_got[4 * k:4 * k + 4]) for k in range(4)
+        add(weight_keep[4 * k:4 * k + 4], weight_got[4 * k:4 * k + 4]) for k in range(1, 4)
     ]
+    quarters = [add_blocks(weight_keep[:4], weight_got[:4]), *quarters]
     arrived = barrier(three_starts(quarters, True))
-    whole = jnp.concatenate([own, one, two, three])
+    whole = join((own, one, two, three))
     spread_out = three_starts((whole,) * 4, True)
     beside = swap(whole)
     line = [add(quarters[0][k], *[part[k] for part in arrived]) for k in range(4)]

time: 146 us -> 146 us (level)
  starting transfers between devices: 42.5 us -> 46.8 us
  waiting for transfers between devices: 63.6 us -> 59.6 us
    ppermute x18, waiting for transfers between devices: 54.6 us -> 50.5 us  [shift(): return lax.ppermute(value, 'src', shift_pairs(step, second))]
    ppermute x6, starting transfers between devices: 15.6 us -> 18.6 us  [swap(): return lax.ppermute(value, 'src', [(s, s ^ 1) for s in range(32)])]
where the time goes in v3:
time: 146 us
  waiting for transfers between devices  59.6 us (41%)
  starting transfers between devices  46.8 us (32%)
  Pallas kernels  33.3 us (23%)
  between operations  2.92 us (2%)
  other arithmetic  2.49 us (2%)
    ppermute x18, waiting for transfers between devices, shift(): return lax.ppermute(value, 'src', shift_pairs(step, second))  50.5 us
    ppermute x18, starting transfers between devices, shift(): return lax.ppermute(value, 'src', shift_pairs(step, second))  19.1 us
    ppermute x6, starting transfers between devices, swap(): return lax.ppermute(value, 'src', [(s, s ^ 1) for s in range(32)])  18.6 us
    pallas_call x1, Pallas kernels, spread_sums(): pl.pallas_call(spread_kernel, out_shape=jax.ShapeDtypeStruct((16, TILE, w...  10.5 us
    pallas_call x1, Pallas kernels, gather_sums(): pl.pallas_call(gather_send_kernel, out_shape=(blocks, jax.ShapeDtypeStruc...  9.24 us
    ppermute x6, starting transfers between devices, turn(): lax.ppermute(value, 'tgt', [(t, (t + step) % SIDE) for t in range(SIDE)])  9.06 us
    pallas_call x1, Pallas kernels, gather_sums(): pl.pallas_call(gather_keep_kernel, out_shape=blocks, in_specs=[spec(SMEM)...  7.02 us
    ppermute x6, waiting for transfers between devices, turn(): lax.ppermute(value, 'tgt', [(t, (t + step) % SIDE) for t in range(SIDE)])  6.09 us
  transfers between devices with their start and end apart: 30, of which 19 were waited for; matrix products, arithmetic and copies ran while one was open for 1% of the time, Pallas kernels for 8%

profile of v3, /device:TPU:7, one launch (start us, length us, event | category | flops | bytes accessed | tf_op | source)
XLA Modules:
  0.0 145.9 jit_solution(16703816824775201767)
XLA Ops:
  2.6 9.2 %gather_send.1 = (bf16[16,384,256]{2,1,0:T(8,128)(2,1)S(1)}, s32[352]{0:T(512)S(1)}, s32[1]{0:T(128)}, bf16[336,128,128]{2,1,0:T(8,128)(2,1)S(1)}, bf16[16,128,256]{2,1,0:T(8,128)(2,1)S(1)}) custom-call(s32[32]{0:T(128)} %owner_map.2, s32[192]{0:T(256)} %targets0.3, s32[96]{0:T(128)} %targets1.3, s32[48]{0:T(128)} %targets2.3, s32[192]{0:T(256)} %sources0.3, ...), custom_call_target="tpu_custom_call" | custom-call | flops 2000000000 | bytes 12000000 | tf_op jit(solution)/shard_map/gather_send/pallas_call | solution.py:204
  11.9 7.0 %gather_keep.1 = bf16[16,384,256]{2,1,0:T(8,128)(2,1)S(1)} custom-call(s32[352]{0:T(512)S(1)} %get-tuple-element.65.codes, s32[1]{0:T(128)} %get-tuple-element.66.amount, bf16[336,128,128]{2,1,0:T(8,128)(2,1)S(1)} %get-tuple-element.67.buffer, bf16[16,128,256]{2,1,0:T(8,128)(2,1)S(1)} %get-tuple-element.68.held), custom_call_target="tpu_custom_call" | custom-call | flops 2000000000 | bytes 12000000 | tf_op jit(solution)/shard_map/gather_keep/pallas_call | solution.py:225
  19.0 1.0 add_convert_fusion
  20.0 1.3 collective-permute-start.1
  21.3 3.6 %collective-permute-start.2 = (bf16[4,384,256]{2,1,0:T(8,128)(2,1)S(1)}, bf16[4,384,256]{2,1,0:T(8,128)(2,1)S(1)}, u32[]{:S(2)}, u32[]{:S(2)}) collective-permute-start(bf16[4,384,256]{2,1,0:T(8,128)(2,1)S(1)} %get-tuple-element.77), channel_id=1, source_target_pairs={{0,32},{4,12},{8,40},{12,20},{16,48},{20,28},{24,56},{28,4},{32,64... | collective-permute-start | bytes 2359304 | tf_op jit(solution)/shard_map/ppermute | solution.py:549
  24.8 4.2 %plan_spread.1 = (s32[216]{0:T(256)S(1)}, s32[216]{0:T(256)S(1)}, s32[216]{0:T(256)S(1)}, s32[1]{0:T(128)}) custom-call(s32[32]{0:T(128)} %owner_map.2, s32[192]{0:T(256)} %targets0.3, s32[96]{0:T(128)} %targets1.3, s32[48]{0:T(128)} %targets2.3, s32[192]{0:T(256)} %sources0.3, s32[96]{0:T(128)} %sources1.3, s32[48]{0:T(128)} %sources2.3, ...), custom_call_target="tpu_custom_call" | custom-call | flops 1000000000 | bytes 1000000 | tf_op jit(solution)/shard_map/plan_spread/pallas_call | solution.py:289
  29.1 3.4 %collective-permute-done.1 = bf16[4,384,256]{2,1,0:T(8,128)(2,1)S(1)} collective-permute-done((bf16[4,384,256]{2,1,0:T(8,128)(2,1)S(1)}, bf16[4,384,256]{2,1,0:T(8,128)(2,1)S(1)}, u32[]{:S(2)}, u32[]{:S(2)}) %collective-permute-start.1) | collective-permute-done | bytes 786464 | tf_op jit(solution)/shard_map/ppermute | solution.py:549
  32.5 8.3 %collective-permute-done.2 = bf16[4,384,256]{2,1,0:T(8,128)(2,1)S(1)} collective-permute-done((bf16[4,384,256]{2,1,0:T(8,128)(2,1)S(1)}, bf16[4,384,256]{2,1,0:T(8,128)(2,1)S(1)}, u32[]{:S(2)}, u32[]{:S(2)}) %collective-permute-start.2) | collective-permute-done | bytes 786464 | tf_op jit(solution)/shard_map/ppermute | solution.py:549
  40.8 1.9 %collective-permute-done.3 = bf16[4,384,256]{2,1,0:T(8,128)(2,1)S(1)} collective-permute-done((bf16[4,384,256]{2,1,0:T(8,128)(2,1)S(1)}, bf16[4,384,256]{2,1,0:T(8,128)(2,1)S(1)}, u32[]{:S(2)}, u32[]{:S(2)}) %collective-permute-start.3) | collective-permute-done | bytes 786464 | tf_op jit(solution)/shard_map/ppermute | solution.py:549
  43.3 1.5 collective-permute-start.6
  44.8 4.6 %collective-permute-done.4.part1 = bf16[384,256]{1,0:T(8,128)(2,1)S(1)} collective-permute-done((bf16[384,256]{1,0:T(8,128)(2,1)S(1)}, bf16[384,256]{1,0:T(8,128)(2,1)S(1)}, u32[]{:S(2)}, u32[]{:S(2)}) %collective-permute-start.4) | collective-permute-done | bytes 196640 | tf_op jit(solution)/shard_map/ppermute | solution.py:549
  49.4 2.0 %collective-permute-done.6.part3 = bf16[384,256]{1,0:T(8,128)(2,1)S(1)} collective-permute-done((bf16[384,256]{1,0:T(8,128)(2,1)S(1)}, bf16[384,256]{1,0:T(8,128)(2,1)S(1)}, u32[]{:S(2)}, u32[]{:S(2)}) %collective-permute-start.6) | collective-permute-done | bytes 196640 | tf_op jit(solution)/shard_map/ppermute | solution.py:549
  51.8 3.0 %collective-permute-start.7 = (bf16[128,256]{1,0:T(8,128)(2,1)S(1)}, bf16[128,256]{1,0:T(8,128)(2,1)S(1)}, u32[]{:S(2)}, u32[]{:S(2)}) collective-permute-start(bf16[128,256]{1,0:T(8,128)(2,1)S(1)} %get-tuple-element.89), channel_id=1, source_target_pairs={{0,2},{1,3},{2,0},{3,1},{4,6},{5,7},{6,4},{7,5},{8,10},{9,11},{10,... | collective-permute-start | bytes 196616 | tf_op jit(solution)/shard_map/ppermute | solution.py:575
  55.2 2.3 %collective-permute-start.9 = (bf16[128,256]{1,0:T(8,128)(2,1)S(1)}, bf16[128,256]{1,0:T(8,128)(2,1)S(1)}, u32[]{:S(2)}, u32[]{:S(2)}) collective-permute-start(bf16[128,256]{1,0:T(8,128)(2,1)S(1)} %get-tuple-element.91), channel_id=1, source_target_pairs={{0,3},{1,0},{2,1},{3,2},{4,7},{5,4},{6,5},{7,6},{8,11},{9,8},{10,9... | collective-permute-start | bytes 196616 | tf_op jit(solution)/shard_map/ppermute | solution.py:575
  57.5 1.6 %collective-permute-done.8 = bf16[128,256]{1,0:T(8,128)(2,1)S(1)} collective-permute-done((bf16[128,256]{1,0:T(8,128)(2,1)S(1)}, bf16[128,256]{1,0:T(8,128)(2,1)S(1)}, u32[]{:S(2)}, u32[]{:S(2)}) %collective-permute-start.8) | collective-permute-done | bytes 65568 | tf_op jit(solution)/shard_map/ppermute | solution.py:575
  59.1 0.8 fusion.6
  59.9 1.7 %collective-permute-start.10 = (bf16[128,256]{1,0:T(8,128)(2,1)S(1)}, bf16[128,256]{1,0:T(8,128)(2,1)S(1)}, u32[]{:S(2)}, u32[]{:S(2)}) collective-permute-start(bf16[128,256]{1,0:T(8,128)(2,1)S(1)} %get-tuple-element.102.grad0), channel_id=1, source_target_pairs={{0,2},{1,3},{2,0},{3,1},{4,6},{5,7},{6,4},{7,5},{8,10},{9,11},{10,... | collective-permute-start | bytes 196616 | tf_op jit(solution)/shard_map/ppermute | solution.py:575
  61.6 1.1 collective-permute-start.11
  63.3 1.2 collective-permute-done.10.grad2
  64.5 1.1 collective-permute-done.11.grad1
  65.6 2.1 %collective-permute-done.12.grad3 = bf16[128,256]{1,0:T(8,128)(2,1)S(1)} collective-permute-done((bf16[128,256]{1,0:T(8,128)(2,1)S(1)}, bf16[128,256]{1,0:T(8,128)(2,1)S(1)}, u32[]{:S(2)}, u32[]{:S(2)}) %collective-permute-start.12) | collective-permute-done | bytes 65568 | tf_op jit(solution)/shard_map/ppermute | solution.py:575
  67.7 0.7 form_messages.1.refs_0_
  68.4 1.1 weight_terms.1
  69.6 3.4 %collective-permute-start.20 = (bf16[16,192,128]{2,1,0:T(8,128)(2,1)S(1)}, bf16[16,192,128]{2,1,0:T(8,128)(2,1)S(1)}, u32[]{:S(2)}, u32[]{:S(2)}) collective-permute-start(bf16[16,192,128]{2,1,0:T(8,128)(2,1)S(1)} %get-tuple-element.108), channel_id=1, source_target_pairs={{0,4},{4,0},{8,12},{12,8},{16,20},{20,16},{24,28},{28,24},{32,36},... | collective-permute-start | bytes 2359304 | tf_op jit(solution)/shard_map/ppermute | solution.py:553
  72.9 1.0 collective-permute-start.13
  73.9 1.9 %collective-permute-start.14 = (bf16[3,128,256]{2,1,0:T(8,128)(2,1)S(1)}, bf16[3,128,256]{2,1,0:T(8,128)(2,1)S(1)}, u32[]{:S(2)}, u32[]{:S(2)}) collective-permute-start(bf16[3,128,256]{2,1,0:T(8,128)(2,1)S(1)} %form_messages.1.refs_0_), channel_id=1, source_target_pairs={{0,32},{4,12},{8,40},{12,20},{16,48},{20,28},{24,56},{28,4},{32,64... | collective-permute-start | bytes 589832 | tf_op jit(solution)/shard_map/ppermute | solution.py:549
  75.9 0.7 collective-permute-start.15
  76.8 1.3 collective-permute-start.21
  78.1 1.2 collective-permute-done.13.refs_2_
  79.2 2.1 %collective-permute-done.14.refs_3_ = bf16[3,128,256]{2,1,0:T(8,128)(2,1)S(1)} collective-permute-done((bf16[3,128,256]{2,1,0:T(8,128)(2,1)S(1)}, bf16[3,128,256]{2,1,0:T(8,128)(2,1)S(1)}, u32[]{:S(2)}, u32[]{:S(2)}) %collective-permute-start.14) | collective-permute-done | bytes 196640 | tf_op jit(solution)/shard_map/ppermute | solution.py:549
  81.4 2.1 %collective-permute-start.16 = (bf16[12,128,256]{2,1,0:T(8,128)(2,1)S(1)}, bf16[12,128,256]{2,1,0:T(8,128)(2,1)S(1)}, u32[]{:S(2)}, u32[]{:S(2)}) collective-permute-start(bf16[12,128,256]{2,1,0:T(8,128)(2,1)S(1)} %join_blocks.1.refs_6_), channel_id=1, source_target_pairs={{0,16},{4,68},{8,24},{12,76},{16,0},{20,84},{24,8},{28,92},{32,48}... | collective-permute-start | bytes 2359304 | tf_op jit(solution)/shard_map/ppermute | solution.py:549
  83.5 0.9 collective-permute-start.17
  84.3 0.6 collective-permute-start.18
  84.9 4.4 %collective-permute-start.19 = (bf16[12,128,256]{2,1,0:T(8,128)(2,1)S(1)}, bf16[12,128,256]{2,1,0:T(8,128)(2,1)S(1)}, u32[]{:S(2)}, u32[]{:S(2)}) collective-permute-start(bf16[12,128,256]{2,1,0:T(8,128)(2,1)S(1)} %join_blocks.1.refs_6_), channel_id=1, source_target_pairs={{0,4},{4,0},{8,12},{12,8},{16,20},{20,16},{24,28},{28,24},{32,36},... | collective-permute-start | bytes 2359304 | tf_op jit(solution)/shard_map/ppermute | solution.py:553
  89.4 13.4 %collective-permute-done.22 = bf16[4,192,128]{2,1,0:T(8,128)(2,1)S(1)} collective-permute-done((bf16[4,192,128]{2,1,0:T(8,128)(2,1)S(1)}, bf16[4,192,128]{2,1,0:T(8,128)(2,1)S(1)}, u32[]{:S(2)}, u32[]{:S(2)}) %collective-permute-start.22) | collective-permute-done | bytes 196640 | tf_op jit(solution)/shard_map/ppermute | solution.py:549
  102.7 1.7 %collective-permute-start.23 = (bf16[4,192,128]{2,1,0:T(8,128)(2,1)S(1)}, bf16[4,192,128]{2,1,0:T(8,128)(2,1)S(1)}, u32[]{:S(2)}, u32[]{:S(2)}) collective-permute-start(bf16[4,192,128]{2,1,0:T(8,128)(2,1)S(1)} %get-tuple-element.138), channel_id=1, source_target_pairs={{0,24},{4,100},{8,0},{12,108},{16,8},{20,116},{24,16},{28,124},{32... | collective-permute-start | bytes 589832 | tf_op jit(solution)/shard_map/ppermute | solution.py:549
  104.5 4.2 %collective-permute-done.23 = bf16[4,192,128]{2,1,0:T(8,128)(2,1)S(1)} collective-permute-done((bf16[4,192,128]{2,1,0:T(8,128)(2,1)S(1)}, bf16[4,192,128]{2,1,0:T(8,128)(2,1)S(1)}, u32[]{:S(2)}, u32[]{:S(2)}) %collective-permute-start.23) | collective-permute-done | bytes 196640 | tf_op jit(solution)/shard_map/ppermute | solution.py:549
  108.9 0.8 collective-permute-start.24
  109.7 3.7 %collective-permute-done.24 = bf16[192,128]{1,0:T(8,128)(2,1)S(1)} collective-permute-done((bf16[192,128]{1,0:T(8,128)(2,1)S(1)}, bf16[192,128]{1,0:T(8,128)(2,1)S(1)}, u32[]{:S(2)}, u32[]{:S(2)}) %collective-permute-start.24) | collective-permute-done | bytes 49184 | tf_op jit(solution)/shard_map/ppermute | solution.py:549
  113.6 3.9 %collective-permute-done.25 = bf16[192,128]{1,0:T(8,128)(2,1)S(1)} collective-permute-done((bf16[192,128]{1,0:T(8,128)(2,1)S(1)}, bf16[192,128]{1,0:T(8,128)(2,1)S(1)}, u32[]{:S(2)}, u32[]{:S(2)}) %collective-permute-start.25) | collective-permute-done | bytes 49184 | tf_op jit(solution)/shard_map/ppermute | solution.py:549
  117.6 1.4 collective-permute-start.26
  119.0 1.8 %collective-permute-done.26 = bf16[192,128]{1,0:T(8,128)(2,1)S(1)} collective-permute-done((bf16[192,128]{1,0:T(8,128)(2,1)S(1)}, bf16[192,128]{1,0:T(8,128)(2,1)S(1)}, u32[]{:S(2)}, u32[]{:S(2)}) %collective-permute-start.26) | collective-permute-done | bytes 49184 | tf_op jit(solution)/shard_map/ppermute | solution.py:549
  120.8 10.2 %collective-permute-start.27 = (bf16[12,128,256]{2,1,0:T(8,128)(2,1)S(1)}, bf16[12,128,256]{2,1,0:T(8,128)(2,1)}, u32[]{:S(2)}, u32[]{:S(2)}) collective-permute-start(bf16[12,128,256]{2,1,0:T(8,128)(2,1)S(1)} %collective-permute-done.16.refs_7_), channel_id=1, source_target_pairs={{0,4},{4,0},{8,12},{12,8},{16,20},{20,16},{24,28},{28,24},{32,36},... | collective-permute-start | bytes 2359304 | tf_op jit(solution)/shard_map/ppermute | solution.py:553
  131.7 0.7 copy.21
  132.4 0.7 collective-permute-done.27.refs_11_
  133.1 1.1 collective-permute-done.28.refs_12_
  134.2 1.1 collective-permute-done.29.refs_13_
  135.3 10.5 %spread_sums.1 = bf16[16,128,256]{2,1,0:T(8,128)(2,1)} custom-call(s32[216]{0:T(256)S(1)} %get-tuple-element.119.pair_a, s32[216]{0:T(256)S(1)} %get-tuple-element.120.pair_b, s32[216]{0:T(256)S(1)} %get-tuple-element.121.pair_spot, s32[1]{0:T(128)} %get-tuple-element.122.amount, s32[1]{0:T(128)S(6)} %copy.24.counts0.refs_0_, s32[1]{0:T(128)S(6)} %copy.25.counts1.refs_1_, ...), custom_call_target="tpu_custom_call" | custom-call | flops 3000000000 | bytes 18000000 | tf_op jit(solution)/shard_map/spread_sums/pallas_call | solution.py:362
  (39 shorter events, 3.4 us)
Async XLA Ops:
  11.8 7.1 %collective-permute-start = (bf16[16,384,256]{2,1,0:T(8,128)(2,1)S(1)}, bf16[16,384,256]{2,1,0:T(8,128)(2,1)S(1)}, u32[]{:S(2)}, u32[]{:S(2)}) collective-permute-start(bf16[16,384,256]{2,1,0:T(8,128)(2,1)S(1)} %get-tuple-element.69), channel_id=1, source_target_pairs={{0,4},{4,0},{8,12},{12,8},{16,20},{20,16},{24,28},{28,24},{32,36},... | collective-permute-start | bytes 9437192 | tf_op jit(solution)/shard_map/ppermute | solution.py:553
  20.0 12.5 %collective-permute-start.1 = (bf16[4,384,256]{2,1,0:T(8,128)(2,1)S(1)}, bf16[4,384,256]{2,1,0:T(8,128)(2,1)S(1)}, u32[]{:S(2)}, u32[]{:S(2)}) collective-permute-start(bf16[4,384,256]{2,1,0:T(8,128)(2,1)S(1)} %get-tuple-element.76), channel_id=1, source_target_pairs={{0,64},{4,20},{8,72},{12,28},{16,80},{20,4},{24,88},{28,12},{32,96... | collective-permute-start | bytes 2359304 | tf_op jit(solution)/shard_map/ppermute | solution.py:549
  21.3 19.6 %collective-permute-start.2 = (bf16[4,384,256]{2,1,0:T(8,128)(2,1)S(1)}, bf16[4,384,256]{2,1,0:T(8,128)(2,1)S(1)}, u32[]{:S(2)}, u32[]{:S(2)}) collective-permute-start(bf16[4,384,256]{2,1,0:T(8,128)(2,1)S(1)} %get-tuple-element.77), channel_id=1, source_target_pairs={{0,32},{4,12},{8,40},{12,20},{16,48},{20,28},{24,56},{28,4},{32,64... | collective-permute-start | bytes 2359304 | tf_op jit(solution)/shard_map/ppermute | solution.py:549
  24.8 17.8 %collective-permute-start.3 = (bf16[4,384,256]{2,1,0:T(8,128)(2,1)S(1)}, bf16[4,384,256]{2,1,0:T(8,128)(2,1)S(1)}, u32[]{:S(2)}, u32[]{:S(2)}) collective-permute-start(bf16[4,384,256]{2,1,0:T(8,128)(2,1)S(1)} %get-tuple-element.78), channel_id=1, source_target_pairs={{0,96},{4,28},{8,104},{12,4},{16,112},{20,12},{24,120},{28,20},{32... | collective-permute-start | bytes 2359304 | tf_op jit(solution)/shard_map/ppermute | solution.py:549
  42.7 8.7 %copy-start = (bf16[3,256,1024]{2,1,0:T(8,128)(2,1)S(1)}, bf16[3,256,1024]{2,1,0:T(8,128)(2,1)}, u32[]{:S(2)}) copy-start(bf16[3,256,1024]{2,1,0:T(8,128)(2,1)} %weights.3) | copy-start | bytes 4718596
  43.1 14.4 %copy-start.2 = (bf16[256]{0:T(256)(128)(2,1)S(1)}, bf16[256]{0:T(256)(128)(2,1)}, u32[]{:S(2)}) copy-start(bf16[256]{0:T(256)(128)(2,1)} %param.32) | copy-start | bytes 1540
  43.1 16.0 %copy-start.1 = (bf16[128,256]{1,0:T(8,128)(2,1)S(1)}, bf16[128,256]{1,0:T(8,128)(2,1)}, u32[]{:S(2)}) copy-start(bf16[128,256]{1,0:T(8,128)(2,1)} %param.33) | copy-start | bytes 196612
  43.1 6.2 %collective-permute-start.4 = (bf16[384,256]{1,0:T(8,128)(2,1)S(1)}, bf16[384,256]{1,0:T(8,128)(2,1)S(1)}, u32[]{:S(2)}, u32[]{:S(2)}) collective-permute-start(bf16[384,256]{1,0:T(8,128)(2,1)S(1)} %get-tuple-element.136), channel_id=1, source_target_pairs={{0,16},{4,68},{8,24},{12,76},{16,0},{20,84},{24,8},{28,92},{32,48}... | collective-permute-start | bytes 589832 | tf_op jit(solution)/shard_map/ppermute | solution.py:549
  43.2 6.1 %collective-permute-start.5 = (bf16[384,256]{1,0:T(8,128)(2,1)S(1)}, bf16[384,256]{1,0:T(8,128)(2,1)S(1)}, u32[]{:S(2)}, u32[]{:S(2)}) collective-permute-start(bf16[384,256]{1,0:T(8,128)(2,1)S(1)} %get-tuple-element.135), channel_id=1, source_target_pairs={{0,8},{4,36},{8,16},{12,44},{16,24},{20,52},{24,0},{28,60},{32,40}... | collective-permute-start | bytes 589832 | tf_op jit(solution)/shard_map/ppermute | solution.py:549
  43.3 8.0 %collective-permute-start.6 = (bf16[384,256]{1,0:T(8,128)(2,1)S(1)}, bf16[384,256]{1,0:T(8,128)(2,1)S(1)}, u32[]{:S(2)}, u32[]{:S(2)}) collective-permute-start(bf16[384,256]{1,0:T(8,128)(2,1)S(1)} %get-tuple-element.134), channel_id=1, source_target_pairs={{0,24},{4,100},{8,0},{12,108},{16,8},{20,116},{24,16},{28,124},{32... | collective-permute-start | bytes 589832 | tf_op jit(solution)/shard_map/ppermute | solution.py:549
  51.8 5.7 %collective-permute-start.7 = (bf16[128,256]{1,0:T(8,128)(2,1)S(1)}, bf16[128,256]{1,0:T(8,128)(2,1)S(1)}, u32[]{:S(2)}, u32[]{:S(2)}) collective-permute-start(bf16[128,256]{1,0:T(8,128)(2,1)S(1)} %get-tuple-element.89), channel_id=1, source_target_pairs={{0,2},{1,3},{2,0},{3,1},{4,6},{5,7},{6,4},{7,5},{8,10},{9,11},{10,... | collective-permute-start | bytes 196616 | tf_op jit(solution)/shard_map/ppermute | solution.py:575
  54.8 4.3 %collective-permute-start.8 = (bf16[128,256]{1,0:T(8,128)(2,1)S(1)}, bf16[128,256]{1,0:T(8,128)(2,1)S(1)}, u32[]{:S(2)}, u32[]{:S(2)}) collective-permute-start(bf16[128,256]{1,0:T(8,128)(2,1)S(1)} %get-tuple-element.90), channel_id=1, source_target_pairs={{0,1},{1,2},{2,3},{3,0},{4,5},{5,6},{6,7},{7,4},{8,9},{9,10},{10,1... | collective-permute-start | bytes 196616 | tf_op jit(solution)/shard_map/ppermute | solution.py:575
  55.2 3.9 %collective-permute-start.9 = (bf16[128,256]{1,0:T(8,128)(2,1)S(1)}, bf16[128,256]{1,0:T(8,128)(2,1)S(1)}, u32[]{:S(2)}, u32[]{:S(2)}) collective-permute-start(bf16[128,256]{1,0:T(8,128)(2,1)S(1)} %get-tuple-element.91), channel_id=1, source_target_pairs={{0,3},{1,0},{2,1},{3,2},{4,7},{5,4},{6,5},{7,6},{8,11},{9,8},{10,9... | collective-permute-start | bytes 196616 | tf_op jit(solution)/shard_map/ppermute | solution.py:575
  59.9 4.6 %collective-permute-start.10 = (bf16[128,256]{1,0:T(8,128)(2,1)S(1)}, bf16[128,256]{1,0:T(8,128)(2,1)S(1)}, u32[]{:S(2)}, u32[]{:S(2)}) collective-permute-start(bf16[128,256]{1,0:T(8,128)(2,1)S(1)} %get-tuple-element.102.grad0), channel_id=1, source_target_pairs={{0,2},{1,3},{2,0},{3,1},{4,6},{5,7},{6,4},{7,5},{8,10},{9,11},{10,... | collective-permute-start | bytes 196616 | tf_op jit(solution)/shard_map/ppermute | solution.py:575
  61.6 4.0 %collective-permute-start.11 = (bf16[128,256]{1,0:T(8,128)(2,1)S(1)}, bf16[128,256]{1,0:T(8,128)(2,1)S(1)}, u32[]{:S(2)}, u32[]{:S(2)}) collective-permute-start(bf16[128,256]{1,0:T(8,128)(2,1)S(1)} %get-tuple-element.102.grad0), channel_id=1, source_target_pairs={{0,3},{1,0},{2,1},{3,2},{4,7},{5,4},{6,5},{7,6},{8,11},{9,8},{10,9... | collective-permute-start | bytes 196616 | tf_op jit(solution)/shard_map/ppermute | solution.py:575
  62.7 5.0 %collective-permute-start.12 = (bf16[128,256]{1,0:T(8,128)(2,1)S(1)}, bf16[128,256]{1,0:T(8,128)(2,1)S(1)}, u32[]{:S(2)}, u32[]{:S(2)}) collective-permute-start(bf16[128,256]{1,0:T(8,128)(2,1)S(1)} %get-tuple-element.102.grad0), channel_id=1, source_target_pairs={{0,1},{1,2},{2,3},{3,0},{4,5},{5,6},{6,7},{7,4},{8,9},{9,10},{10,1... | collective-permute-start | bytes 196616 | tf_op jit(solution)/shard_map/ppermute | solution.py:575
  69.6 7.1 %collective-permute-start.20 = (bf16[16,192,128]{2,1,0:T(8,128)(2,1)S(1)}, bf16[16,192,128]{2,1,0:T(8,128)(2,1)S(1)}, u32[]{:S(2)}, u32[]{:S(2)}) collective-permute-start(bf16[16,192,128]{2,1,0:T(8,128)(2,1)S(1)} %get-tuple-element.108), channel_id=1, source_target_pairs={{0,4},{4,0},{8,12},{12,8},{16,20},{20,16},{24,28},{28,24},{32,36},... | collective-permute-start | bytes 2359304 | tf_op jit(solution)/shard_map/ppermute | solution.py:553
  72.9 6.3 %collective-permute-start.13 = (bf16[3,128,256]{2,1,0:T(8,128)(2,1)S(1)}, bf16[3,128,256]{2,1,0:T(8,128)(2,1)S(1)}, u32[]{:S(2)}, u32[]{:S(2)}) collective-permute-start(bf16[3,128,256]{2,1,0:T(8,128)(2,1)S(1)} %form_messages.1.refs_0_), channel_id=1, source_target_pairs={{0,64},{4,20},{8,72},{12,28},{16,80},{20,4},{24,88},{28,12},{32,96... | collective-permute-start | bytes 589832 | tf_op jit(solution)/shard_map/ppermute | solution.py:549
  73.9 7.4 %collective-permute-start.14 = (bf16[3,128,256]{2,1,0:T(8,128)(2,1)S(1)}, bf16[3,128,256]{2,1,0:T(8,128)(2,1)S(1)}, u32[]{:S(2)}, u32[]{:S(2)}) collective-permute-start(bf16[3,128,256]{2,1,0:T(8,128)(2,1)S(1)} %form_messages.1.refs_0_), channel_id=1, source_target_pairs={{0,32},{4,12},{8,40},{12,20},{16,48},{20,28},{24,56},{28,4},{32,64... | collective-permute-start | bytes 589832 | tf_op jit(solution)/shard_map/ppermute | solution.py:549
  75.9 5.5 %collective-permute-start.15 = (bf16[3,128,256]{2,1,0:T(8,128)(2,1)S(1)}, bf16[3,128,256]{2,1,0:T(8,128)(2,1)S(1)}, u32[]{:S(2)}, u32[]{:S(2)}) collective-permute-start(bf16[3,128,256]{2,1,0:T(8,128)(2,1)S(1)} %form_messages.1.refs_0_), channel_id=1, source_target_pairs={{0,96},{4,28},{8,104},{12,4},{16,112},{20,12},{24,120},{28,20},{32... | collective-permute-start | bytes 589832 | tf_op jit(solution)/shard_map/ppermute | solution.py:549
  76.8 12.6 %collective-permute-start.21 = (bf16[4,192,128]{2,1,0:T(8,128)(2,1)S(1)}, bf16[4,192,128]{2,1,0:T(8,128)(2,1)S(1)}, u32[]{:S(2)}, u32[]{:S(2)}) collective-permute-start(bf16[4,192,128]{2,1,0:T(8,128)(2,1)S(1)} %get-tuple-element.140), channel_id=1, source_target_pairs={{0,16},{4,68},{8,24},{12,76},{16,0},{20,84},{24,8},{28,92},{32,48}... | collective-permute-start | bytes 589832 | tf_op jit(solution)/shard_map/ppermute | solution.py:549
  81.4 39.4 %collective-permute-start.16 = (bf16[12,128,256]{2,1,0:T(8,128)(2,1)S(1)}, bf16[12,128,256]{2,1,0:T(8,128)(2,1)S(1)}, u32[]{:S(2)}, u32[]{:S(2)}) collective-permute-start(bf16[12,128,256]{2,1,0:T(8,128)(2,1)S(1)} %join_blocks.1.refs_6_), channel_id=1, source_target_pairs={{0,16},{4,68},{8,24},{12,76},{16,0},{20,84},{24,8},{28,92},{32,48}... | collective-permute-start | bytes 2359304 | tf_op jit(solution)/shard_map/ppermute | solution.py:549
  83.5 37.3 %collective-permute-start.17 = (bf16[12,128,256]{2,1,0:T(8,128)(2,1)S(1)}, bf16[12,128,256]{2,1,0:T(8,128)(2,1)S(1)}, u32[]{:S(2)}, u32[]{:S(2)}) collective-permute-start(bf16[12,128,256]{2,1,0:T(8,128)(2,1)S(1)} %join_blocks.1.refs_6_), channel_id=1, source_target_pairs={{0,8},{4,36},{8,16},{12,44},{16,24},{20,52},{24,0},{28,60},{32,40}... | collective-permute-start | bytes 2359304 | tf_op jit(solution)/shard_map/ppermute | solution.py:549
  84.3 36.5 %collective-permute-start.18 = (bf16[12,128,256]{2,1,0:T(8,128)(2,1)S(1)}, bf16[12,128,256]{2,1,0:T(8,128)(2,1)}, u32[]{:S(2)}, u32[]{:S(2)}) collective-permute-start(bf16[12,128,256]{2,1,0:T(8,128)(2,1)S(1)} %join_blocks.1.refs_6_), channel_id=1, source_target_pairs={{0,24},{4,100},{8,0},{12,108},{16,8},{20,116},{24,16},{28,124},{32... | collective-permute-start | bytes 2359304 | tf_op jit(solution)/shard_map/ppermute | solution.py:549
  84.9 35.9 %collective-permute-start.19 = (bf16[12,128,256]{2,1,0:T(8,128)(2,1)S(1)}, bf16[12,128,256]{2,1,0:T(8,128)(2,1)S(1)}, u32[]{:S(2)}, u32[]{:S(2)}) collective-permute-start(bf16[12,128,256]{2,1,0:T(8,128)(2,1)S(1)} %join_blocks.1.refs_6_), channel_id=1, source_target_pairs={{0,4},{4,0},{8,12},{12,8},{16,20},{20,16},{24,28},{28,24},{32,36},... | collective-permute-start | bytes 2359304 | tf_op jit(solution)/shard_map/ppermute | solution.py:553
  89.4 13.4 %collective-permute-start.22 = (bf16[4,192,128]{2,1,0:T(8,128)(2,1)S(1)}, bf16[4,192,128]{2,1,0:T(8,128)(2,1)S(1)}, u32[]{:S(2)}, u32[]{:S(2)}) collective-permute-start(bf16[4,192,128]{2,1,0:T(8,128)(2,1)S(1)} %get-tuple-element.139), channel_id=1, source_target_pairs={{0,8},{4,36},{8,16},{12,44},{16,24},{20,52},{24,0},{28,60},{32,40}... | collective-permute-start | bytes 589832 | tf_op jit(solution)/shard_map/ppermute | solution.py:549
  102.7 6.0 %collective-permute-start.23 = (bf16[4,192,128]{2,1,0:T(8,128)(2,1)S(1)}, bf16[4,192,128]{2,1,0:T(8,128)(2,1)S(1)}, u32[]{:S(2)}, u32[]{:S(2)}) collective-permute-start(bf16[4,192,128]{2,1,0:T(8,128)(2,1)S(1)} %get-tuple-element.138), channel_id=1, source_target_pairs={{0,24},{4,100},{8,0},{12,108},{16,8},{20,116},{24,16},{28,124},{32... | collective-permute-start | bytes 589832 | tf_op jit(solution)/shard_map/ppermute | solution.py:549
  108.9 4.5 %collective-permute-start.24 = (bf16[192,128]{1,0:T(8,128)(2,1)S(1)}, bf16[192,128]{1,0:T(8,128)(2,1)S(1)}, u32[]{:S(2)}, u32[]{:S(2)}) collective-permute-start(bf16[192,128]{1,0:T(8,128)(2,1)S(1)} %get-tuple-element.143), channel_id=1, source_target_pairs={{0,64},{4,20},{8,72},{12,28},{16,80},{20,4},{24,88},{28,12},{32,96... | collective-permute-start | bytes 147464 | tf_op jit(solution)/shard_map/ppermute | solution.py:549
  113.4 4.2 %collective-permute-start.25 = (bf16[192,128]{1,0:T(8,128)(2,1)S(1)}, bf16[192,128]{1,0:T(8,128)(2,1)S(1)}, u32[]{:S(2)}, u32[]{:S(2)}) collective-permute-start(bf16[192,128]{1,0:T(8,128)(2,1)S(1)} %get-tuple-element.142), channel_id=1, source_target_pairs={{0,32},{4,12},{8,40},{12,20},{16,48},{20,28},{24,56},{28,4},{32,64... | collective-permute-start | bytes 147464 | tf_op jit(solution)/shard_map/ppermute | solution.py:549
  117.6 3.2 %collective-permute-start.26 = (bf16[192,128]{1,0:T(8,128)(2,1)S(1)}, bf16[192,128]{1,0:T(8,128)(2,1)S(1)}, u32[]{:S(2)}, u32[]{:S(2)}) collective-permute-start(bf16[192,128]{1,0:T(8,128)(2,1)S(1)} %get-tuple-element.141), channel_id=1, source_target_pairs={{0,96},{4,28},{8,104},{12,4},{16,112},{20,12},{24,120},{28,20},{32... | collective-permute-start | bytes 147464 | tf_op jit(solution)/shard_map/ppermute | solution.py:549
  120.8 12.3 %collective-permute-start.27 = (bf16[12,128,256]{2,1,0:T(8,128)(2,1)S(1)}, bf16[12,128,256]{2,1,0:T(8,128)(2,1)}, u32[]{:S(2)}, u32[]{:S(2)}) collective-permute-start(bf16[12,128,256]{2,1,0:T(8,128)(2,1)S(1)} %collective-permute-done.16.refs_7_), channel_id=1, source_target_pairs={{0,4},{4,0},{8,12},{12,8},{16,20},{20,16},{24,28},{28,24},{32,36},... | collective-permute-start | bytes 2359304 | tf_op jit(solution)/shard_map/ppermute | solution.py:553
  131.0 3.2 %collective-permute-start.28 = (bf16[12,128,256]{2,1,0:T(8,128)(2,1)S(1)}, bf16[12,128,256]{2,1,0:T(8,128)(2,1)}, u32[]{:S(2)}, u32[]{:S(2)}) collective-permute-start(bf16[12,128,256]{2,1,0:T(8,128)(2,1)S(1)} %collective-permute-done.17.refs_8_), channel_id=1, source_target_pairs={{0,4},{4,0},{8,12},{12,8},{16,20},{20,16},{24,28},{28,24},{32,36},... | collective-permute-start | bytes 2359304 | tf_op jit(solution)/shard_map/ppermute | solution.py:553
  131.1 4.2 %collective-permute-start.29 = (bf16[12,128,256]{2,1,0:T(8,128)(2,1)}, bf16[12,128,256]{2,1,0:T(8,128)(2,1)}, u32[]{:S(2)}, u32[]{:S(2)}) collective-permute-start(bf16[12,128,256]{2,1,0:T(8,128)(2,1)} %collective-permute-done.18.refs_9_), channel_id=1, source_target_pairs={{0,4},{4,0},{8,12},{12,8},{16,20},{20,16},{24,28},{28,24},{32,36},... | collective-permute-start | bytes 2359304 | tf_op jit(solution)/shard_map/ppermute | solution.py:553

commit v4 on v3

--- a/solution.py
+++ b/solution.py
@@ -16,7 +16,7 @@
 F32 = jnp.float32
 MIB = 1024 * 1024
 GATHER_LIMIT = 36 * MIB
-SPREAD_LIMIT = 28 * MIB
+SPREAD_LIMIT = 20 * MIB
 barrier = lax.optimization_barrier
 
 
@@ -234,12 +234,15 @@
     return keep, send
 
 
+EARLY = 20
+
+
 def plan_kernel(
     owner_map,
     targets0, targets1, targets2, sources0, sources1, sources2, counts0, counts1, counts2,
-    pair_a, pair_b, pair_spot, amount,
+    pair_a, pair_b, pair_spot, amounts,
     table, pending,
-    *, blank,
+    *, room, blank,
 ):
     targets, sources = (targets0, targets1, targets2), (sources0, sources1, sources2)
     counts = (counts0, counts1, counts2)
@@ -248,90 +251,81 @@
 
     def fill(slot, carry):
         first, second, away = place_of(slot, mine)
-        table[owner_map[slot]] = (away * 16 + second * SIDE + first) * 3
+        place = away * 16 + second * SIDE + first
+        late = jnp.where(place >= EARLY, 1, 0)
+        table[owner_map[slot]] = (place - late * EARLY) * 3 + late * 128
+        pending[slot] = -1
         return carry
 
     lax.fori_loop(0, 32, fill, 0)
-    for spot in range(17):
-        pending[spot] = -1
-
-    def put(found, a, b, spot, yes):
-        pair_a[found] = a
-        pair_b[found] = b
-        pair_spot[found] = spot
-        return found + jnp.where(yes, 1, 0)
-
-    found = jnp.int32(0)
+    pending[32] = -1
+
+    def put(found, late, a, b, spot, yes):
+        at = jnp.where(late == 1, room + found[1], found[0])
+        pair_a[at] = a
+        pair_b[at] = b
+        pair_spot[at] = spot
+        return found[0] + yes * (1 - late), found[1] + yes * late
+
+    found = (jnp.int32(0), jnp.int32(0))
     for number in range(3):
         def match(group, found, number=number):
             for lane in range(GROUP):
                 j = group * GROUP + lane
                 live = j < counts[number][0]
-                code = begins[number] * GROUP + j + (table[targets[number][j]] + number) * 1024
-                spot = jnp.where(live, sources[number][j], 16)
+                place = table[targets[number][j]]
+                late = place >> 7
+                source = sources[number][j]
+                code = begins[number] * GROUP + j + ((place & 127) + number) * 1024
+                spot = jnp.where(live, late * 16 + source, 32)
                 waiting = pending[spot]
                 hit = live & (waiting >= 0)
-                found = put(found, waiting, code, spot, hit)
+                found = put(found, late, waiting, code, source, jnp.where(hit, 1, 0))
                 pending[spot] = jnp.where(hit, -1, code)
             return found
 
         found = lax.fori_loop(0, (counts[number][0] + GROUP - 1) // GROUP, match, found)
-    for spot in range(16):
-        found = put(found, pending[spot], blank, spot, pending[spot] >= 0)
-    for lane in range(PAIRS):
-        put(found + lane, blank, blank, 16, False)
-    amount[0] = found
+
+    def flush(spot, found):
+        waiting = pending[spot]
+        yes = jnp.where(waiting >= 0, 1, 0)
+        return put(found, spot >> 4, waiting, blank, spot & 15, yes)
+
+    found = lax.fori_loop(0, 32, flush, found)
+    for late in range(2):
+        for lane in range(PAIRS):
+            pair_a[late * room + found[late] + lane] = blank
+            pair_b[late * room + found[late] + lane] = blank
+            pair_spot[late * room + found[late] + lane] = 16
+        amounts[late] = found[late]
+
+
+def pair_room(slots):
+    return slots // 2 + 32 + PAIRS
 
 
 def plan_spread(owner_map, relations):
     slots = sum(relation[0].shape[0] for relation in relations)
-    pairs = jax.ShapeDtypeStruct((slots // 2 + 16 + 2 * PAIRS,), jnp.int32)
+    room = pair_room(slots)
+    pairs = jax.ShapeDtypeStruct((2 * room,), jnp.int32)
     return pl.pallas_call(
-        functools.partial(plan_kernel, blank=slots),
-        out_shape=(pairs, pairs, pairs, jax.ShapeDtypeStruct((1,), jnp.int32)),
+        functools.partial(plan_kernel, room=room, blank=slots),
+        out_shape=(pairs, pairs, pairs, jax.ShapeDtypeStruct((2,), jnp.int32)),
         in_specs=[spec(SMEM)] * 10,
         out_specs=tuple([spec(SMEM)] * 4),
-        scratch_shapes=[pltpu.SMEM((32,), jnp.int32), pltpu.SMEM((17,), jnp.int32)],
+        scratch_shapes=[pltpu.SMEM((32,), jnp.int32), pltpu.SMEM((33,), jnp.int32)],
         compiler_params=pltpu.CompilerParams(vmem_limit_bytes=MIB),
         cost_estimate=pl.CostEstimate(flops=10**9, bytes_accessed=10**6, transcendentals=0),
         name="plan_spread",
     )(*flat_args(owner_map, relations))
 
 
-PLACES = (0, 8, 12, 4, 16, 24, 28, 20)
-FAR = (3, 5, 6, 7)
-
-
-def spread_kernel(pair_a, pair_b, pair_spot, amount, *refs):
-    counts, tiles, pieces, refs = refs[:3], refs[3:6], refs[6:14], refs[14:]
-    out, buffer, messages, total, tile_sems, piece_sems = refs
-    copies = [
-        pltpu.make_async_copy(
-            pieces[number], messages.at[pl.ds(PLACES[number] * 3, 12)], piece_sems.at[sem]
-        )
-        for sem, number in enumerate(FAR)
-    ]
-    for copy in copies:
-        copy.start()
-    begins = start_tiles(tiles, counts, buffer, tile_sems)
-
-    def place(block, carry):
-        for number, (piece, at) in enumerate(zip(pieces, PLACES)):
-            if number not in FAR:
-                messages[at * 3 + block] = piece[block]
-        return carry
-
-    lax.fori_loop(0, 12, place, 0)
-    blank = buffer.shape[0] - 1
-    buffer[blank] = jnp.zeros((TILE, TILE), BF16)
-    clear(total, 16)
-    for copy in copies:
-        copy.wait()
+def spread_list(plan, offset, amount, messages, buffer, total, ready):
+    pair_a, pair_b, pair_spot = plan
 
     def add_group(group, waited):
-        at = group * PAIRS
-        needed = jnp.minimum(((pair_b[at + PAIRS - 1] & 1023) >> 4) + 1, begins[3])
-        waited = wait_tiles(tiles[0], buffer, tile_sems, waited, needed)
+        at = offset + group * PAIRS
+        waited = ready(waited, pair_b[at + PAIRS - 1] & 1023)
         products = []
         for lane in range(PAIRS):
             marks = (pair_a[at + lane], pair_b[at + lane])
@@ -346,44 +340,138 @@
             total[pair_spot[at + lane]] += products[lane]
         return waited
 
-    waited = lax.fori_loop(0, (amount[0] + PAIRS - 1) // PAIRS, add_group, jnp.int32(0))
-    wait_tiles(tiles[0], buffer, tile_sems, waited, begins[3])
+    return lax.fori_loop(0, (amount + PAIRS - 1) // PAIRS, add_group, jnp.int32(0))
+
+
+def start_pieces(pieces, places, messages, sems):
+    copies = [
+        pltpu.make_async_copy(piece, messages.at[pl.ds(at * 3, 12)], sems.at[number])
+        for number, (piece, at) in enumerate(zip(pieces, places))
+    ]
+    for copy in copies:
+        copy.start()
+    return copies
+
+
+def spread_early_kernel(
+    pair_a, pair_b, pair_spot, amounts, counts0, counts1, counts2, tiles0, tiles1, tiles2,
+    own0, own2, own3, own1, sib0,
+    out, buffer, messages, total, tile_sems, piece_sems,
+):
+    tiles = (tiles0, tiles1, tiles2)
+    copies = start_pieces((own1,), (4,), messages, piece_sems)
+    begins = start_tiles(tiles, (counts0, counts1, counts2), buffer, tile_sems)
+
+    def place(block, carry):
+        for piece, at in ((own0, 0), (own2, 8), (own3, 12), (sib0, 16)):
+            messages[at * 3 + block] = piece[block]
+        return carry
+
+    lax.fori_loop(0, 12, place, 0)
+    buffer[buffer.shape[0] - 1] = jnp.zeros((TILE, TILE), BF16)
+    clear(total, 16)
+    for copy in copies:
+        copy.wait()
+
+    def ready(waited, last):
+        needed = jnp.minimum((last >> 4) + 1, begins[3])
+        return wait_tiles(tiles0, buffer, tile_sems, waited, needed)
+
+    waited = spread_list(
+        (pair_a, pair_b, pair_spot), 0, amounts[0], messages, buffer, total, ready
+    )
+    wait_tiles(tiles0, buffer, tile_sems, waited, begins[3])
 
     def emit(block, carry):
-        out[block] = total[block].astype(out.dtype)
+        out[block] = total[block]
         return carry
 
     lax.fori_loop(0, 16, emit, 0)
 
 
-def spread_sums(plan, relations, pieces):
+def spread_late_kernel(
+    pair_a, pair_b, pair_spot, amounts, buffer, before, sib2, sib3, sib1,
+    out, messages, total, piece_sems,
+):
+    copies = start_pieces((sib2, sib3, sib1), (4, 8, 0), messages, piece_sems)
+
+    def take(block, carry):
+        total[block] = before[block]
+        return carry
+
+    lax.fori_loop(0, 16, take, 0)
+    for copy in copies:
+        copy.wait()
+    spread_list(
+        (pair_a, pair_b, pair_spot),
+        pair_a.shape[0] // 2,
+        amounts[1],
+        messages,
+        buffer,
+        total,
+        lambda waited, last: waited,
+    )
+
+    def emit(block, carry):
+        out[block] = total[block].astype(BF16)
+        return carry
+
+    lax.fori_loop(0, 16, emit, 0)
+
+
+def spread_early(plan, relations, pieces):
     width = pieces[0].shape[-1]
     slots = sum(relation[0].shape[0] for relation in relations)
+    whole, own2, own3, own1, beside = pieces
     return pl.pallas_call(
-        spread_kernel,
-        out_shape=jax.ShapeDtypeStruct((16, TILE, width), BF16),
+        spread_early_kernel,
+        out_shape=(
+            jax.ShapeDtypeStruct((16, TILE, width), F32),
+            jax.ShapeDtypeStruct((slots + 1, TILE, TILE), BF16),
+        ),
         in_specs=[spec(SMEM)] * 7
         + [spec(ANY)] * 3
-        + [spec(ANY if number in FAR else VMEM) for number in range(8)],
-        out_specs=spec(VMEM),
+        + [spec(VMEM)] * 3
+        + [spec(ANY), spec(VMEM)],
+        out_specs=(spec(VMEM), spec(VMEM)),
         scratch_shapes=[
-            pltpu.VMEM((slots + 1, TILE, TILE), BF16),
-            pltpu.VMEM((96, TILE, width), BF16),
+            pltpu.VMEM((3 * EARLY, TILE, width), BF16),
             pltpu.VMEM((17, TILE, width), F32),
             pltpu.SemaphoreType.DMA((slots // GROUP,)),
-            pltpu.SemaphoreType.DMA((len(FAR),)),
+            pltpu.SemaphoreType.DMA((1,)),
         ],
         compiler_params=pltpu.CompilerParams(vmem_limit_bytes=SPREAD_LIMIT),
         cost_estimate=pl.CostEstimate(
-            flops=3 * 10**9, bytes_accessed=18 * 10**6, transcendentals=0
+            flops=2 * 10**9, bytes_accessed=14 * 10**6, transcendentals=0
         ),
-        name="spread_sums",
+        name="spread_early",
     )(
         *plan,
         *[relation[3] for relation in relations],
         *tile_args(relations),
-        *[in_hbm(piece) if number in FAR else piece for number, piece in enumerate(pieces)],
-    )
+        whole, own2, own3, in_hbm(own1), beside,
+    )
+
+
+def spread_late(plan, early, pieces):
+    before, buffer = early
+    width = pieces[0].shape[-1]
+    return pl.pallas_call(
+        spread_late_kernel,
+        out_shape=jax.ShapeDtypeStruct((16, TILE, width), BF16),
+        in_specs=[spec(SMEM)] * 4 + [spec(VMEM)] * 2 + [spec(ANY)] * 3,
+        out_specs=spec(VMEM),
+        scratch_shapes=[
+            pltpu.VMEM((3 * (32 - EARLY), TILE, width), BF16),
+            pltpu.VMEM((17, TILE, width), F32),
+            pltpu.SemaphoreType.DMA((3,)),
+        ],
+        compiler_params=pltpu.CompilerParams(vmem_limit_bytes=SPREAD_LIMIT),
+        cost_estimate=pl.CostEstimate(
+            flops=10**9, bytes_accessed=4 * 10**6, transcendentals=0
+        ),
+        name="spread_late",
+    )(*plan, buffer, before, *[in_hbm(piece) for piece in pieces])
 
 
 def columns_at(step, width):
@@ -640,7 +728,8 @@
     *spread_out, beside, l0, w0, w1, w2 = barrier((*spread_out, beside, line[0], *weight_parts))
     weight_parts = (w0, w1, w2)
     siblings = [swap(piece) for piece in spread_out]
-    grad_source = spread_sums(plan, relations, [whole, *spread_out, beside, *siblings])
+    early = spread_early(plan, relations, [whole, *spread_out, beside])
+    grad_source = spread_late(plan, early, siblings)
     weight_sum = l0.astype(F32)
     for part in weight_parts:
         weight_sum = weight_sum + part.astype(F32)

time: 146 us -> 145 us (level)
  waiting for transfers between devices: 59.6 us -> 55.3 us
  Pallas kernels: 33.3 us -> 36.4 us
    pallas_call x2 -> x3, Pallas kernels: 14.7 us -> 17.8 us  [the longest x1 6.68 us: spread_early(): pl.pallas_call(spread_early_kernel, out_shape=(jax.ShapeDtypeStruct((16,...]
    ppermute x6, waiting for transfers between devices: 2.97 us -> 0.02 us  [swap(): return lax.ppermute(value, 'src', [(s, s ^ 1) for s in range(32)])]
  transfers between devices with their start and end apart: 30 -> 30, of which waited for: 19 -> 16; matrix products, arithmetic and copies ran while one was open for 1% -> 1% of each run, Pallas kernels for 8% -> 13%
where the time goes in v4:
time: 145 us
  waiting for transfers between devices  55.3 us (38%)
  starting transfers between devices  46.8 us (32%)
  Pallas kernels  36.4 us (25%)
  between operations  2.95 us (2%)
  other arithmetic  2.49 us (2%)
    ppermute x18, waiting for transfers between devices, shift(): return lax.ppermute(value, 'src', shift_pairs(step, second))  49.2 us
    ppermute x18, starting transfers between devices, shift(): return lax.ppermute(value, 'src', shift_pairs(step, second))  19.1 us
    ppermute x6, starting transfers between devices, swap(): return lax.ppermute(value, 'src', [(s, s ^ 1) for s in range(32)])  18.6 us
    pallas_call x1, Pallas kernels, gather_sums(): pl.pallas_call(gather_send_kernel, out_shape=(blocks, jax.ShapeDtypeStruc...  9.24 us
    ppermute x6, starting transfers between devices, turn(): lax.ppermute(value, 'tgt', [(t, (t + step) % SIDE) for t in range(SIDE)])  9.06 us
    pallas_call x1, Pallas kernels, gather_sums(): pl.pallas_call(gather_keep_kernel, out_shape=blocks, in_specs=[spec(SMEM)...  7.02 us
    pallas_call x1, Pallas kernels, spread_early(): pl.pallas_call(spread_early_kernel, out_shape=(jax.ShapeDtypeStruct((16,...  6.68 us
    ppermute x6, waiting for transfers between devices, turn(): lax.ppermute(value, 'tgt', [(t, (t + step) % SIDE) for t in range(SIDE)])  6.09 us
  transfers between devices with their start and end apart: 30, of which 16 were waited for; matrix products, arithmetic and copies ran while one was open for 1% of the time, Pallas kernels for 13%

profile of v4, /device:TPU:7, one launch (start us, length us, event | category | flops | bytes accessed | tf_op | source)
XLA Modules:
  0.0 144.8 jit_solution(1811563020665957251)
XLA Ops:
  2.6 9.2 %gather_send.1 = (bf16[16,384,256]{2,1,0:T(8,128)(2,1)S(1)}, s32[352]{0:T(512)S(1)}, s32[1]{0:T(128)}, bf16[336,128,128]{2,1,0:T(8,128)(2,1)S(1)}, bf16[16,128,256]{2,1,0:T(8,128)(2,1)S(1)}) custom-call(s32[32]{0:T(128)} %owner_map.2, s32[192]{0:T(256)} %targets0.3, s32[96]{0:T(128)} %targets1.3, s32[48]{0:T(128)} %targets2.3, s32[192]{0:T(256)} %sources0.3, ...), custom_call_target="tpu_custom_call" | custom-call | flops 2000000000 | bytes 12000000 | tf_op jit(solution)/shard_map/gather_send/pallas_call | solution.py:204
  11.9 7.0 %gather_keep.1 = bf16[16,384,256]{2,1,0:T(8,128)(2,1)S(1)} custom-call(s32[352]{0:T(512)S(1)} %get-tuple-element.67.codes, s32[1]{0:T(128)} %get-tuple-element.68.amount, bf16[336,128,128]{2,1,0:T(8,128)(2,1)S(1)} %get-tuple-element.69.buffer, bf16[16,128,256]{2,1,0:T(8,128)(2,1)S(1)} %get-tuple-element.70.held), custom_call_target="tpu_custom_call" | custom-call | flops 2000000000 | bytes 12000000 | tf_op jit(solution)/shard_map/gather_keep/pallas_call | solution.py:225
  19.0 1.0 add_convert_fusion
  20.0 1.3 collective-permute-start.1
  21.3 3.6 %collective-permute-start.2 = (bf16[4,384,256]{2,1,0:T(8,128)(2,1)S(1)}, bf16[4,384,256]{2,1,0:T(8,128)(2,1)S(1)}, u32[]{:S(2)}, u32[]{:S(2)}) collective-permute-start(bf16[4,384,256]{2,1,0:T(8,128)(2,1)S(1)} %get-tuple-element.79), channel_id=1, source_target_pairs={{0,32},{4,12},{8,40},{12,20},{16,48},{20,28},{24,56},{28,4},{32,64... | collective-permute-start | bytes 2359304 | tf_op jit(solution)/shard_map/ppermute | solution.py:637
  24.8 5.6 %plan_spread.1 = (s32[432]{0:T(512)S(1)}, s32[432]{0:T(512)S(1)}, s32[432]{0:T(512)S(1)}, s32[2]{0:T(128)S(1)}) custom-call(s32[32]{0:T(128)} %owner_map.2, s32[192]{0:T(256)} %targets0.3, s32[96]{0:T(128)} %targets1.3, s32[48]{0:T(128)} %targets2.3, s32[192]{0:T(256)} %sources0.3, s32[96]{0:T(128)} %sources1.3, s32[48]{0:T(128)} %sources2.3, ...), custom_call_target="tpu_custom_call" | custom-call | flops 1000000000 | bytes 1000000 | tf_op jit(solution)/shard_map/plan_spread/pallas_call | solution.py:311
  30.4 2.1 %collective-permute-done.1 = bf16[4,384,256]{2,1,0:T(8,128)(2,1)S(1)} collective-permute-done((bf16[4,384,256]{2,1,0:T(8,128)(2,1)S(1)}, bf16[4,384,256]{2,1,0:T(8,128)(2,1)S(1)}, u32[]{:S(2)}, u32[]{:S(2)}) %collective-permute-start.1) | collective-permute-done | bytes 786464 | tf_op jit(solution)/shard_map/ppermute | solution.py:637
  32.5 8.3 %collective-permute-done.2 = bf16[4,384,256]{2,1,0:T(8,128)(2,1)S(1)} collective-permute-done((bf16[4,384,256]{2,1,0:T(8,128)(2,1)S(1)}, bf16[4,384,256]{2,1,0:T(8,128)(2,1)S(1)}, u32[]{:S(2)}, u32[]{:S(2)}) %collective-permute-start.2) | collective-permute-done | bytes 786464 | tf_op jit(solution)/shard_map/ppermute | solution.py:637
  40.8 1.9 %collective-permute-done.3 = bf16[4,384,256]{2,1,0:T(8,128)(2,1)S(1)} collective-permute-done((bf16[4,384,256]{2,1,0:T(8,128)(2,1)S(1)}, bf16[4,384,256]{2,1,0:T(8,128)(2,1)S(1)}, u32[]{:S(2)}, u32[]{:S(2)}) %collective-permute-start.3) | collective-permute-done | bytes 786464 | tf_op jit(solution)/shard_map/ppermute | solution.py:637
  43.3 1.5 %collective-permute-start.6 = (bf16[384,256]{1,0:T(8,128)(2,1)S(1)}, bf16[384,256]{1,0:T(8,128)(2,1)S(1)}, u32[]{:S(2)}, u32[]{:S(2)}) collective-permute-start(bf16[384,256]{1,0:T(8,128)(2,1)S(1)} %get-tuple-element.138), channel_id=1, source_target_pairs={{0,24},{4,100},{8,0},{12,108},{16,8},{20,116},{24,16},{28,124},{32... | collective-permute-start | bytes 589832 | tf_op jit(solution)/shard_map/ppermute | solution.py:637
  44.8 4.6 %collective-permute-done.4.part1 = bf16[384,256]{1,0:T(8,128)(2,1)S(1)} collective-permute-done((bf16[384,256]{1,0:T(8,128)(2,1)S(1)}, bf16[384,256]{1,0:T(8,128)(2,1)S(1)}, u32[]{:S(2)}, u32[]{:S(2)}) %collective-permute-start.4) | collective-permute-done | bytes 196640 | tf_op jit(solution)/shard_map/ppermute | solution.py:637
  49.4 2.0 %collective-permute-done.6.part3 = bf16[384,256]{1,0:T(8,128)(2,1)S(1)} collective-permute-done((bf16[384,256]{1,0:T(8,128)(2,1)S(1)}, bf16[384,256]{1,0:T(8,128)(2,1)S(1)}, u32[]{:S(2)}, u32[]{:S(2)}) %collective-permute-start.6) | collective-permute-done | bytes 196640 | tf_op jit(solution)/shard_map/ppermute | solution.py:637
  51.4 0.4 hidden_terms.1
  51.8 3.0 %collective-permute-start.7 = (bf16[128,256]{1,0:T(8,128)(2,1)S(1)}, bf16[128,256]{1,0:T(8,128)(2,1)S(1)}, u32[]{:S(2)}, u32[]{:S(2)}) collective-permute-start(bf16[128,256]{1,0:T(8,128)(2,1)S(1)} %get-tuple-element.91), channel_id=1, source_target_pairs={{0,2},{1,3},{2,0},{3,1},{4,6},{5,7},{6,4},{7,5},{8,10},{9,11},{10,... | collective-permute-start | bytes 196616 | tf_op jit(solution)/shard_map/ppermute | solution.py:663
  55.2 2.3 %collective-permute-start.9 = (bf16[128,256]{1,0:T(8,128)(2,1)S(1)}, bf16[128,256]{1,0:T(8,128)(2,1)S(1)}, u32[]{:S(2)}, u32[]{:S(2)}) collective-permute-start(bf16[128,256]{1,0:T(8,128)(2,1)S(1)} %get-tuple-element.93), channel_id=1, source_target_pairs={{0,3},{1,0},{2,1},{3,2},{4,7},{5,4},{6,5},{7,6},{8,11},{9,8},{10,9... | collective-permute-start | bytes 196616 | tf_op jit(solution)/shard_map/ppermute | solution.py:663
  57.5 1.6 %collective-permute-done.8 = bf16[128,256]{1,0:T(8,128)(2,1)S(1)} collective-permute-done((bf16[128,256]{1,0:T(8,128)(2,1)S(1)}, bf16[128,256]{1,0:T(8,128)(2,1)S(1)}, u32[]{:S(2)}, u32[]{:S(2)}) %collective-permute-start.8) | collective-permute-done | bytes 65568 | tf_op jit(solution)/shard_map/ppermute | solution.py:663
  59.1 0.8 fusion.6
  59.9 1.7 %collective-permute-start.10 = (bf16[128,256]{1,0:T(8,128)(2,1)S(1)}, bf16[128,256]{1,0:T(8,128)(2,1)S(1)}, u32[]{:S(2)}, u32[]{:S(2)}) collective-permute-start(bf16[128,256]{1,0:T(8,128)(2,1)S(1)} %get-tuple-element.104.grad0), channel_id=1, source_target_pairs={{0,2},{1,3},{2,0},{3,1},{4,6},{5,7},{6,4},{7,5},{8,10},{9,11},{10,... | collective-permute-start | bytes 196616 | tf_op jit(solution)/shard_map/ppermute | solution.py:663
  61.6 1.1 collective-permute-start.11
  62.7 0.6 collective-permute-start.12
  63.3 1.2 collective-permute-done.10.grad2
  64.5 1.1 collective-permute-done.11.grad1
  65.6 2.1 %collective-permute-done.12.grad3 = bf16[128,256]{1,0:T(8,128)(2,1)S(1)} collective-permute-done((bf16[128,256]{1,0:T(8,128)(2,1)S(1)}, bf16[128,256]{1,0:T(8,128)(2,1)S(1)}, u32[]{:S(2)}, u32[]{:S(2)}) %collective-permute-start.12) | collective-permute-done | bytes 65568 | tf_op jit(solution)/shard_map/ppermute | solution.py:663
  67.7 0.7 form_messages.1.refs_0_
  68.4 1.1 weight_terms.1
  69.6 3.4 %collective-permute-start.20 = (bf16[16,192,128]{2,1,0:T(8,128)(2,1)S(1)}, bf16[16,192,128]{2,1,0:T(8,128)(2,1)S(1)}, u32[]{:S(2)}, u32[]{:S(2)}) collective-permute-start(bf16[16,192,128]{2,1,0:T(8,128)(2,1)S(1)} %get-tuple-element.110), channel_id=1, source_target_pairs={{0,4},{4,0},{8,12},{12,8},{16,20},{20,16},{24,28},{28,24},{32,36},... | collective-permute-start | bytes 2359304 | tf_op jit(solution)/shard_map/ppermute | solution.py:641
  72.9 1.0 collective-permute-start.13
  73.9 1.9 %collective-permute-start.14 = (bf16[3,128,256]{2,1,0:T(8,128)(2,1)S(1)}, bf16[3,128,256]{2,1,0:T(8,128)(2,1)S(1)}, u32[]{:S(2)}, u32[]{:S(2)}) collective-permute-start(bf16[3,128,256]{2,1,0:T(8,128)(2,1)S(1)} %form_messages.1.refs_0_), channel_id=1, source_target_pairs={{0,32},{4,12},{8,40},{12,20},{16,48},{20,28},{24,56},{28,4},{32,64... | collective-permute-start | bytes 589832 | tf_op jit(solution)/shard_map/ppermute | solution.py:637
  75.9 0.7 collective-permute-start.15
  76.8 1.3 collective-permute-start.21
  78.1 1.2 collective-permute-done.13.refs_2_
  79.2 2.1 %collective-permute-done.14.refs_3_ = bf16[3,128,256]{2,1,0:T(8,128)(2,1)S(1)} collective-permute-done((bf16[3,128,256]{2,1,0:T(8,128)(2,1)S(1)}, bf16[3,128,256]{2,1,0:T(8,128)(2,1)S(1)}, u32[]{:S(2)}, u32[]{:S(2)}) %collective-permute-start.14) | collective-permute-done | bytes 196640 | tf_op jit(solution)/shard_map/ppermute | solution.py:637
  81.4 2.1 %collective-permute-start.16 = (bf16[12,128,256]{2,1,0:T(8,128)(2,1)S(1)}, bf16[12,128,256]{2,1,0:T(8,128)(2,1)S(1)}, u32[]{:S(2)}, u32[]{:S(2)}) collective-permute-start(bf16[12,128,256]{2,1,0:T(8,128)(2,1)S(1)} %join_blocks.1.own0), channel_id=1, source_target_pairs={{0,16},{4,68},{8,24},{12,76},{16,0},{20,84},{24,8},{28,92},{32,48}... | collective-permute-start | bytes 2359304 | tf_op jit(solution)/shard_map/ppermute | solution.py:637
  83.5 0.9 collective-permute-start.17
  84.3 0.6 collective-permute-start.18
  84.9 4.4 %collective-permute-start.19 = (bf16[12,128,256]{2,1,0:T(8,128)(2,1)S(1)}, bf16[12,128,256]{2,1,0:T(8,128)(2,1)S(1)}, u32[]{:S(2)}, u32[]{:S(2)}) collective-permute-start(bf16[12,128,256]{2,1,0:T(8,128)(2,1)S(1)} %join_blocks.1.own0), channel_id=1, source_target_pairs={{0,4},{4,0},{8,12},{12,8},{16,20},{20,16},{24,28},{28,24},{32,36},... | collective-permute-start | bytes 2359304 | tf_op jit(solution)/shard_map/ppermute | solution.py:641
  89.4 13.4 %collective-permute-done.22 = bf16[4,192,128]{2,1,0:T(8,128)(2,1)S(1)} collective-permute-done((bf16[4,192,128]{2,1,0:T(8,128)(2,1)S(1)}, bf16[4,192,128]{2,1,0:T(8,128)(2,1)S(1)}, u32[]{:S(2)}, u32[]{:S(2)}) %collective-permute-start.22) | collective-permute-done | bytes 196640 | tf_op jit(solution)/shard_map/ppermute | solution.py:637
  102.7 1.7 %collective-permute-start.23 = (bf16[4,192,128]{2,1,0:T(8,128)(2,1)S(1)}, bf16[4,192,128]{2,1,0:T(8,128)(2,1)S(1)}, u32[]{:S(2)}, u32[]{:S(2)}) collective-permute-start(bf16[4,192,128]{2,1,0:T(8,128)(2,1)S(1)} %get-tuple-element.142), channel_id=1, source_target_pairs={{0,24},{4,100},{8,0},{12,108},{16,8},{20,116},{24,16},{28,124},{32... | collective-permute-start | bytes 589832 | tf_op jit(solution)/shard_map/ppermute | solution.py:637
  104.5 4.2 %collective-permute-done.23 = bf16[4,192,128]{2,1,0:T(8,128)(2,1)S(1)} collective-permute-done((bf16[4,192,128]{2,1,0:T(8,128)(2,1)S(1)}, bf16[4,192,128]{2,1,0:T(8,128)(2,1)S(1)}, u32[]{:S(2)}, u32[]{:S(2)}) %collective-permute-start.23) | collective-permute-done | bytes 196640 | tf_op jit(solution)/shard_map/ppermute | solution.py:637
  108.9 0.8 collective-permute-start.24
  109.7 3.7 %collective-permute-done.24 = bf16[192,128]{1,0:T(8,128)(2,1)S(1)} collective-permute-done((bf16[192,128]{1,0:T(8,128)(2,1)S(1)}, bf16[192,128]{1,0:T(8,128)(2,1)S(1)}, u32[]{:S(2)}, u32[]{:S(2)}) %collective-permute-start.24) | collective-permute-done | bytes 49184 | tf_op jit(solution)/shard_map/ppermute | solution.py:637
  113.6 3.9 %collective-permute-done.25 = bf16[192,128]{1,0:T(8,128)(2,1)S(1)} collective-permute-done((bf16[192,128]{1,0:T(8,128)(2,1)S(1)}, bf16[192,128]{1,0:T(8,128)(2,1)S(1)}, u32[]{:S(2)}, u32[]{:S(2)}) %collective-permute-start.25) | collective-permute-done | bytes 49184 | tf_op jit(solution)/shard_map/ppermute | solution.py:637
  117.6 1.4 collective-permute-start.26
  119.0 1.8 %collective-permute-done.26 = bf16[192,128]{1,0:T(8,128)(2,1)S(1)} collective-permute-done((bf16[192,128]{1,0:T(8,128)(2,1)S(1)}, bf16[192,128]{1,0:T(8,128)(2,1)S(1)}, u32[]{:S(2)}, u32[]{:S(2)}) %collective-permute-start.26) | collective-permute-done | bytes 49184 | tf_op jit(solution)/shard_map/ppermute | solution.py:637
  120.8 10.2 %collective-permute-start.27 = (bf16[12,128,256]{2,1,0:T(8,128)(2,1)S(1)}, bf16[12,128,256]{2,1,0:T(8,128)(2,1)}, u32[]{:S(2)}, u32[]{:S(2)}) collective-permute-start(bf16[12,128,256]{2,1,0:T(8,128)(2,1)S(1)} %collective-permute-done.16.own2), channel_id=1, source_target_pairs={{0,4},{4,0},{8,12},{12,8},{16,20},{20,16},{24,28},{28,24},{32,36},... | collective-permute-start | bytes 2359304 | tf_op jit(solution)/shard_map/ppermute | solution.py:641
  131.7 0.7 copy.21
  132.4 6.7 %spread_early.1 = (f32[16,128,256]{2,1,0:T(8,128)S(1)}, bf16[337,128,128]{2,1,0:T(8,128)(2,1)S(1)}) custom-call(s32[432]{0:T(512)S(1)} %get-tuple-element.121.pair_a, s32[432]{0:T(512)S(1)} %get-tuple-element.122.pair_b, s32[432]{0:T(512)S(1)} %get-tuple-element.123.pair_spot, s32[2]{0:T(128)S(1)} %get-tuple-element.124.amounts, s32[1]{0:T(128)S(6)} %copy.24.counts0, ...), custom_call_target="tpu_custom_call" | custom-call | flops 2000000000 | bytes 14000000 | tf_op jit(solution)/shard_map/spread_early/pallas_call | solution.py:426
  139.1 5.6 %spread_late.1 = bf16[16,128,256]{2,1,0:T(8,128)(2,1)} custom-call(s32[432]{0:T(512)S(1)} %get-tuple-element.121.pair_a, s32[432]{0:T(512)S(1)} %get-tuple-element.122.pair_b, s32[432]{0:T(512)S(1)} %get-tuple-element.123.pair_spot, s32[2]{0:T(128)S(1)} %get-tuple-element.124.amounts, bf16[337,128,128]{2,1,0:T(8,128)(2,1)S(1)} %get-tuple-element.129.buffer, ...), custom_call_target="tpu_custom_call" | custom-call | flops 1000000000 | bytes 4000000 | tf_op jit(solution)/shard_map/spread_late/pallas_call | solution.py:459
  (40 shorter events, 2.4 us)
Async XLA Ops:
  11.8 7.1 %collective-permute-start = (bf16[16,384,256]{2,1,0:T(8,128)(2,1)S(1)}, bf16[16,384,256]{2,1,0:T(8,128)(2,1)S(1)}, u32[]{:S(2)}, u32[]{:S(2)}) collective-permute-start(bf16[16,384,256]{2,1,0:T(8,128)(2,1)S(1)} %get-tuple-element.71), channel_id=1, source_target_pairs={{0,4},{4,0},{8,12},{12,8},{16,20},{20,16},{24,28},{28,24},{32,36},... | collective-permute-start | bytes 9437192 | tf_op jit(solution)/shard_map/ppermute | solution.py:641
  20.0 12.5 %collective-permute-start.1 = (bf16[4,384,256]{2,1,0:T(8,128)(2,1)S(1)}, bf16[4,384,256]{2,1,0:T(8,128)(2,1)S(1)}, u32[]{:S(2)}, u32[]{:S(2)}) collective-permute-start(bf16[4,384,256]{2,1,0:T(8,128)(2,1)S(1)} %get-tuple-element.78), channel_id=1, source_target_pairs={{0,64},{4,20},{8,72},{12,28},{16,80},{20,4},{24,88},{28,12},{32,96... | collective-permute-start | bytes 2359304 | tf_op jit(solution)/shard_map/ppermute | solution.py:637
  21.3 19.6 %collective-permute-start.2 = (bf16[4,384,256]{2,1,0:T(8,128)(2,1)S(1)}, bf16[4,384,256]{2,1,0:T(8,128)(2,1)S(1)}, u32[]{:S(2)}, u32[]{:S(2)}) collective-permute-start(bf16[4,384,256]{2,1,0:T(8,128)(2,1)S(1)} %get-tuple-element.79), channel_id=1, source_target_pairs={{0,32},{4,12},{8,40},{12,20},{16,48},{20,28},{24,56},{28,4},{32,64... | collective-permute-start | bytes 2359304 | tf_op jit(solution)/shard_map/ppermute | solution.py:637
  24.8 17.8 %collective-permute-start.3 = (bf16[4,384,256]{2,1,0:T(8,128)(2,1)S(1)}, bf16[4,384,256]{2,1,0:T(8,128)(2,1)S(1)}, u32[]{:S(2)}, u32[]{:S(2)}) collective-permute-start(bf16[4,384,256]{2,1,0:T(8,128)(2,1)S(1)} %get-tuple-element.80), channel_id=1, source_target_pairs={{0,96},{4,28},{8,104},{12,4},{16,112},{20,12},{24,120},{28,20},{32... | collective-permute-start | bytes 2359304 | tf_op jit(solution)/shard_map/ppermute | solution.py:637
  42.7 8.7 %copy-start = (bf16[3,256,1024]{2,1,0:T(8,128)(2,1)S(1)}, bf16[3,256,1024]{2,1,0:T(8,128)(2,1)}, u32[]{:S(2)}) copy-start(bf16[3,256,1024]{2,1,0:T(8,128)(2,1)} %weights.3) | copy-start | bytes 4718596
  43.1 14.4 %copy-start.2 = (bf16[256]{0:T(256)(128)(2,1)S(1)}, bf16[256]{0:T(256)(128)(2,1)}, u32[]{:S(2)}) copy-start(bf16[256]{0:T(256)(128)(2,1)} %param.32) | copy-start | bytes 1540
  43.1 16.0 %copy-start.1 = (bf16[128,256]{1,0:T(8,128)(2,1)S(1)}, bf16[128,256]{1,0:T(8,128)(2,1)}, u32[]{:S(2)}) copy-start(bf16[128,256]{1,0:T(8,128)(2,1)} %param.33) | copy-start | bytes 196612
  43.1 6.2 %collective-permute-start.4 = (bf16[384,256]{1,0:T(8,128)(2,1)S(1)}, bf16[384,256]{1,0:T(8,128)(2,1)S(1)}, u32[]{:S(2)}, u32[]{:S(2)}) collective-permute-start(bf16[384,256]{1,0:T(8,128)(2,1)S(1)} %get-tuple-element.140), channel_id=1, source_target_pairs={{0,16},{4,68},{8,24},{12,76},{16,0},{20,84},{24,8},{28,92},{32,48}... | collective-permute-start | bytes 589832 | tf_op jit(solution)/shard_map/ppermute | solution.py:637
  43.2 6.1 %collective-permute-start.5 = (bf16[384,256]{1,0:T(8,128)(2,1)S(1)}, bf16[384,256]{1,0:T(8,128)(2,1)S(1)}, u32[]{:S(2)}, u32[]{:S(2)}) collective-permute-start(bf16[384,256]{1,0:T(8,128)(2,1)S(1)} %get-tuple-element.139), channel_id=1, source_target_pairs={{0,8},{4,36},{8,16},{12,44},{16,24},{20,52},{24,0},{28,60},{32,40}... | collective-permute-start | bytes 589832 | tf_op jit(solution)/shard_map/ppermute | solution.py:637
  43.3 8.0 %collective-permute-start.6 = (bf16[384,256]{1,0:T(8,128)(2,1)S(1)}, bf16[384,256]{1,0:T(8,128)(2,1)S(1)}, u32[]{:S(2)}, u32[]{:S(2)}) collective-permute-start(bf16[384,256]{1,0:T(8,128)(2,1)S(1)} %get-tuple-element.138), channel_id=1, source_target_pairs={{0,24},{4,100},{8,0},{12,108},{16,8},{20,116},{24,16},{28,124},{32... | collective-permute-start | bytes 589832 | tf_op jit(solution)/shard_map/ppermute | solution.py:637
  51.8 5.7 %collective-permute-start.7 = (bf16[128,256]{1,0:T(8,128)(2,1)S(1)}, bf16[128,256]{1,0:T(8,128)(2,1)S(1)}, u32[]{:S(2)}, u32[]{:S(2)}) collective-permute-start(bf16[128,256]{1,0:T(8,128)(2,1)S(1)} %get-tuple-element.91), channel_id=1, source_target_pairs={{0,2},{1,3},{2,0},{3,1},{4,6},{5,7},{6,4},{7,5},{8,10},{9,11},{10,... | collective-permute-start | bytes 196616 | tf_op jit(solution)/shard_map/ppermute | solution.py:663
  54.8 4.3 %collective-permute-start.8 = (bf16[128,256]{1,0:T(8,128)(2,1)S(1)}, bf16[128,256]{1,0:T(8,128)(2,1)S(1)}, u32[]{:S(2)}, u32[]{:S(2)}) collective-permute-start(bf16[128,256]{1,0:T(8,128)(2,1)S(1)} %get-tuple-element.92), channel_id=1, source_target_pairs={{0,1},{1,2},{2,3},{3,0},{4,5},{5,6},{6,7},{7,4},{8,9},{9,10},{10,1... | collective-permute-start | bytes 196616 | tf_op jit(solution)/shard_map/ppermute | solution.py:663
  55.2 3.9 %collective-permute-start.9 = (bf16[128,256]{1,0:T(8,128)(2,1)S(1)}, bf16[128,256]{1,0:T(8,128)(2,1)S(1)}, u32[]{:S(2)}, u32[]{:S(2)}) collective-permute-start(bf16[128,256]{1,0:T(8,128)(2,1)S(1)} %get-tuple-element.93), channel_id=1, source_target_pairs={{0,3},{1,0},{2,1},{3,2},{4,7},{5,4},{6,5},{7,6},{8,11},{9,8},{10,9... | collective-permute-start | bytes 196616 | tf_op jit(solution)/shard_map/ppermute | solution.py:663
  59.9 4.6 %collective-permute-start.10 = (bf16[128,256]{1,0:T(8,128)(2,1)S(1)}, bf16[128,256]{1,0:T(8,128)(2,1)S(1)}, u32[]{:S(2)}, u32[]{:S(2)}) collective-permute-start(bf16[128,256]{1,0:T(8,128)(2,1)S(1)} %get-tuple-element.104.grad0), channel_id=1, source_target_pairs={{0,2},{1,3},{2,0},{3,1},{4,6},{5,7},{6,4},{7,5},{8,10},{9,11},{10,... | collective-permute-start | bytes 196616 | tf_op jit(solution)/shard_map/ppermute | solution.py:663
  61.6 4.0 %collective-permute-start.11 = (bf16[128,256]{1,0:T(8,128)(2,1)S(1)}, bf16[128,256]{1,0:T(8,128)(2,1)S(1)}, u32[]{:S(2)}, u32[]{:S(2)}) collective-permute-start(bf16[128,256]{1,0:T(8,128)(2,1)S(1)} %get-tuple-element.104.grad0), channel_id=1, source_target_pairs={{0,3},{1,0},{2,1},{3,2},{4,7},{5,4},{6,5},{7,6},{8,11},{9,8},{10,9... | collective-permute-start | bytes 196616 | tf_op jit(solution)/shard_map/ppermute | solution.py:663
  62.7 5.0 %collective-permute-start.12 = (bf16[128,256]{1,0:T(8,128)(2,1)S(1)}, bf16[128,256]{1,0:T(8,128)(2,1)S(1)}, u32[]{:S(2)}, u32[]{:S(2)}) collective-permute-start(bf16[128,256]{1,0:T(8,128)(2,1)S(1)} %get-tuple-element.104.grad0), channel_id=1, source_target_pairs={{0,1},{1,2},{2,3},{3,0},{4,5},{5,6},{6,7},{7,4},{8,9},{9,10},{10,1... | collective-permute-start | bytes 196616 | tf_op jit(solution)/shard_map/ppermute | solution.py:663
  69.6 7.1 %collective-permute-start.20 = (bf16[16,192,128]{2,1,0:T(8,128)(2,1)S(1)}, bf16[16,192,128]{2,1,0:T(8,128)(2,1)S(1)}, u32[]{:S(2)}, u32[]{:S(2)}) collective-permute-start(bf16[16,192,128]{2,1,0:T(8,128)(2,1)S(1)} %get-tuple-element.110), channel_id=1, source_target_pairs={{0,4},{4,0},{8,12},{12,8},{16,20},{20,16},{24,28},{28,24},{32,36},... | collective-permute-start | bytes 2359304 | tf_op jit(solution)/shard_map/ppermute | solution.py:641
  72.9 6.3 %collective-permute-start.13 = (bf16[3,128,256]{2,1,0:T(8,128)(2,1)S(1)}, bf16[3,128,256]{2,1,0:T(8,128)(2,1)S(1)}, u32[]{:S(2)}, u32[]{:S(2)}) collective-permute-start(bf16[3,128,256]{2,1,0:T(8,128)(2,1)S(1)} %form_messages.1.refs_0_), channel_id=1, source_target_pairs={{0,64},{4,20},{8,72},{12,28},{16,80},{20,4},{24,88},{28,12},{32,96... | collective-permute-start | bytes 589832 | tf_op jit(solution)/shard_map/ppermute | solution.py:637
  73.9 7.4 %collective-permute-start.14 = (bf16[3,128,256]{2,1,0:T(8,128)(2,1)S(1)}, bf16[3,128,256]{2,1,0:T(8,128)(2,1)S(1)}, u32[]{:S(2)}, u32[]{:S(2)}) collective-permute-start(bf16[3,128,256]{2,1,0:T(8,128)(2,1)S(1)} %form_messages.1.refs_0_), channel_id=1, source_target_pairs={{0,32},{4,12},{8,40},{12,20},{16,48},{20,28},{24,56},{28,4},{32,64... | collective-permute-start | bytes 589832 | tf_op jit(solution)/shard_map/ppermute | solution.py:637
  75.9 5.5 %collective-permute-start.15 = (bf16[3,128,256]{2,1,0:T(8,128)(2,1)S(1)}, bf16[3,128,256]{2,1,0:T(8,128)(2,1)S(1)}, u32[]{:S(2)}, u32[]{:S(2)}) collective-permute-start(bf16[3,128,256]{2,1,0:T(8,128)(2,1)S(1)} %form_messages.1.refs_0_), channel_id=1, source_target_pairs={{0,96},{4,28},{8,104},{12,4},{16,112},{20,12},{24,120},{28,20},{32... | collective-permute-start | bytes 589832 | tf_op jit(solution)/shard_map/ppermute | solution.py:637
  76.8 12.6 %collective-permute-start.21 = (bf16[4,192,128]{2,1,0:T(8,128)(2,1)S(1)}, bf16[4,192,128]{2,1,0:T(8,128)(2,1)S(1)}, u32[]{:S(2)}, u32[]{:S(2)}) collective-permute-start(bf16[4,192,128]{2,1,0:T(8,128)(2,1)S(1)} %get-tuple-element.144), channel_id=1, source_target_pairs={{0,16},{4,68},{8,24},{12,76},{16,0},{20,84},{24,8},{28,92},{32,48}... | collective-permute-start | bytes 589832 | tf_op jit(solution)/shard_map/ppermute | solution.py:637
  81.4 39.4 %collective-permute-start.16 = (bf16[12,128,256]{2,1,0:T(8,128)(2,1)S(1)}, bf16[12,128,256]{2,1,0:T(8,128)(2,1)S(1)}, u32[]{:S(2)}, u32[]{:S(2)}) collective-permute-start(bf16[12,128,256]{2,1,0:T(8,128)(2,1)S(1)} %join_blocks.1.own0), channel_id=1, source_target_pairs={{0,16},{4,68},{8,24},{12,76},{16,0},{20,84},{24,8},{28,92},{32,48}... | collective-permute-start | bytes 2359304 | tf_op jit(solution)/shard_map/ppermute | solution.py:637
  83.5 37.3 %collective-permute-start.17 = (bf16[12,128,256]{2,1,0:T(8,128)(2,1)S(1)}, bf16[12,128,256]{2,1,0:T(8,128)(2,1)S(1)}, u32[]{:S(2)}, u32[]{:S(2)}) collective-permute-start(bf16[12,128,256]{2,1,0:T(8,128)(2,1)S(1)} %join_blocks.1.own0), channel_id=1, source_target_pairs={{0,8},{4,36},{8,16},{12,44},{16,24},{20,52},{24,0},{28,60},{32,40}... | collective-permute-start | bytes 2359304 | tf_op jit(solution)/shard_map/ppermute | solution.py:637
  84.3 36.5 %collective-permute-start.18 = (bf16[12,128,256]{2,1,0:T(8,128)(2,1)S(1)}, bf16[12,128,256]{2,1,0:T(8,128)(2,1)}, u32[]{:S(2)}, u32[]{:S(2)}) collective-permute-start(bf16[12,128,256]{2,1,0:T(8,128)(2,1)S(1)} %join_blocks.1.own0), channel_id=1, source_target_pairs={{0,24},{4,100},{8,0},{12,108},{16,8},{20,116},{24,16},{28,124},{32... | collective-permute-start | bytes 2359304 | tf_op jit(solution)/shard_map/ppermute | solution.py:637
  84.9 35.9 %collective-permute-start.19 = (bf16[12,128,256]{2,1,0:T(8,128)(2,1)S(1)}, bf16[12,128,256]{2,1,0:T(8,128)(2,1)S(1)}, u32[]{:S(2)}, u32[]{:S(2)}) collective-permute-start(bf16[12,128,256]{2,1,0:T(8,128)(2,1)S(1)} %join_blocks.1.own0), channel_id=1, source_target_pairs={{0,4},{4,0},{8,12},{12,8},{16,20},{20,16},{24,28},{28,24},{32,36},... | collective-permute-start | bytes 2359304 | tf_op jit(solution)/shard_map/ppermute | solution.py:641
  89.4 13.4 %collective-permute-start.22 = (bf16[4,192,128]{2,1,0:T(8,128)(2,1)S(1)}, bf16[4,192,128]{2,1,0:T(8,128)(2,1)S(1)}, u32[]{:S(2)}, u32[]{:S(2)}) collective-permute-start(bf16[4,192,128]{2,1,0:T(8,128)(2,1)S(1)} %get-tuple-element.143), channel_id=1, source_target_pairs={{0,8},{4,36},{8,16},{12,44},{16,24},{20,52},{24,0},{28,60},{32,40}... | collective-permute-start | bytes 589832 | tf_op jit(solution)/shard_map/ppermute | solution.py:637
  102.7 6.0 %collective-permute-start.23 = (bf16[4,192,128]{2,1,0:T(8,128)(2,1)S(1)}, bf16[4,192,128]{2,1,0:T(8,128)(2,1)S(1)}, u32[]{:S(2)}, u32[]{:S(2)}) collective-permute-start(bf16[4,192,128]{2,1,0:T(8,128)(2,1)S(1)} %get-tuple-element.142), channel_id=1, source_target_pairs={{0,24},{4,100},{8,0},{12,108},{16,8},{20,116},{24,16},{28,124},{32... | collective-permute-start | bytes 589832 | tf_op jit(solution)/shard_map/ppermute | solution.py:637
  108.9 4.5 %collective-permute-start.24 = (bf16[192,128]{1,0:T(8,128)(2,1)S(1)}, bf16[192,128]{1,0:T(8,128)(2,1)S(1)}, u32[]{:S(2)}, u32[]{:S(2)}) collective-permute-start(bf16[192,128]{1,0:T(8,128)(2,1)S(1)} %get-tuple-element.147), channel_id=1, source_target_pairs={{0,64},{4,20},{8,72},{12,28},{16,80},{20,4},{24,88},{28,12},{32,96... | collective-permute-start | bytes 147464 | tf_op jit(solution)/shard_map/ppermute | solution.py:637
  113.4 4.2 %collective-permute-start.25 = (bf16[192,128]{1,0:T(8,128)(2,1)S(1)}, bf16[192,128]{1,0:T(8,128)(2,1)S(1)}, u32[]{:S(2)}, u32[]{:S(2)}) collective-permute-start(bf16[192,128]{1,0:T(8,128)(2,1)S(1)} %get-tuple-element.146), channel_id=1, source_target_pairs={{0,32},{4,12},{8,40},{12,20},{16,48},{20,28},{24,56},{28,4},{32,64... | collective-permute-start | bytes 147464 | tf_op jit(solution)/shard_map/ppermute | solution.py:637
  117.6 3.2 %collective-permute-start.26 = (bf16[192,128]{1,0:T(8,128)(2,1)S(1)}, bf16[192,128]{1,0:T(8,128)(2,1)S(1)}, u32[]{:S(2)}, u32[]{:S(2)}) collective-permute-start(bf16[192,128]{1,0:T(8,128)(2,1)S(1)} %get-tuple-element.145), channel_id=1, source_target_pairs={{0,96},{4,28},{8,104},{12,4},{16,112},{20,12},{24,120},{28,20},{32... | collective-permute-start | bytes 147464 | tf_op jit(solution)/shard_map/ppermute | solution.py:637
  120.8 18.2 %collective-permute-start.27 = (bf16[12,128,256]{2,1,0:T(8,128)(2,1)S(1)}, bf16[12,128,256]{2,1,0:T(8,128)(2,1)}, u32[]{:S(2)}, u32[]{:S(2)}) collective-permute-start(bf16[12,128,256]{2,1,0:T(8,128)(2,1)S(1)} %collective-permute-done.16.own2), channel_id=1, source_target_pairs={{0,4},{4,0},{8,12},{12,8},{16,20},{20,16},{24,28},{28,24},{32,36},... | collective-permute-start | bytes 2359304 | tf_op jit(solution)/shard_map/ppermute | solution.py:641
  131.0 8.0 %collective-permute-start.28 = (bf16[12,128,256]{2,1,0:T(8,128)(2,1)S(1)}, bf16[12,128,256]{2,1,0:T(8,128)(2,1)}, u32[]{:S(2)}, u32[]{:S(2)}) collective-permute-start(bf16[12,128,256]{2,1,0:T(8,128)(2,1)S(1)} %collective-permute-done.17.own3), channel_id=1, source_target_pairs={{0,4},{4,0},{8,12},{12,8},{16,20},{20,16},{24,28},{28,24},{32,36},... | collective-permute-start | bytes 2359304 | tf_op jit(solution)/shard_map/ppermute | solution.py:641
  131.1 8.0 %collective-permute-start.29 = (bf16[12,128,256]{2,1,0:T(8,128)(2,1)}, bf16[12,128,256]{2,1,0:T(8,128)(2,1)}, u32[]{:S(2)}, u32[]{:S(2)}) collective-permute-start(bf16[12,128,256]{2,1,0:T(8,128)(2,1)} %collective-permute-done.18.own1), channel_id=1, source_target_pairs={{0,4},{4,0},{8,12},{12,8},{16,20},{20,16},{24,28},{28,24},{32,36},... | collective-permute-start | bytes 2359304 | tf_op jit(solution)/shard_map/ppermute | solution.py:641

commit v5 on v4

--- a/solution.py
+++ b/solution.py
@@ -16,7 +16,7 @@
 F32 = jnp.float32
 MIB = 1024 * 1024
 GATHER_LIMIT = 36 * MIB
-SPREAD_LIMIT = 20 * MIB
+SPREAD_LIMIT = 12 * MIB
 barrier = lax.optimization_barrier
 
 
@@ -343,35 +343,25 @@
     return lax.fori_loop(0, (amount + PAIRS - 1) // PAIRS, add_group, jnp.int32(0))
 
 
-def start_pieces(pieces, places, messages, sems):
-    copies = [
-        pltpu.make_async_copy(piece, messages.at[pl.ds(at * 3, 12)], sems.at[number])
-        for number, (piece, at) in enumerate(zip(pieces, places))
-    ]
-    for copy in copies:
-        copy.start()
-    return copies
-
-
 def spread_early_kernel(
     pair_a, pair_b, pair_spot, amounts, counts0, counts1, counts2, tiles0, tiles1, tiles2,
     own0, own2, own3, own1, sib0,
-    out, buffer, messages, total, tile_sems, piece_sems,
+    out, buffer, messages, total, tile_sems, piece_sem,
 ):
     tiles = (tiles0, tiles1, tiles2)
-    copies = start_pieces((own1,), (4,), messages, piece_sems)
+    copy = pltpu.make_async_copy(sib0, messages.at[pl.ds(48, 12)], piece_sem)
+    copy.start()
     begins = start_tiles(tiles, (counts0, counts1, counts2), buffer, tile_sems)
 
     def place(block, carry):
-        for piece, at in ((own0, 0), (own2, 8), (own3, 12), (sib0, 16)):
+        for piece, at in ((own0, 0), (own2, 8), (own3, 12), (own1, 4)):
             messages[at * 3 + block] = piece[block]
         return carry
 
     lax.fori_loop(0, 12, place, 0)
     buffer[buffer.shape[0] - 1] = jnp.zeros((TILE, TILE), BF16)
     clear(total, 16)
-    for copy in copies:
-        copy.wait()
+    copy.wait()
 
     def ready(waited, last):
         needed = jnp.minimum((last >> 4) + 1, begins[3])
@@ -391,17 +381,20 @@
 
 def spread_late_kernel(
     pair_a, pair_b, pair_spot, amounts, buffer, before, sib2, sib3, sib1,
-    out, messages, total, piece_sems,
+    out, messages, total,
 ):
-    copies = start_pieces((sib2, sib3, sib1), (4, 8, 0), messages, piece_sems)
+    def place(block, carry):
+        for piece, at in ((sib2, 4), (sib3, 8), (sib1, 0)):
+            messages[at * 3 + block] = piece[block]
+        return carry
+
+    lax.fori_loop(0, 12, place, 0)
 
     def take(block, carry):
         total[block] = before[block]
         return carry
 
     lax.fori_loop(0, 16, take, 0)
-    for copy in copies:
-        copy.wait()
     spread_list(
         (pair_a, pair_b, pair_spot),
         pair_a.shape[0] // 2,
@@ -431,14 +424,14 @@
         ),
         in_specs=[spec(SMEM)] * 7
         + [spec(ANY)] * 3
-        + [spec(VMEM)] * 3
-        + [spec(ANY), spec(VMEM)],
+        + [spec(VMEM)] * 4
+        + [spec(ANY)],
         out_specs=(spec(VMEM), spec(VMEM)),
         scratch_shapes=[
             pltpu.VMEM((3 * EARLY, TILE, width), BF16),
             pltpu.VMEM((17, TILE, width), F32),
             pltpu.SemaphoreType.DMA((slots // GROUP,)),
-            pltpu.SemaphoreType.DMA((1,)),
+            pltpu.SemaphoreType.DMA(()),
         ],
         compiler_params=pltpu.CompilerParams(vmem_limit_bytes=SPREAD_LIMIT),
         cost_estimate=pl.CostEstimate(
@@ -449,7 +442,7 @@
         *plan,
         *[relation[3] for relation in relations],
         *tile_args(relations),
-        whole, own2, own3, in_hbm(own1), beside,
+        whole, own2, own3, own1, in_hbm(beside),
     )
 
 
@@ -459,19 +452,18 @@
     return pl.pallas_call(
         spread_late_kernel,
         out_shape=jax.ShapeDtypeStruct((16, TILE, width), BF16),
-        in_specs=[spec(SMEM)] * 4 + [spec(VMEM)] * 2 + [spec(ANY)] * 3,
+        in_specs=[spec(SMEM)] * 4 + [spec(VMEM)] * 5,
         out_specs=spec(VMEM),
         scratch_shapes=[
             pltpu.VMEM((3 * (32 - EARLY), TILE, width), BF16),
             pltpu.VMEM((17, TILE, width), F32),
-            pltpu.SemaphoreType.DMA((3,)),
         ],
         compiler_params=pltpu.CompilerParams(vmem_limit_bytes=SPREAD_LIMIT),
         cost_estimate=pl.CostEstimate(
             flops=10**9, bytes_accessed=4 * 10**6, transcendentals=0
         ),
         name="spread_late",
-    )(*plan, buffer, before, *[in_hbm(piece) for piece in pieces])
+    )(*plan, buffer, before, *pieces)
 
 
 def columns_at(step, width):
@@ -725,18 +717,18 @@
     beside = swap(whole)
     line = [add(quarters[0][k], *[part[k] for part in arrived]) for k in range(4)]
     weight_parts = three_ways(line)
-    *spread_out, beside, l0, w0, w1, w2 = barrier((*spread_out, beside, line[0], *weight_parts))
-    weight_parts = (w0, w1, w2)
+    weight_sum = line[0].astype(F32)
+    for part in weight_parts:
+        weight_sum = weight_sum + part.astype(F32)
+    grad_weight = weight_sum.reshape(3 * width // TILE, 32, TILE).transpose(0, 2, 1)
+    grad_weight = grad_weight.reshape(3, width, 32)
+    *spread_out, beside, grad_weight = barrier((*spread_out, beside, grad_weight))
     siblings = [swap(piece) for piece in spread_out]
     early = spread_early(plan, relations, [whole, *spread_out, beside])
     grad_source = spread_late(plan, early, siblings)
-    weight_sum = l0.astype(F32)
-    for part in weight_parts:
-        weight_sum = weight_sum + part.astype(F32)
-    grad_weight = weight_sum.reshape(3 * width // TILE, 32, TILE).transpose(0, 2, 1)
     return (
         mixed_out.astype(BF16),
-        grad_weight.reshape(3, width, 32),
+        grad_weight,
         grad_source.reshape(-1, width),
     )
 

time: 145 us -> 122 us (0.84)
  starting transfers between devices: 46.8 us -> 34.8 us
  waiting for transfers between devices: 55.3 us -> 45.6 us
    ppermute x6, starting transfers between devices: 18.6 us -> 8.93 us  [swap(): return lax.ppermute(value, 'src', [(s, s ^ 1) for s in range(32)])]
    ppermute x18, waiting for transfers between devices: 49.2 us -> 39.5 us  [shift(): return lax.ppermute(value, 'src', shift_pairs(step, second))]
    ppermute x18, starting transfers between devices: 19.1 us -> 16.8 us  [shift(): return lax.ppermute(value, 'src', shift_pairs(step, second))]
  transfers between devices with their start and end apart: 30 -> 30, of which waited for: 16 -> 15; matrix products, arithmetic and copies ran while one was open for 1% -> 1% of each run, Pallas kernels for 13% -> 16%
where the time goes in v5:
time: 122 us
  waiting for transfers between devices  45.6 us (37%)
  Pallas kernels  35.1 us (29%)
  starting transfers between devices  34.8 us (29%)
  between operations  2.83 us (2%)
  other arithmetic  2.49 us (2%)
    ppermute x18, waiting for transfers between devices, shift(): return lax.ppermute(value, 'src', shift_pairs(step, second))  39.5 us
    ppermute x18, starting transfers between devices, shift(): return lax.ppermute(value, 'src', shift_pairs(step, second))  16.8 us
    pallas_call x1, Pallas kernels, gather_sums(): pl.pallas_call(gather_send_kernel, out_shape=(blocks, jax.ShapeDtypeStruc...  9.24 us
    ppermute x6, starting transfers between devices, turn(): lax.ppermute(value, 'tgt', [(t, (t + step) % SIDE) for t in range(SIDE)])  9.06 us
    ppermute x6, starting transfers between devices, swap(): return lax.ppermute(value, 'src', [(s, s ^ 1) for s in range(32)])  8.93 us
    pallas_call x1, Pallas kernels, gather_sums(): pl.pallas_call(gather_keep_kernel, out_shape=blocks, in_specs=[spec(SMEM)...  7.02 us
    pallas_call x1, Pallas kernels, spread_early(): pl.pallas_call(spread_early_kernel, out_shape=(jax.ShapeDtypeStruct((16,...  6.68 us
    ppermute x6, waiting for transfers between devices, turn(): lax.ppermute(value, 'tgt', [(t, (t + step) % SIDE) for t in range(SIDE)])  6.09 us
  transfers between devices with their start and end apart: 30, of which 15 were waited for; matrix products, arithmetic and copies ran while one was open for 1% of the time, Pallas kernels for 16%

profile of v5, /device:TPU:7, one launch (start us, length us, event | category | flops | bytes accessed | tf_op | source)
XLA Modules:
  0.0 121.7 jit_solution(15454462795317250165)
XLA Ops:
  2.6 9.2 %gather_send.1 = (bf16[16,384,256]{2,1,0:T(8,128)(2,1)S(1)}, s32[352]{0:T(512)S(1)}, s32[1]{0:T(128)}, bf16[336,128,128]{2,1,0:T(8,128)(2,1)S(1)}, bf16[16,128,256]{2,1,0:T(8,128)(2,1)S(1)}) custom-call(s32[32]{0:T(128)} %owner_map.2, s32[192]{0:T(256)} %targets0.3, s32[96]{0:T(128)} %targets1.3, s32[48]{0:T(128)} %targets2.3, s32[192]{0:T(256)} %sources0.3, ...), custom_call_target="tpu_custom_call" | custom-call | flops 2000000000 | bytes 12000000 | tf_op jit(solution)/shard_map/gather_send/pallas_call | solution.py:204
  11.9 7.0 %gather_keep.1 = bf16[16,384,256]{2,1,0:T(8,128)(2,1)S(1)} custom-call(s32[352]{0:T(512)S(1)} %get-tuple-element.64.codes, s32[1]{0:T(128)} %get-tuple-element.65.amount, bf16[336,128,128]{2,1,0:T(8,128)(2,1)S(1)} %get-tuple-element.66.buffer, bf16[16,128,256]{2,1,0:T(8,128)(2,1)S(1)} %get-tuple-element.67.held), custom_call_target="tpu_custom_call" | custom-call | flops 2000000000 | bytes 12000000 | tf_op jit(solution)/shard_map/gather_keep/pallas_call | solution.py:225
  19.0 1.0 add_convert_fusion
  20.0 1.3 %collective-permute-start.1 = (bf16[4,384,256]{2,1,0:T(8,128)(2,1)S(1)}, bf16[4,384,256]{2,1,0:T(8,128)(2,1)S(1)}, u32[]{:S(2)}, u32[]{:S(2)}) collective-permute-start(bf16[4,384,256]{2,1,0:T(8,128)(2,1)S(1)} %get-tuple-element.75), channel_id=1, source_target_pairs={{0,64},{4,20},{8,72},{12,28},{16,80},{20,4},{24,88},{28,12},{32,96... | collective-permute-start | bytes 2359304 | tf_op jit(solution)/shard_map/ppermute | solution.py:629
  21.3 3.6 %collective-permute-start.2 = (bf16[4,384,256]{2,1,0:T(8,128)(2,1)S(1)}, bf16[4,384,256]{2,1,0:T(8,128)(2,1)S(1)}, u32[]{:S(2)}, u32[]{:S(2)}) collective-permute-start(bf16[4,384,256]{2,1,0:T(8,128)(2,1)S(1)} %get-tuple-element.76), channel_id=1, source_target_pairs={{0,32},{4,12},{8,40},{12,20},{16,48},{20,28},{24,56},{28,4},{32,64... | collective-permute-start | bytes 2359304 | tf_op jit(solution)/shard_map/ppermute | solution.py:629
  24.8 5.6 %plan_spread.1 = (s32[432]{0:T(512)S(1)}, s32[432]{0:T(512)S(1)}, s32[432]{0:T(512)S(1)}, s32[2]{0:T(128)S(1)}) custom-call(s32[32]{0:T(128)} %owner_map.2, s32[192]{0:T(256)} %targets0.3, s32[96]{0:T(128)} %targets1.3, s32[48]{0:T(128)} %targets2.3, s32[192]{0:T(256)} %sources0.3, s32[96]{0:T(128)} %sources1.3, s32[48]{0:T(128)} %sources2.3, ...), custom_call_target="tpu_custom_call" | custom-call | flops 1000000000 | bytes 1000000 | tf_op jit(solution)/shard_map/plan_spread/pallas_call | solution.py:311
  30.4 2.1 %collective-permute-done.1 = bf16[4,384,256]{2,1,0:T(8,128)(2,1)S(1)} collective-permute-done((bf16[4,384,256]{2,1,0:T(8,128)(2,1)S(1)}, bf16[4,384,256]{2,1,0:T(8,128)(2,1)S(1)}, u32[]{:S(2)}, u32[]{:S(2)}) %collective-permute-start.1) | collective-permute-done | bytes 786464 | tf_op jit(solution)/shard_map/ppermute | solution.py:629
  32.5 8.3 %collective-permute-done.2 = bf16[4,384,256]{2,1,0:T(8,128)(2,1)S(1)} collective-permute-done((bf16[4,384,256]{2,1,0:T(8,128)(2,1)S(1)}, bf16[4,384,256]{2,1,0:T(8,128)(2,1)S(1)}, u32[]{:S(2)}, u32[]{:S(2)}) %collective-permute-start.2) | collective-permute-done | bytes 786464 | tf_op jit(solution)/shard_map/ppermute | solution.py:629
  40.8 1.9 %collective-permute-done.3 = bf16[4,384,256]{2,1,0:T(8,128)(2,1)S(1)} collective-permute-done((bf16[4,384,256]{2,1,0:T(8,128)(2,1)S(1)}, bf16[4,384,256]{2,1,0:T(8,128)(2,1)S(1)}, u32[]{:S(2)}, u32[]{:S(2)}) %collective-permute-start.3) | collective-permute-done | bytes 786464 | tf_op jit(solution)/shard_map/ppermute | solution.py:629
  42.7 0.4 fusion.3
  43.3 1.5 %collective-permute-start.6 = (bf16[384,256]{1,0:T(8,128)(2,1)S(1)}, bf16[384,256]{1,0:T(8,128)(2,1)S(1)}, u32[]{:S(2)}, u32[]{:S(2)}) collective-permute-start(bf16[384,256]{1,0:T(8,128)(2,1)S(1)} %get-tuple-element.132), channel_id=1, source_target_pairs={{0,24},{4,100},{8,0},{12,108},{16,8},{20,116},{24,16},{28,124},{32... | collective-permute-start | bytes 589832 | tf_op jit(solution)/shard_map/ppermute | solution.py:629
  44.8 4.6 %collective-permute-done.4.part1 = bf16[384,256]{1,0:T(8,128)(2,1)S(1)} collective-permute-done((bf16[384,256]{1,0:T(8,128)(2,1)S(1)}, bf16[384,256]{1,0:T(8,128)(2,1)S(1)}, u32[]{:S(2)}, u32[]{:S(2)}) %collective-permute-start.4) | collective-permute-done | bytes 196640 | tf_op jit(solution)/shard_map/ppermute | solution.py:629
  49.4 2.0 %collective-permute-done.6.part3 = bf16[384,256]{1,0:T(8,128)(2,1)S(1)} collective-permute-done((bf16[384,256]{1,0:T(8,128)(2,1)S(1)}, bf16[384,256]{1,0:T(8,128)(2,1)S(1)}, u32[]{:S(2)}, u32[]{:S(2)}) %collective-permute-start.6) | collective-permute-done | bytes 196640 | tf_op jit(solution)/shard_map/ppermute | solution.py:629
  51.4 0.4 hidden_terms.1
  51.8 3.0 %collective-permute-start.7 = (bf16[128,256]{1,0:T(8,128)(2,1)S(1)}, bf16[128,256]{1,0:T(8,128)(2,1)S(1)}, u32[]{:S(2)}, u32[]{:S(2)}) collective-permute-start(bf16[128,256]{1,0:T(8,128)(2,1)S(1)} %get-tuple-element.88), channel_id=1, source_target_pairs={{0,2},{1,3},{2,0},{3,1},{4,6},{5,7},{6,4},{7,5},{8,10},{9,11},{10,... | collective-permute-start | bytes 196616 | tf_op jit(solution)/shard_map/ppermute | solution.py:655
  54.8 0.4 collective-permute-start.8
  55.2 2.3 %collective-permute-start.9 = (bf16[128,256]{1,0:T(8,128)(2,1)S(1)}, bf16[128,256]{1,0:T(8,128)(2,1)S(1)}, u32[]{:S(2)}, u32[]{:S(2)}) collective-permute-start(bf16[128,256]{1,0:T(8,128)(2,1)S(1)} %get-tuple-element.90), channel_id=1, source_target_pairs={{0,3},{1,0},{2,1},{3,2},{4,7},{5,4},{6,5},{7,6},{8,11},{9,8},{10,9... | collective-permute-start | bytes 196616 | tf_op jit(solution)/shard_map/ppermute | solution.py:655
  57.5 1.6 %collective-permute-done.8 = bf16[128,256]{1,0:T(8,128)(2,1)S(1)} collective-permute-done((bf16[128,256]{1,0:T(8,128)(2,1)S(1)}, bf16[128,256]{1,0:T(8,128)(2,1)S(1)}, u32[]{:S(2)}, u32[]{:S(2)}) %collective-permute-start.8) | collective-permute-done | bytes 65568 | tf_op jit(solution)/shard_map/ppermute | solution.py:655
  59.1 0.8 fusion.6
  59.9 1.7 %collective-permute-start.10 = (bf16[128,256]{1,0:T(8,128)(2,1)S(1)}, bf16[128,256]{1,0:T(8,128)(2,1)S(1)}, u32[]{:S(2)}, u32[]{:S(2)}) collective-permute-start(bf16[128,256]{1,0:T(8,128)(2,1)S(1)} %get-tuple-element.101.grad0), channel_id=1, source_target_pairs={{0,2},{1,3},{2,0},{3,1},{4,6},{5,7},{6,4},{7,5},{8,10},{9,11},{10,... | collective-permute-start | bytes 196616 | tf_op jit(solution)/shard_map/ppermute | solution.py:655
  61.6 1.1 collective-permute-start.11
  62.7 0.6 collective-permute-start.12
  63.3 1.2 %collective-permute-done.10.grad2 = bf16[128,256]{1,0:T(8,128)(2,1)S(1)} collective-permute-done((bf16[128,256]{1,0:T(8,128)(2,1)S(1)}, bf16[128,256]{1,0:T(8,128)(2,1)S(1)}, u32[]{:S(2)}, u32[]{:S(2)}) %collective-permute-start.10) | collective-permute-done | bytes 65568 | tf_op jit(solution)/shard_map/ppermute | solution.py:655
  64.5 1.1 collective-permute-done.11.grad1
  65.6 2.1 %collective-permute-done.12.grad3 = bf16[128,256]{1,0:T(8,128)(2,1)S(1)} collective-permute-done((bf16[128,256]{1,0:T(8,128)(2,1)S(1)}, bf16[128,256]{1,0:T(8,128)(2,1)S(1)}, u32[]{:S(2)}, u32[]{:S(2)}) %collective-permute-start.12) | collective-permute-done | bytes 65568 | tf_op jit(solution)/shard_map/ppermute | solution.py:655
  67.7 0.7 form_messages.1.refs_0_
  68.4 1.1 weight_terms.1
  69.6 3.4 %collective-permute-start.20 = (bf16[16,192,128]{2,1,0:T(8,128)(2,1)S(1)}, bf16[16,192,128]{2,1,0:T(8,128)(2,1)S(1)}, u32[]{:S(2)}, u32[]{:S(2)}) collective-permute-start(bf16[16,192,128]{2,1,0:T(8,128)(2,1)S(1)} %get-tuple-element.107), channel_id=1, source_target_pairs={{0,4},{4,0},{8,12},{12,8},{16,20},{20,16},{24,28},{28,24},{32,36},... | collective-permute-start | bytes 2359304 | tf_op jit(solution)/shard_map/ppermute | solution.py:633
  72.9 1.0 collective-permute-start.13
  73.9 1.9 %collective-permute-start.14 = (bf16[3,128,256]{2,1,0:T(8,128)(2,1)S(1)}, bf16[3,128,256]{2,1,0:T(8,128)(2,1)S(1)}, u32[]{:S(2)}, u32[]{:S(2)}) collective-permute-start(bf16[3,128,256]{2,1,0:T(8,128)(2,1)S(1)} %form_messages.1.refs_0_), channel_id=1, source_target_pairs={{0,32},{4,12},{8,40},{12,20},{16,48},{20,28},{24,56},{28,4},{32,64... | collective-permute-start | bytes 589832 | tf_op jit(solution)/shard_map/ppermute | solution.py:629
  75.9 0.7 collective-permute-start.15
  76.8 1.3 %collective-permute-start.21 = (bf16[4,192,128]{2,1,0:T(8,128)(2,1)S(1)}, bf16[4,192,128]{2,1,0:T(8,128)(2,1)S(1)}, u32[]{:S(2)}, u32[]{:S(2)}) collective-permute-start(bf16[4,192,128]{2,1,0:T(8,128)(2,1)S(1)} %get-tuple-element.138), channel_id=1, source_target_pairs={{0,16},{4,68},{8,24},{12,76},{16,0},{20,84},{24,8},{28,92},{32,48}... | collective-permute-start | bytes 589832 | tf_op jit(solution)/shard_map/ppermute | solution.py:629
  78.1 0.9 collective-permute-start.22
  79.2 0.3 collective-permute-start.23
  79.5 1.8 %collective-permute-done.14.refs_3_ = bf16[3,128,256]{2,1,0:T(8,128)(2,1)S(1)} collective-permute-done((bf16[3,128,256]{2,1,0:T(8,128)(2,1)S(1)}, bf16[3,128,256]{2,1,0:T(8,128)(2,1)S(1)}, u32[]{:S(2)}, u32[]{:S(2)}) %collective-permute-start.14) | collective-permute-done | bytes 196640 | tf_op jit(solution)/shard_map/ppermute | solution.py:629
  81.4 2.1 %collective-permute-start.16 = (bf16[12,128,256]{2,1,0:T(8,128)(2,1)S(1)}, bf16[12,128,256]{2,1,0:T(8,128)(2,1)S(1)}, u32[]{:S(2)}, u32[]{:S(2)}) collective-permute-start(bf16[12,128,256]{2,1,0:T(8,128)(2,1)S(1)} %join_blocks.1.own0), channel_id=1, source_target_pairs={{0,16},{4,68},{8,24},{12,76},{16,0},{20,84},{24,8},{28,92},{32,48}... | collective-permute-start | bytes 2359304 | tf_op jit(solution)/shard_map/ppermute | solution.py:629
  83.5 0.9 collective-permute-start.17
  84.4 0.6 collective-permute-start.18
  84.9 4.8 %collective-permute-start.19 = (bf16[12,128,256]{2,1,0:T(8,128)(2,1)S(1)}, bf16[12,128,256]{2,1,0:T(8,128)(2,1)}, u32[]{:S(2)}, u32[]{:S(2)}) collective-permute-start(bf16[12,128,256]{2,1,0:T(8,128)(2,1)S(1)} %join_blocks.1.own0), channel_id=1, source_target_pairs={{0,4},{4,0},{8,12},{12,8},{16,20},{20,16},{24,28},{28,24},{32,36},... | collective-permute-start | bytes 2359304 | tf_op jit(solution)/shard_map/ppermute | solution.py:633
  89.9 6.2 %collective-permute-done.23 = bf16[4,192,128]{2,1,0:T(8,128)(2,1)S(1)} collective-permute-done((bf16[4,192,128]{2,1,0:T(8,128)(2,1)S(1)}, bf16[4,192,128]{2,1,0:T(8,128)(2,1)S(1)}, u32[]{:S(2)}, u32[]{:S(2)}) %collective-permute-start.23) | collective-permute-done | bytes 196640 | tf_op jit(solution)/shard_map/ppermute | solution.py:629
  96.2 5.0 %collective-permute-done.24 = bf16[192,128]{1,0:T(8,128)(2,1)S(1)} collective-permute-done((bf16[192,128]{1,0:T(8,128)(2,1)S(1)}, bf16[192,128]{1,0:T(8,128)(2,1)S(1)}, u32[]{:S(2)}, u32[]{:S(2)}) %collective-permute-start.24) | collective-permute-done | bytes 49184 | tf_op jit(solution)/shard_map/ppermute | solution.py:629
  101.2 5.0 %collective-permute-done.25 = bf16[192,128]{1,0:T(8,128)(2,1)S(1)} collective-permute-done((bf16[192,128]{1,0:T(8,128)(2,1)S(1)}, bf16[192,128]{1,0:T(8,128)(2,1)S(1)}, u32[]{:S(2)}, u32[]{:S(2)}) %collective-permute-start.25) | collective-permute-done | bytes 49184 | tf_op jit(solution)/shard_map/ppermute | solution.py:629
  106.2 0.4 collective-permute-start.26
  106.6 2.5 %collective-permute-done.26 = bf16[192,128]{1,0:T(8,128)(2,1)S(1)} collective-permute-done((bf16[192,128]{1,0:T(8,128)(2,1)S(1)}, bf16[192,128]{1,0:T(8,128)(2,1)S(1)}, u32[]{:S(2)}, u32[]{:S(2)}) %collective-permute-start.26) | collective-permute-done | bytes 49184 | tf_op jit(solution)/shard_map/ppermute | solution.py:629
  109.4 0.5 collective-permute-start.28
  110.0 0.7 copy.21
  110.7 6.7 %spread_early.1 = (f32[16,128,256]{2,1,0:T(8,128)S(1)}, bf16[337,128,128]{2,1,0:T(8,128)(2,1)S(1)}) custom-call(s32[432]{0:T(512)S(1)} %get-tuple-element.115.pair_a, s32[432]{0:T(512)S(1)} %get-tuple-element.116.pair_b, s32[432]{0:T(512)S(1)} %get-tuple-element.117.pair_spot, s32[2]{0:T(128)S(1)} %get-tuple-element.118.amounts, s32[1]{0:T(128)S(6)} %copy.24.counts0, ...), custom_call_target="tpu_custom_call" | custom-call | flops 2000000000 | bytes 14000000 | tf_op jit(solution)/shard_map/spread_early/pallas_call | solution.py:419
  117.4 4.3 %spread_late.1 = bf16[16,128,256]{2,1,0:T(8,128)(2,1)} custom-call(s32[432]{0:T(512)S(1)} %get-tuple-element.115.pair_a, s32[432]{0:T(512)S(1)} %get-tuple-element.116.pair_b, s32[432]{0:T(512)S(1)} %get-tuple-element.117.pair_spot, s32[2]{0:T(128)S(1)} %get-tuple-element.118.amounts, bf16[337,128,128]{2,1,0:T(8,128)(2,1)S(1)} %get-tuple-element.123.buffer, ...), custom_call_target="tpu_custom_call" | custom-call | flops 1000000000 | bytes 4000000 | tf_op jit(solution)/shard_map/spread_late/pallas_call | solution.py:452
  (40 shorter events, 1.3 us)
Async XLA Ops:
  11.8 7.1 %collective-permute-start = (bf16[16,384,256]{2,1,0:T(8,128)(2,1)S(1)}, bf16[16,384,256]{2,1,0:T(8,128)(2,1)S(1)}, u32[]{:S(2)}, u32[]{:S(2)}) collective-permute-start(bf16[16,384,256]{2,1,0:T(8,128)(2,1)S(1)} %get-tuple-element.68), channel_id=1, source_target_pairs={{0,4},{4,0},{8,12},{12,8},{16,20},{20,16},{24,28},{28,24},{32,36},... | collective-permute-start | bytes 9437192 | tf_op jit(solution)/shard_map/ppermute | solution.py:633
  20.0 12.5 %collective-permute-start.1 = (bf16[4,384,256]{2,1,0:T(8,128)(2,1)S(1)}, bf16[4,384,256]{2,1,0:T(8,128)(2,1)S(1)}, u32[]{:S(2)}, u32[]{:S(2)}) collective-permute-start(bf16[4,384,256]{2,1,0:T(8,128)(2,1)S(1)} %get-tuple-element.75), channel_id=1, source_target_pairs={{0,64},{4,20},{8,72},{12,28},{16,80},{20,4},{24,88},{28,12},{32,96... | collective-permute-start | bytes 2359304 | tf_op jit(solution)/shard_map/ppermute | solution.py:629
  21.3 19.6 %collective-permute-start.2 = (bf16[4,384,256]{2,1,0:T(8,128)(2,1)S(1)}, bf16[4,384,256]{2,1,0:T(8,128)(2,1)S(1)}, u32[]{:S(2)}, u32[]{:S(2)}) collective-permute-start(bf16[4,384,256]{2,1,0:T(8,128)(2,1)S(1)} %get-tuple-element.76), channel_id=1, source_target_pairs={{0,32},{4,12},{8,40},{12,20},{16,48},{20,28},{24,56},{28,4},{32,64... | collective-permute-start | bytes 2359304 | tf_op jit(solution)/shard_map/ppermute | solution.py:629
  24.8 17.8 %collective-permute-start.3 = (bf16[4,384,256]{2,1,0:T(8,128)(2,1)S(1)}, bf16[4,384,256]{2,1,0:T(8,128)(2,1)S(1)}, u32[]{:S(2)}, u32[]{:S(2)}) collective-permute-start(bf16[4,384,256]{2,1,0:T(8,128)(2,1)S(1)} %get-tuple-element.77), channel_id=1, source_target_pairs={{0,96},{4,28},{8,104},{12,4},{16,112},{20,12},{24,120},{28,20},{32... | collective-permute-start | bytes 2359304 | tf_op jit(solution)/shard_map/ppermute | solution.py:629
  42.7 8.7 %copy-start = (bf16[3,256,1024]{2,1,0:T(8,128)(2,1)S(1)}, bf16[3,256,1024]{2,1,0:T(8,128)(2,1)}, u32[]{:S(2)}) copy-start(bf16[3,256,1024]{2,1,0:T(8,128)(2,1)} %weights.3) | copy-start | bytes 4718596
  43.1 14.4 %copy-start.2 = (bf16[256]{0:T(256)(128)(2,1)S(1)}, bf16[256]{0:T(256)(128)(2,1)}, u32[]{:S(2)}) copy-start(bf16[256]{0:T(256)(128)(2,1)} %param.32) | copy-start | bytes 1540
  43.1 16.0 %copy-start.1 = (bf16[128,256]{1,0:T(8,128)(2,1)S(1)}, bf16[128,256]{1,0:T(8,128)(2,1)}, u32[]{:S(2)}) copy-start(bf16[128,256]{1,0:T(8,128)(2,1)} %param.33) | copy-start | bytes 196612
  43.1 6.2 %collective-permute-start.4 = (bf16[384,256]{1,0:T(8,128)(2,1)S(1)}, bf16[384,256]{1,0:T(8,128)(2,1)S(1)}, u32[]{:S(2)}, u32[]{:S(2)}) collective-permute-start(bf16[384,256]{1,0:T(8,128)(2,1)S(1)} %get-tuple-element.134), channel_id=1, source_target_pairs={{0,16},{4,68},{8,24},{12,76},{16,0},{20,84},{24,8},{28,92},{32,48}... | collective-permute-start | bytes 589832 | tf_op jit(solution)/shard_map/ppermute | solution.py:629
  43.2 6.1 %collective-permute-start.5 = (bf16[384,256]{1,0:T(8,128)(2,1)S(1)}, bf16[384,256]{1,0:T(8,128)(2,1)S(1)}, u32[]{:S(2)}, u32[]{:S(2)}) collective-permute-start(bf16[384,256]{1,0:T(8,128)(2,1)S(1)} %get-tuple-element.133), channel_id=1, source_target_pairs={{0,8},{4,36},{8,16},{12,44},{16,24},{20,52},{24,0},{28,60},{32,40}... | collective-permute-start | bytes 589832 | tf_op jit(solution)/shard_map/ppermute | solution.py:629
  43.3 8.0 %collective-permute-start.6 = (bf16[384,256]{1,0:T(8,128)(2,1)S(1)}, bf16[384,256]{1,0:T(8,128)(2,1)S(1)}, u32[]{:S(2)}, u32[]{:S(2)}) collective-permute-start(bf16[384,256]{1,0:T(8,128)(2,1)S(1)} %get-tuple-element.132), channel_id=1, source_target_pairs={{0,24},{4,100},{8,0},{12,108},{16,8},{20,116},{24,16},{28,124},{32... | collective-permute-start | bytes 589832 | tf_op jit(solution)/shard_map/ppermute | solution.py:629
  51.8 5.7 %collective-permute-start.7 = (bf16[128,256]{1,0:T(8,128)(2,1)S(1)}, bf16[128,256]{1,0:T(8,128)(2,1)S(1)}, u32[]{:S(2)}, u32[]{:S(2)}) collective-permute-start(bf16[128,256]{1,0:T(8,128)(2,1)S(1)} %get-tuple-element.88), channel_id=1, source_target_pairs={{0,2},{1,3},{2,0},{3,1},{4,6},{5,7},{6,4},{7,5},{8,10},{9,11},{10,... | collective-permute-start | bytes 196616 | tf_op jit(solution)/shard_map/ppermute | solution.py:655
  54.8 4.3 %collective-permute-start.8 = (bf16[128,256]{1,0:T(8,128)(2,1)S(1)}, bf16[128,256]{1,0:T(8,128)(2,1)S(1)}, u32[]{:S(2)}, u32[]{:S(2)}) collective-permute-start(bf16[128,256]{1,0:T(8,128)(2,1)S(1)} %get-tuple-element.89), channel_id=1, source_target_pairs={{0,1},{1,2},{2,3},{3,0},{4,5},{5,6},{6,7},{7,4},{8,9},{9,10},{10,1... | collective-permute-start | bytes 196616 | tf_op jit(solution)/shard_map/ppermute | solution.py:655
  55.2 3.9 %collective-permute-start.9 = (bf16[128,256]{1,0:T(8,128)(2,1)S(1)}, bf16[128,256]{1,0:T(8,128)(2,1)S(1)}, u32[]{:S(2)}, u32[]{:S(2)}) collective-permute-start(bf16[128,256]{1,0:T(8,128)(2,1)S(1)} %get-tuple-element.90), channel_id=1, source_target_pairs={{0,3},{1,0},{2,1},{3,2},{4,7},{5,4},{6,5},{7,6},{8,11},{9,8},{10,9... | collective-permute-start | bytes 196616 | tf_op jit(solution)/shard_map/ppermute | solution.py:655
  59.9 4.6 %collective-permute-start.10 = (bf16[128,256]{1,0:T(8,128)(2,1)S(1)}, bf16[128,256]{1,0:T(8,128)(2,1)S(1)}, u32[]{:S(2)}, u32[]{:S(2)}) collective-permute-start(bf16[128,256]{1,0:T(8,128)(2,1)S(1)} %get-tuple-element.101.grad0), channel_id=1, source_target_pairs={{0,2},{1,3},{2,0},{3,1},{4,6},{5,7},{6,4},{7,5},{8,10},{9,11},{10,... | collective-permute-start | bytes 196616 | tf_op jit(solution)/shard_map/ppermute | solution.py:655
  61.6 4.0 %collective-permute-start.11 = (bf16[128,256]{1,0:T(8,128)(2,1)S(1)}, bf16[128,256]{1,0:T(8,128)(2,1)S(1)}, u32[]{:S(2)}, u32[]{:S(2)}) collective-permute-start(bf16[128,256]{1,0:T(8,128)(2,1)S(1)} %get-tuple-element.101.grad0), channel_id=1, source_target_pairs={{0,3},{1,0},{2,1},{3,2},{4,7},{5,4},{6,5},{7,6},{8,11},{9,8},{10,9... | collective-permute-start | bytes 196616 | tf_op jit(solution)/shard_map/ppermute | solution.py:655
  62.7 5.0 %collective-permute-start.12 = (bf16[128,256]{1,0:T(8,128)(2,1)S(1)}, bf16[128,256]{1,0:T(8,128)(2,1)S(1)}, u32[]{:S(2)}, u32[]{:S(2)}) collective-permute-start(bf16[128,256]{1,0:T(8,128)(2,1)S(1)} %get-tuple-element.101.grad0), channel_id=1, source_target_pairs={{0,1},{1,2},{2,3},{3,0},{4,5},{5,6},{6,7},{7,4},{8,9},{9,10},{10,1... | collective-permute-start | bytes 196616 | tf_op jit(solution)/shard_map/ppermute | solution.py:655
  69.6 7.1 %collective-permute-start.20 = (bf16[16,192,128]{2,1,0:T(8,128)(2,1)S(1)}, bf16[16,192,128]{2,1,0:T(8,128)(2,1)S(1)}, u32[]{:S(2)}, u32[]{:S(2)}) collective-permute-start(bf16[16,192,128]{2,1,0:T(8,128)(2,1)S(1)} %get-tuple-element.107), channel_id=1, source_target_pairs={{0,4},{4,0},{8,12},{12,8},{16,20},{20,16},{24,28},{28,24},{32,36},... | collective-permute-start | bytes 2359304 | tf_op jit(solution)/shard_map/ppermute | solution.py:633
  72.9 6.3 %collective-permute-start.13 = (bf16[3,128,256]{2,1,0:T(8,128)(2,1)S(1)}, bf16[3,128,256]{2,1,0:T(8,128)(2,1)S(1)}, u32[]{:S(2)}, u32[]{:S(2)}) collective-permute-start(bf16[3,128,256]{2,1,0:T(8,128)(2,1)S(1)} %form_messages.1.refs_0_), channel_id=1, source_target_pairs={{0,64},{4,20},{8,72},{12,28},{16,80},{20,4},{24,88},{28,12},{32,96... | collective-permute-start | bytes 589832 | tf_op jit(solution)/shard_map/ppermute | solution.py:629
  73.9 7.4 %collective-permute-start.14 = (bf16[3,128,256]{2,1,0:T(8,128)(2,1)S(1)}, bf16[3,128,256]{2,1,0:T(8,128)(2,1)S(1)}, u32[]{:S(2)}, u32[]{:S(2)}) collective-permute-start(bf16[3,128,256]{2,1,0:T(8,128)(2,1)S(1)} %form_messages.1.refs_0_), channel_id=1, source_target_pairs={{0,32},{4,12},{8,40},{12,20},{16,48},{20,28},{24,56},{28,4},{32,64... | collective-permute-start | bytes 589832 | tf_op jit(solution)/shard_map/ppermute | solution.py:629
  75.9 5.5 %collective-permute-start.15 = (bf16[3,128,256]{2,1,0:T(8,128)(2,1)S(1)}, bf16[3,128,256]{2,1,0:T(8,128)(2,1)S(1)}, u32[]{:S(2)}, u32[]{:S(2)}) collective-permute-start(bf16[3,128,256]{2,1,0:T(8,128)(2,1)S(1)} %form_messages.1.refs_0_), channel_id=1, source_target_pairs={{0,96},{4,28},{8,104},{12,4},{16,112},{20,12},{24,120},{28,20},{32... | collective-permute-start | bytes 589832 | tf_op jit(solution)/shard_map/ppermute | solution.py:629
  76.8 7.6 %collective-permute-start.21 = (bf16[4,192,128]{2,1,0:T(8,128)(2,1)S(1)}, bf16[4,192,128]{2,1,0:T(8,128)(2,1)S(1)}, u32[]{:S(2)}, u32[]{:S(2)}) collective-permute-start(bf16[4,192,128]{2,1,0:T(8,128)(2,1)S(1)} %get-tuple-element.138), channel_id=1, source_target_pairs={{0,16},{4,68},{8,24},{12,76},{16,0},{20,84},{24,8},{28,92},{32,48}... | collective-permute-start | bytes 589832 | tf_op jit(solution)/shard_map/ppermute | solution.py:629
  78.1 6.9 %collective-permute-start.22 = (bf16[4,192,128]{2,1,0:T(8,128)(2,1)S(1)}, bf16[4,192,128]{2,1,0:T(8,128)(2,1)S(1)}, u32[]{:S(2)}, u32[]{:S(2)}) collective-permute-start(bf16[4,192,128]{2,1,0:T(8,128)(2,1)S(1)} %get-tuple-element.137), channel_id=1, source_target_pairs={{0,8},{4,36},{8,16},{12,44},{16,24},{20,52},{24,0},{28,60},{32,40}... | collective-permute-start | bytes 589832 | tf_op jit(solution)/shard_map/ppermute | solution.py:629
  79.2 16.8 %collective-permute-start.23 = (bf16[4,192,128]{2,1,0:T(8,128)(2,1)S(1)}, bf16[4,192,128]{2,1,0:T(8,128)(2,1)S(1)}, u32[]{:S(2)}, u32[]{:S(2)}) collective-permute-start(bf16[4,192,128]{2,1,0:T(8,128)(2,1)S(1)} %get-tuple-element.136), channel_id=1, source_target_pairs={{0,24},{4,100},{8,0},{12,108},{16,8},{20,116},{24,16},{28,124},{32... | collective-permute-start | bytes 589832 | tf_op jit(solution)/shard_map/ppermute | solution.py:629
  81.4 27.9 %collective-permute-start.16 = (bf16[12,128,256]{2,1,0:T(8,128)(2,1)S(1)}, bf16[12,128,256]{2,1,0:T(8,128)(2,1)S(1)}, u32[]{:S(2)}, u32[]{:S(2)}) collective-permute-start(bf16[12,128,256]{2,1,0:T(8,128)(2,1)S(1)} %join_blocks.1.own0), channel_id=1, source_target_pairs={{0,16},{4,68},{8,24},{12,76},{16,0},{20,84},{24,8},{28,92},{32,48}... | collective-permute-start | bytes 2359304 | tf_op jit(solution)/shard_map/ppermute | solution.py:629
  83.5 25.8 %collective-permute-start.17 = (bf16[12,128,256]{2,1,0:T(8,128)(2,1)S(1)}, bf16[12,128,256]{2,1,0:T(8,128)(2,1)S(1)}, u32[]{:S(2)}, u32[]{:S(2)}) collective-permute-start(bf16[12,128,256]{2,1,0:T(8,128)(2,1)S(1)} %join_blocks.1.own0), channel_id=1, source_target_pairs={{0,8},{4,36},{8,16},{12,44},{16,24},{20,52},{24,0},{28,60},{32,40}... | collective-permute-start | bytes 2359304 | tf_op jit(solution)/shard_map/ppermute | solution.py:629
  84.4 25.0 %collective-permute-start.18 = (bf16[12,128,256]{2,1,0:T(8,128)(2,1)S(1)}, bf16[12,128,256]{2,1,0:T(8,128)(2,1)S(1)}, u32[]{:S(2)}, u32[]{:S(2)}) collective-permute-start(bf16[12,128,256]{2,1,0:T(8,128)(2,1)S(1)} %join_blocks.1.own0), channel_id=1, source_target_pairs={{0,24},{4,100},{8,0},{12,108},{16,8},{20,116},{24,16},{28,124},{32... | collective-permute-start | bytes 2359304 | tf_op jit(solution)/shard_map/ppermute | solution.py:629
  84.9 24.4 %collective-permute-start.19 = (bf16[12,128,256]{2,1,0:T(8,128)(2,1)S(1)}, bf16[12,128,256]{2,1,0:T(8,128)(2,1)}, u32[]{:S(2)}, u32[]{:S(2)}) collective-permute-start(bf16[12,128,256]{2,1,0:T(8,128)(2,1)S(1)} %join_blocks.1.own0), channel_id=1, source_target_pairs={{0,4},{4,0},{8,12},{12,8},{16,20},{20,16},{24,28},{28,24},{32,36},... | collective-permute-start | bytes 2359304 | tf_op jit(solution)/shard_map/ppermute | solution.py:633
  96.1 5.0 %collective-permute-start.24 = (bf16[192,128]{1,0:T(8,128)(2,1)S(1)}, bf16[192,128]{1,0:T(8,128)(2,1)S(1)}, u32[]{:S(2)}, u32[]{:S(2)}) collective-permute-start(bf16[192,128]{1,0:T(8,128)(2,1)S(1)} %get-tuple-element.141), channel_id=1, source_target_pairs={{0,64},{4,20},{8,72},{12,28},{16,80},{20,4},{24,88},{28,12},{32,96... | collective-permute-start | bytes 147464 | tf_op jit(solution)/shard_map/ppermute | solution.py:629
  101.2 5.0 %collective-permute-start.25 = (bf16[192,128]{1,0:T(8,128)(2,1)S(1)}, bf16[192,128]{1,0:T(8,128)(2,1)S(1)}, u32[]{:S(2)}, u32[]{:S(2)}) collective-permute-start(bf16[192,128]{1,0:T(8,128)(2,1)S(1)} %get-tuple-element.140), channel_id=1, source_target_pairs={{0,32},{4,12},{8,40},{12,20},{16,48},{20,28},{24,56},{28,4},{32,64... | collective-permute-start | bytes 147464 | tf_op jit(solution)/shard_map/ppermute | solution.py:629
  106.2 2.9 %collective-permute-start.26 = (bf16[192,128]{1,0:T(8,128)(2,1)S(1)}, bf16[192,128]{1,0:T(8,128)(2,1)S(1)}, u32[]{:S(2)}, u32[]{:S(2)}) collective-permute-start(bf16[192,128]{1,0:T(8,128)(2,1)S(1)} %get-tuple-element.139), channel_id=1, source_target_pairs={{0,96},{4,28},{8,104},{12,4},{16,112},{20,12},{24,120},{28,20},{32... | collective-permute-start | bytes 147464 | tf_op jit(solution)/shard_map/ppermute | solution.py:629
  109.3 8.0 %collective-permute-start.27 = (bf16[12,128,256]{2,1,0:T(8,128)(2,1)S(1)}, bf16[12,128,256]{2,1,0:T(8,128)(2,1)S(1)}, u32[]{:S(2)}, u32[]{:S(2)}) collective-permute-start(bf16[12,128,256]{2,1,0:T(8,128)(2,1)S(1)} %collective-permute-done.16.own2), channel_id=1, source_target_pairs={{0,4},{4,0},{8,12},{12,8},{16,20},{20,16},{24,28},{28,24},{32,36},... | collective-permute-start | bytes 2359304 | tf_op jit(solution)/shard_map/ppermute | solution.py:633
  109.4 8.0 %collective-permute-start.28 = (bf16[12,128,256]{2,1,0:T(8,128)(2,1)S(1)}, bf16[12,128,256]{2,1,0:T(8,128)(2,1)S(1)}, u32[]{:S(2)}, u32[]{:S(2)}) collective-permute-start(bf16[12,128,256]{2,1,0:T(8,128)(2,1)S(1)} %collective-permute-done.17.own3), channel_id=1, source_target_pairs={{0,4},{4,0},{8,12},{12,8},{16,20},{20,16},{24,28},{28,24},{32,36},... | collective-permute-start | bytes 2359304 | tf_op jit(solution)/shard_map/ppermute | solution.py:633
  109.9 7.5 %collective-permute-start.29 = (bf16[12,128,256]{2,1,0:T(8,128)(2,1)S(1)}, bf16[12,128,256]{2,1,0:T(8,128)(2,1)S(1)}, u32[]{:S(2)}, u32[]{:S(2)}) collective-permute-start(bf16[12,128,256]{2,1,0:T(8,128)(2,1)S(1)} %collective-permute-done.18.own1), channel_id=1, source_target_pairs={{0,4},{4,0},{8,12},{12,8},{16,20},{20,16},{24,28},{28,24},{32,36},... | collective-permute-start | bytes 2359304 | tf_op jit(solution)/shard_map/ppermute | solution.py:633

commit v6 on v5

--- a/solution.py
+++ b/solution.py
@@ -11,6 +11,7 @@
 TILE = 128
 SIDE = 4
 GROUP = 16
+BATCH = 32
 PAIRS = 16
 BF16 = jnp.bfloat16
 F32 = jnp.float32
@@ -83,8 +84,8 @@
 
 def gather_list(codes, amount, features, buffer, total, ready):
     def add_group(group, waited):
-        waited = ready(waited, codes[jnp.minimum(group * GROUP + GROUP, amount) - 1] & 1023)
-        marks = [codes[group * GROUP + lane] for lane in range(GROUP)]
+        waited = ready(waited, codes[jnp.minimum(group * BATCH + BATCH, amount) - 1] & 1023)
+        marks = [codes[group * BATCH + lane] for lane in range(BATCH)]
         products = [
             jnp.dot(
                 buffer[mark & 1023], features[(mark >> 10) & 15], preferred_element_type=F32
@@ -95,7 +96,7 @@
             total[mark >> 14] += product
         return waited
 
-    return lax.fori_loop(0, (amount + GROUP - 1) // GROUP, add_group, jnp.int32(0))
+    return lax.fori_loop(0, (amount + BATCH - 1) // BATCH, add_group, jnp.int32(0))
 
 
 def emit_blocks(total, target):
@@ -152,7 +153,7 @@
         sent, kept = lax.fori_loop(
             0, (counts[number][0] + GROUP - 1) // GROUP, sort, (sent, kept)
         )
-    for lane in range(GROUP):
+    for lane in range(BATCH):
         send_codes[sent + lane] = 48 * 16384
         keep_codes[kept + lane] = 48 * 16384
     keep_amount[0] = kept
@@ -205,7 +206,7 @@
         gather_send_kernel,
         out_shape=(
             blocks,
-            jax.ShapeDtypeStruct((slots + GROUP,), jnp.int32),
+            jax.ShapeDtypeStruct((slots + BATCH,), jnp.int32),
             jax.ShapeDtypeStruct((1,), jnp.int32),
             jax.ShapeDtypeStruct((slots, TILE, TILE), BF16),
             jax.ShapeDtypeStruct(features.shape, BF16),
@@ -215,7 +216,7 @@
         scratch_shapes=[
             total,
             pltpu.SMEM((32,), jnp.int32),
-            pltpu.SMEM((slots + GROUP,), jnp.int32),
+            pltpu.SMEM((slots + BATCH,), jnp.int32),
             pltpu.SemaphoreType.DMA((slots // GROUP,)),
             pltpu.SemaphoreType.DMA(()),
         ],

time: 122 us -> 121 us (level)
  no operation moved by 1% of the time
where the time goes in v6:
time: 121 us
  waiting for transfers between devices  46.1 us (38%)
  Pallas kernels  34.5 us (29%)
  starting transfers between devices  34 us (28%)
  between operations  2.81 us (2%)
  other arithmetic  2.49 us (2%)
    ppermute x18, waiting for transfers between devices, shift(): return lax.ppermute(value, 'src', shift_pairs(step, second))  39.6 us
    ppermute x18, starting transfers between devices, shift(): return lax.ppermute(value, 'src', shift_pairs(step, second))  16.2 us
    pallas_call x1, Pallas kernels, gather_sums(): pl.pallas_call(gather_send_kernel, out_shape=(blocks, jax.ShapeDtypeStruc...  8.99 us
    ppermute x6, starting transfers between devices, turn(): lax.ppermute(value, 'tgt', [(t, (t + step) % SIDE) for t in range(SIDE)])  8.96 us
    ppermute x6, starting transfers between devices, swap(): return lax.ppermute(value, 'src', [(s, s ^ 1) for s in range(32)])  8.83 us
    pallas_call x1, Pallas kernels, spread_early(): pl.pallas_call(spread_early_kernel, out_shape=(jax.ShapeDtypeStruct((16,...  6.68 us
    pallas_call x1, Pallas kernels, gather_sums(): pl.pallas_call(gather_keep_kernel, out_shape=blocks, in_specs=[spec(SMEM)...  6.66 us
    ppermute x6, waiting for transfers between devices, turn(): lax.ppermute(value, 'tgt', [(t, (t + step) % SIDE) for t in range(SIDE)])  6.5 us
  transfers between devices with their start and end apart: 30, of which 15 were waited for; matrix products, arithmetic and copies ran while one was open for 1% of the time, Pallas kernels for 16%

profile of v6, /device:TPU:7, one launch (start us, length us, event | category | flops | bytes accessed | tf_op | source)
XLA Modules:
  0.0 120.7 jit_solution(10234218243044719232)
XLA Ops:
  2.6 9.0 %gather_send.1 = (bf16[16,384,256]{2,1,0:T(8,128)(2,1)S(1)}, s32[368]{0:T(512)S(1)}, s32[1]{0:T(128)}, bf16[336,128,128]{2,1,0:T(8,128)(2,1)S(1)}, bf16[16,128,256]{2,1,0:T(8,128)(2,1)S(1)}) custom-call(s32[32]{0:T(128)} %owner_map.2, s32[192]{0:T(256)} %targets0.3, s32[96]{0:T(128)} %targets1.3, s32[48]{0:T(128)} %targets2.3, s32[192]{0:T(256)} %sources0.3, ...), custom_call_target="tpu_custom_call" | custom-call | flops 2000000000 | bytes 12000000 | tf_op jit(solution)/shard_map/gather_send/pallas_call | solution.py:205
  11.7 6.7 %gather_keep.1 = bf16[16,384,256]{2,1,0:T(8,128)(2,1)S(1)} custom-call(s32[368]{0:T(512)S(1)} %get-tuple-element.64.codes, s32[1]{0:T(128)} %get-tuple-element.65.amount, bf16[336,128,128]{2,1,0:T(8,128)(2,1)S(1)} %get-tuple-element.66.buffer, bf16[16,128,256]{2,1,0:T(8,128)(2,1)S(1)} %get-tuple-element.67.held), custom_call_target="tpu_custom_call" | custom-call | flops 2000000000 | bytes 12000000 | tf_op jit(solution)/shard_map/gather_keep/pallas_call | solution.py:226
  18.3 1.0 add_convert_fusion
  19.4 1.3 %collective-permute-start.1 = (bf16[4,384,256]{2,1,0:T(8,128)(2,1)S(1)}, bf16[4,384,256]{2,1,0:T(8,128)(2,1)S(1)}, u32[]{:S(2)}, u32[]{:S(2)}) collective-permute-start(bf16[4,384,256]{2,1,0:T(8,128)(2,1)S(1)} %get-tuple-element.75), channel_id=1, source_target_pairs={{0,64},{4,20},{8,72},{12,28},{16,80},{20,4},{24,88},{28,12},{32,96... | collective-permute-start | bytes 2359304 | tf_op jit(solution)/shard_map/ppermute | solution.py:630
  20.7 3.1 %collective-permute-start.2 = (bf16[4,384,256]{2,1,0:T(8,128)(2,1)S(1)}, bf16[4,384,256]{2,1,0:T(8,128)(2,1)S(1)}, u32[]{:S(2)}, u32[]{:S(2)}) collective-permute-start(bf16[4,384,256]{2,1,0:T(8,128)(2,1)S(1)} %get-tuple-element.76), channel_id=1, source_target_pairs={{0,32},{4,12},{8,40},{12,20},{16,48},{20,28},{24,56},{28,4},{32,64... | collective-permute-start | bytes 2359304 | tf_op jit(solution)/shard_map/ppermute | solution.py:630
  23.8 5.6 %plan_spread.1 = (s32[432]{0:T(512)S(1)}, s32[432]{0:T(512)S(1)}, s32[432]{0:T(512)S(1)}, s32[2]{0:T(128)S(1)}) custom-call(s32[32]{0:T(128)} %owner_map.2, s32[192]{0:T(256)} %targets0.3, s32[96]{0:T(128)} %targets1.3, s32[48]{0:T(128)} %targets2.3, s32[192]{0:T(256)} %sources0.3, s32[96]{0:T(128)} %sources1.3, s32[48]{0:T(128)} %sources2.3, ...), custom_call_target="tpu_custom_call" | custom-call | flops 1000000000 | bytes 1000000 | tf_op jit(solution)/shard_map/plan_spread/pallas_call | solution.py:312
  29.4 2.5 %collective-permute-done.1 = bf16[4,384,256]{2,1,0:T(8,128)(2,1)S(1)} collective-permute-done((bf16[4,384,256]{2,1,0:T(8,128)(2,1)S(1)}, bf16[4,384,256]{2,1,0:T(8,128)(2,1)S(1)}, u32[]{:S(2)}, u32[]{:S(2)}) %collective-permute-start.1) | collective-permute-done | bytes 786464 | tf_op jit(solution)/shard_map/ppermute | solution.py:630
  31.9 8.3 %collective-permute-done.2 = bf16[4,384,256]{2,1,0:T(8,128)(2,1)S(1)} collective-permute-done((bf16[4,384,256]{2,1,0:T(8,128)(2,1)S(1)}, bf16[4,384,256]{2,1,0:T(8,128)(2,1)S(1)}, u32[]{:S(2)}, u32[]{:S(2)}) %collective-permute-start.2) | collective-permute-done | bytes 786464 | tf_op jit(solution)/shard_map/ppermute | solution.py:630
  40.2 1.4 %collective-permute-done.3 = bf16[4,384,256]{2,1,0:T(8,128)(2,1)S(1)} collective-permute-done((bf16[4,384,256]{2,1,0:T(8,128)(2,1)S(1)}, bf16[4,384,256]{2,1,0:T(8,128)(2,1)S(1)}, u32[]{:S(2)}, u32[]{:S(2)}) %collective-permute-start.3) | collective-permute-done | bytes 786464 | tf_op jit(solution)/shard_map/ppermute | solution.py:630
  41.6 0.4 fusion.3
  42.3 0.5 collective-permute-start.5
  42.8 1.0 collective-permute-start.6
  43.8 4.5 %collective-permute-done.4.part1 = bf16[384,256]{1,0:T(8,128)(2,1)S(1)} collective-permute-done((bf16[384,256]{1,0:T(8,128)(2,1)S(1)}, bf16[384,256]{1,0:T(8,128)(2,1)S(1)}, u32[]{:S(2)}, u32[]{:S(2)}) %collective-permute-start.4) | collective-permute-done | bytes 196640 | tf_op jit(solution)/shard_map/ppermute | solution.py:630
  48.3 2.0 %collective-permute-done.6.part3 = bf16[384,256]{1,0:T(8,128)(2,1)S(1)} collective-permute-done((bf16[384,256]{1,0:T(8,128)(2,1)S(1)}, bf16[384,256]{1,0:T(8,128)(2,1)S(1)}, u32[]{:S(2)}, u32[]{:S(2)}) %collective-permute-start.6) | collective-permute-done | bytes 196640 | tf_op jit(solution)/shard_map/ppermute | solution.py:630
  50.3 0.4 hidden_terms.1
  50.7 3.0 %collective-permute-start.7 = (bf16[128,256]{1,0:T(8,128)(2,1)S(1)}, bf16[128,256]{1,0:T(8,128)(2,1)S(1)}, u32[]{:S(2)}, u32[]{:S(2)}) collective-permute-start(bf16[128,256]{1,0:T(8,128)(2,1)S(1)} %get-tuple-element.88), channel_id=1, source_target_pairs={{0,2},{1,3},{2,0},{3,1},{4,6},{5,7},{6,4},{7,5},{8,10},{9,11},{10,... | collective-permute-start | bytes 196616 | tf_op jit(solution)/shard_map/ppermute | solution.py:656
  53.7 0.4 collective-permute-start.8
  54.1 2.3 %collective-permute-start.9 = (bf16[128,256]{1,0:T(8,128)(2,1)S(1)}, bf16[128,256]{1,0:T(8,128)(2,1)S(1)}, u32[]{:S(2)}, u32[]{:S(2)}) collective-permute-start(bf16[128,256]{1,0:T(8,128)(2,1)S(1)} %get-tuple-element.90), channel_id=1, source_target_pairs={{0,3},{1,0},{2,1},{3,2},{4,7},{5,4},{6,5},{7,6},{8,11},{9,8},{10,9... | collective-permute-start | bytes 196616 | tf_op jit(solution)/shard_map/ppermute | solution.py:656
  56.4 1.9 %collective-permute-done.8 = bf16[128,256]{1,0:T(8,128)(2,1)S(1)} collective-permute-done((bf16[128,256]{1,0:T(8,128)(2,1)S(1)}, bf16[128,256]{1,0:T(8,128)(2,1)S(1)}, u32[]{:S(2)}, u32[]{:S(2)}) %collective-permute-start.8) | collective-permute-done | bytes 65568 | tf_op jit(solution)/shard_map/ppermute | solution.py:656
  58.3 0.8 fusion.6
  59.1 1.8 %collective-permute-start.10 = (bf16[128,256]{1,0:T(8,128)(2,1)S(1)}, bf16[128,256]{1,0:T(8,128)(2,1)S(1)}, u32[]{:S(2)}, u32[]{:S(2)}) collective-permute-start(bf16[128,256]{1,0:T(8,128)(2,1)S(1)} %get-tuple-element.101.grad0), channel_id=1, source_target_pairs={{0,2},{1,3},{2,0},{3,1},{4,6},{5,7},{6,4},{7,5},{8,10},{9,11},{10,... | collective-permute-start | bytes 196616 | tf_op jit(solution)/shard_map/ppermute | solution.py:656
  60.9 0.9 collective-permute-start.11
  61.8 0.6 collective-permute-start.12
  62.4 1.3 %collective-permute-done.10.grad2 = bf16[128,256]{1,0:T(8,128)(2,1)S(1)} collective-permute-done((bf16[128,256]{1,0:T(8,128)(2,1)S(1)}, bf16[128,256]{1,0:T(8,128)(2,1)S(1)}, u32[]{:S(2)}, u32[]{:S(2)}) %collective-permute-start.10) | collective-permute-done | bytes 65568 | tf_op jit(solution)/shard_map/ppermute | solution.py:656
  63.7 1.0 collective-permute-done.11.grad1
  64.7 2.2 %collective-permute-done.12.grad3 = bf16[128,256]{1,0:T(8,128)(2,1)S(1)} collective-permute-done((bf16[128,256]{1,0:T(8,128)(2,1)S(1)}, bf16[128,256]{1,0:T(8,128)(2,1)S(1)}, u32[]{:S(2)}, u32[]{:S(2)}) %collective-permute-start.12) | collective-permute-done | bytes 65568 | tf_op jit(solution)/shard_map/ppermute | solution.py:656
  67.0 0.6 form_messages.1.refs_0_
  67.6 1.1 weight_terms.1
  68.8 3.4 %collective-permute-start.20 = (bf16[16,192,128]{2,1,0:T(8,128)(2,1)S(1)}, bf16[16,192,128]{2,1,0:T(8,128)(2,1)S(1)}, u32[]{:S(2)}, u32[]{:S(2)}) collective-permute-start(bf16[16,192,128]{2,1,0:T(8,128)(2,1)S(1)} %get-tuple-element.107), channel_id=1, source_target_pairs={{0,4},{4,0},{8,12},{12,8},{16,20},{20,16},{24,28},{28,24},{32,36},... | collective-permute-start | bytes 2359304 | tf_op jit(solution)/shard_map/ppermute | solution.py:634
  72.2 1.2 collective-permute-start.13
  73.4 1.8 %collective-permute-start.14 = (bf16[3,128,256]{2,1,0:T(8,128)(2,1)S(1)}, bf16[3,128,256]{2,1,0:T(8,128)(2,1)S(1)}, u32[]{:S(2)}, u32[]{:S(2)}) collective-permute-start(bf16[3,128,256]{2,1,0:T(8,128)(2,1)S(1)} %form_messages.1.refs_0_), channel_id=1, source_target_pairs={{0,32},{4,12},{8,40},{12,20},{16,48},{20,28},{24,56},{28,4},{32,64... | collective-permute-start | bytes 589832 | tf_op jit(solution)/shard_map/ppermute | solution.py:630
  75.2 0.9 collective-permute-start.15
  76.2 1.1 collective-permute-start.21
  77.3 0.9 collective-permute-start.22
  78.8 1.8 %collective-permute-done.14.refs_3_ = bf16[3,128,256]{2,1,0:T(8,128)(2,1)S(1)} collective-permute-done((bf16[3,128,256]{2,1,0:T(8,128)(2,1)S(1)}, bf16[3,128,256]{2,1,0:T(8,128)(2,1)S(1)}, u32[]{:S(2)}, u32[]{:S(2)}) %collective-permute-start.14) | collective-permute-done | bytes 196640 | tf_op jit(solution)/shard_map/ppermute | solution.py:630
  80.7 1.8 %collective-permute-start.16 = (bf16[12,128,256]{2,1,0:T(8,128)(2,1)S(1)}, bf16[12,128,256]{2,1,0:T(8,128)(2,1)S(1)}, u32[]{:S(2)}, u32[]{:S(2)}) collective-permute-start(bf16[12,128,256]{2,1,0:T(8,128)(2,1)S(1)} %join_blocks.1.own0), channel_id=1, source_target_pairs={{0,16},{4,68},{8,24},{12,76},{16,0},{20,84},{24,8},{28,92},{32,48}... | collective-permute-start | bytes 2359304 | tf_op jit(solution)/shard_map/ppermute | solution.py:630
  82.5 0.9 collective-permute-start.17
  83.4 0.5 collective-permute-start.18
  83.9 4.7 %collective-permute-start.19 = (bf16[12,128,256]{2,1,0:T(8,128)(2,1)S(1)}, bf16[12,128,256]{2,1,0:T(8,128)(2,1)}, u32[]{:S(2)}, u32[]{:S(2)}) collective-permute-start(bf16[12,128,256]{2,1,0:T(8,128)(2,1)S(1)} %join_blocks.1.own0), channel_id=1, source_target_pairs={{0,4},{4,0},{8,12},{12,8},{16,20},{20,16},{24,28},{28,24},{32,36},... | collective-permute-start | bytes 2359304 | tf_op jit(solution)/shard_map/ppermute | solution.py:634
  88.7 6.4 %collective-permute-done.23 = bf16[4,192,128]{2,1,0:T(8,128)(2,1)S(1)} collective-permute-done((bf16[4,192,128]{2,1,0:T(8,128)(2,1)S(1)}, bf16[4,192,128]{2,1,0:T(8,128)(2,1)S(1)}, u32[]{:S(2)}, u32[]{:S(2)}) %collective-permute-start.23) | collective-permute-done | bytes 196640 | tf_op jit(solution)/shard_map/ppermute | solution.py:630
  95.3 5.0 %collective-permute-done.24 = bf16[192,128]{1,0:T(8,128)(2,1)S(1)} collective-permute-done((bf16[192,128]{1,0:T(8,128)(2,1)S(1)}, bf16[192,128]{1,0:T(8,128)(2,1)S(1)}, u32[]{:S(2)}, u32[]{:S(2)}) %collective-permute-start.24) | collective-permute-done | bytes 49184 | tf_op jit(solution)/shard_map/ppermute | solution.py:630
  100.3 5.0 %collective-permute-done.25 = bf16[192,128]{1,0:T(8,128)(2,1)S(1)} collective-permute-done((bf16[192,128]{1,0:T(8,128)(2,1)S(1)}, bf16[192,128]{1,0:T(8,128)(2,1)S(1)}, u32[]{:S(2)}, u32[]{:S(2)}) %collective-permute-start.25) | collective-permute-done | bytes 49184 | tf_op jit(solution)/shard_map/ppermute | solution.py:630
  105.2 0.6 collective-permute-start.26
  105.9 2.3 %collective-permute-done.26 = bf16[192,128]{1,0:T(8,128)(2,1)S(1)} collective-permute-done((bf16[192,128]{1,0:T(8,128)(2,1)S(1)}, bf16[192,128]{1,0:T(8,128)(2,1)S(1)}, u32[]{:S(2)}, u32[]{:S(2)}) %collective-permute-start.26) | collective-permute-done | bytes 49184 | tf_op jit(solution)/shard_map/ppermute | solution.py:630
  108.5 0.5 collective-permute-start.28
  109.1 0.7 copy.21
  109.7 6.7 %spread_early.1 = (f32[16,128,256]{2,1,0:T(8,128)S(1)}, bf16[337,128,128]{2,1,0:T(8,128)(2,1)S(1)}) custom-call(s32[432]{0:T(512)S(1)} %get-tuple-element.115.pair_a, s32[432]{0:T(512)S(1)} %get-tuple-element.116.pair_b, s32[432]{0:T(512)S(1)} %get-tuple-element.117.pair_spot, s32[2]{0:T(128)S(1)} %get-tuple-element.118.amounts, s32[1]{0:T(128)S(6)} %copy.24.counts0, ...), custom_call_target="tpu_custom_call" | custom-call | flops 2000000000 | bytes 14000000 | tf_op jit(solution)/shard_map/spread_early/pallas_call | solution.py:420
  116.5 4.3 %spread_late.1 = bf16[16,128,256]{2,1,0:T(8,128)(2,1)} custom-call(s32[432]{0:T(512)S(1)} %get-tuple-element.115.pair_a, s32[432]{0:T(512)S(1)} %get-tuple-element.116.pair_b, s32[432]{0:T(512)S(1)} %get-tuple-element.117.pair_spot, s32[2]{0:T(128)S(1)} %get-tuple-element.118.amounts, bf16[337,128,128]{2,1,0:T(8,128)(2,1)S(1)} %get-tuple-element.123.buffer, ...), custom_call_target="tpu_custom_call" | custom-call | flops 1000000000 | bytes 4000000 | tf_op jit(solution)/shard_map/spread_late/pallas_call | solution.py:453
  (40 shorter events, 1.7 us)
Async XLA Ops:
  11.6 6.8 %collective-permute-start = (bf16[16,384,256]{2,1,0:T(8,128)(2,1)S(1)}, bf16[16,384,256]{2,1,0:T(8,128)(2,1)S(1)}, u32[]{:S(2)}, u32[]{:S(2)}) collective-permute-start(bf16[16,384,256]{2,1,0:T(8,128)(2,1)S(1)} %get-tuple-element.68), channel_id=1, source_target_pairs={{0,4},{4,0},{8,12},{12,8},{16,20},{20,16},{24,28},{28,24},{32,36},... | collective-permute-start | bytes 9437192 | tf_op jit(solution)/shard_map/ppermute | solution.py:634
  19.4 12.5 %collective-permute-start.1 = (bf16[4,384,256]{2,1,0:T(8,128)(2,1)S(1)}, bf16[4,384,256]{2,1,0:T(8,128)(2,1)S(1)}, u32[]{:S(2)}, u32[]{:S(2)}) collective-permute-start(bf16[4,384,256]{2,1,0:T(8,128)(2,1)S(1)} %get-tuple-element.75), channel_id=1, source_target_pairs={{0,64},{4,20},{8,72},{12,28},{16,80},{20,4},{24,88},{28,12},{32,96... | collective-permute-start | bytes 2359304 | tf_op jit(solution)/shard_map/ppermute | solution.py:630
  20.7 19.5 %collective-permute-start.2 = (bf16[4,384,256]{2,1,0:T(8,128)(2,1)S(1)}, bf16[4,384,256]{2,1,0:T(8,128)(2,1)S(1)}, u32[]{:S(2)}, u32[]{:S(2)}) collective-permute-start(bf16[4,384,256]{2,1,0:T(8,128)(2,1)S(1)} %get-tuple-element.76), channel_id=1, source_target_pairs={{0,32},{4,12},{8,40},{12,20},{16,48},{20,28},{24,56},{28,4},{32,64... | collective-permute-start | bytes 2359304 | tf_op jit(solution)/shard_map/ppermute | solution.py:630
  23.8 17.8 %collective-permute-start.3 = (bf16[4,384,256]{2,1,0:T(8,128)(2,1)S(1)}, bf16[4,384,256]{2,1,0:T(8,128)(2,1)S(1)}, u32[]{:S(2)}, u32[]{:S(2)}) collective-permute-start(bf16[4,384,256]{2,1,0:T(8,128)(2,1)S(1)} %get-tuple-element.77), channel_id=1, source_target_pairs={{0,96},{4,28},{8,104},{12,4},{16,112},{20,12},{24,120},{28,20},{32... | collective-permute-start | bytes 2359304 | tf_op jit(solution)/shard_map/ppermute | solution.py:630
  41.6 8.7 %copy-start = (bf16[3,256,1024]{2,1,0:T(8,128)(2,1)S(1)}, bf16[3,256,1024]{2,1,0:T(8,128)(2,1)}, u32[]{:S(2)}) copy-start(bf16[3,256,1024]{2,1,0:T(8,128)(2,1)} %weights.3) | copy-start | bytes 4718596
  42.0 14.4 %copy-start.2 = (bf16[256]{0:T(256)(128)(2,1)S(1)}, bf16[256]{0:T(256)(128)(2,1)}, u32[]{:S(2)}) copy-start(bf16[256]{0:T(256)(128)(2,1)} %param.32) | copy-start | bytes 1540
  42.1 16.3 %copy-start.1 = (bf16[128,256]{1,0:T(8,128)(2,1)S(1)}, bf16[128,256]{1,0:T(8,128)(2,1)}, u32[]{:S(2)}) copy-start(bf16[128,256]{1,0:T(8,128)(2,1)} %param.33) | copy-start | bytes 196612
  42.1 6.2 %collective-permute-start.4 = (bf16[384,256]{1,0:T(8,128)(2,1)S(1)}, bf16[384,256]{1,0:T(8,128)(2,1)S(1)}, u32[]{:S(2)}, u32[]{:S(2)}) collective-permute-start(bf16[384,256]{1,0:T(8,128)(2,1)S(1)} %get-tuple-element.134), channel_id=1, source_target_pairs={{0,16},{4,68},{8,24},{12,76},{16,0},{20,84},{24,8},{28,92},{32,48}... | collective-permute-start | bytes 589832 | tf_op jit(solution)/shard_map/ppermute | solution.py:630
  42.3 6.0 %collective-permute-start.5 = (bf16[384,256]{1,0:T(8,128)(2,1)S(1)}, bf16[384,256]{1,0:T(8,128)(2,1)S(1)}, u32[]{:S(2)}, u32[]{:S(2)}) collective-permute-start(bf16[384,256]{1,0:T(8,128)(2,1)S(1)} %get-tuple-element.133), channel_id=1, source_target_pairs={{0,8},{4,36},{8,16},{12,44},{16,24},{20,52},{24,0},{28,60},{32,40}... | collective-permute-start | bytes 589832 | tf_op jit(solution)/shard_map/ppermute | solution.py:630
  42.8 7.5 %collective-permute-start.6 = (bf16[384,256]{1,0:T(8,128)(2,1)S(1)}, bf16[384,256]{1,0:T(8,128)(2,1)S(1)}, u32[]{:S(2)}, u32[]{:S(2)}) collective-permute-start(bf16[384,256]{1,0:T(8,128)(2,1)S(1)} %get-tuple-element.132), channel_id=1, source_target_pairs={{0,24},{4,100},{8,0},{12,108},{16,8},{20,116},{24,16},{28,124},{32... | collective-permute-start | bytes 589832 | tf_op jit(solution)/shard_map/ppermute | solution.py:630
  50.7 5.7 %collective-permute-start.7 = (bf16[128,256]{1,0:T(8,128)(2,1)S(1)}, bf16[128,256]{1,0:T(8,128)(2,1)S(1)}, u32[]{:S(2)}, u32[]{:S(2)}) collective-permute-start(bf16[128,256]{1,0:T(8,128)(2,1)S(1)} %get-tuple-element.88), channel_id=1, source_target_pairs={{0,2},{1,3},{2,0},{3,1},{4,6},{5,7},{6,4},{7,5},{8,10},{9,11},{10,... | collective-permute-start | bytes 196616 | tf_op jit(solution)/shard_map/ppermute | solution.py:656
  53.7 4.6 %collective-permute-start.8 = (bf16[128,256]{1,0:T(8,128)(2,1)S(1)}, bf16[128,256]{1,0:T(8,128)(2,1)S(1)}, u32[]{:S(2)}, u32[]{:S(2)}) collective-permute-start(bf16[128,256]{1,0:T(8,128)(2,1)S(1)} %get-tuple-element.89), channel_id=1, source_target_pairs={{0,1},{1,2},{2,3},{3,0},{4,5},{5,6},{6,7},{7,4},{8,9},{9,10},{10,1... | collective-permute-start | bytes 196616 | tf_op jit(solution)/shard_map/ppermute | solution.py:656
  54.1 4.2 %collective-permute-start.9 = (bf16[128,256]{1,0:T(8,128)(2,1)S(1)}, bf16[128,256]{1,0:T(8,128)(2,1)S(1)}, u32[]{:S(2)}, u32[]{:S(2)}) collective-permute-start(bf16[128,256]{1,0:T(8,128)(2,1)S(1)} %get-tuple-element.90), channel_id=1, source_target_pairs={{0,3},{1,0},{2,1},{3,2},{4,7},{5,4},{6,5},{7,6},{8,11},{9,8},{10,9... | collective-permute-start | bytes 196616 | tf_op jit(solution)/shard_map/ppermute | solution.py:656
  59.1 4.6 %collective-permute-start.10 = (bf16[128,256]{1,0:T(8,128)(2,1)S(1)}, bf16[128,256]{1,0:T(8,128)(2,1)S(1)}, u32[]{:S(2)}, u32[]{:S(2)}) collective-permute-start(bf16[128,256]{1,0:T(8,128)(2,1)S(1)} %get-tuple-element.101.grad0), channel_id=1, source_target_pairs={{0,2},{1,3},{2,0},{3,1},{4,6},{5,7},{6,4},{7,5},{8,10},{9,11},{10,... | collective-permute-start | bytes 196616 | tf_op jit(solution)/shard_map/ppermute | solution.py:656
  60.9 3.8 %collective-permute-start.11 = (bf16[128,256]{1,0:T(8,128)(2,1)S(1)}, bf16[128,256]{1,0:T(8,128)(2,1)S(1)}, u32[]{:S(2)}, u32[]{:S(2)}) collective-permute-start(bf16[128,256]{1,0:T(8,128)(2,1)S(1)} %get-tuple-element.101.grad0), channel_id=1, source_target_pairs={{0,3},{1,0},{2,1},{3,2},{4,7},{5,4},{6,5},{7,6},{8,11},{9,8},{10,9... | collective-permute-start | bytes 196616 | tf_op jit(solution)/shard_map/ppermute | solution.py:656
  61.8 5.2 %collective-permute-start.12 = (bf16[128,256]{1,0:T(8,128)(2,1)S(1)}, bf16[128,256]{1,0:T(8,128)(2,1)S(1)}, u32[]{:S(2)}, u32[]{:S(2)}) collective-permute-start(bf16[128,256]{1,0:T(8,128)(2,1)S(1)} %get-tuple-element.101.grad0), channel_id=1, source_target_pairs={{0,1},{1,2},{2,3},{3,0},{4,5},{5,6},{6,7},{7,4},{8,9},{9,10},{10,1... | collective-permute-start | bytes 196616 | tf_op jit(solution)/shard_map/ppermute | solution.py:656
  68.8 7.3 %collective-permute-start.20 = (bf16[16,192,128]{2,1,0:T(8,128)(2,1)S(1)}, bf16[16,192,128]{2,1,0:T(8,128)(2,1)S(1)}, u32[]{:S(2)}, u32[]{:S(2)}) collective-permute-start(bf16[16,192,128]{2,1,0:T(8,128)(2,1)S(1)} %get-tuple-element.107), channel_id=1, source_target_pairs={{0,4},{4,0},{8,12},{12,8},{16,20},{20,16},{24,28},{28,24},{32,36},... | collective-permute-start | bytes 2359304 | tf_op jit(solution)/shard_map/ppermute | solution.py:634
  72.2 6.3 %collective-permute-start.13 = (bf16[3,128,256]{2,1,0:T(8,128)(2,1)S(1)}, bf16[3,128,256]{2,1,0:T(8,128)(2,1)S(1)}, u32[]{:S(2)}, u32[]{:S(2)}) collective-permute-start(bf16[3,128,256]{2,1,0:T(8,128)(2,1)S(1)} %form_messages.1.refs_0_), channel_id=1, source_target_pairs={{0,64},{4,20},{8,72},{12,28},{16,80},{20,4},{24,88},{28,12},{32,96... | collective-permute-start | bytes 589832 | tf_op jit(solution)/shard_map/ppermute | solution.py:630
  73.4 7.3 %collective-permute-start.14 = (bf16[3,128,256]{2,1,0:T(8,128)(2,1)S(1)}, bf16[3,128,256]{2,1,0:T(8,128)(2,1)S(1)}, u32[]{:S(2)}, u32[]{:S(2)}) collective-permute-start(bf16[3,128,256]{2,1,0:T(8,128)(2,1)S(1)} %form_messages.1.refs_0_), channel_id=1, source_target_pairs={{0,32},{4,12},{8,40},{12,20},{16,48},{20,28},{24,56},{28,4},{32,64... | collective-permute-start | bytes 589832 | tf_op jit(solution)/shard_map/ppermute | solution.py:630
  75.2 5.5 %collective-permute-start.15 = (bf16[3,128,256]{2,1,0:T(8,128)(2,1)S(1)}, bf16[3,128,256]{2,1,0:T(8,128)(2,1)S(1)}, u32[]{:S(2)}, u32[]{:S(2)}) collective-permute-start(bf16[3,128,256]{2,1,0:T(8,128)(2,1)S(1)} %form_messages.1.refs_0_), channel_id=1, source_target_pairs={{0,96},{4,28},{8,104},{12,4},{16,112},{20,12},{24,120},{28,20},{32... | collective-permute-start | bytes 589832 | tf_op jit(solution)/shard_map/ppermute | solution.py:630
  76.2 7.2 %collective-permute-start.21 = (bf16[4,192,128]{2,1,0:T(8,128)(2,1)S(1)}, bf16[4,192,128]{2,1,0:T(8,128)(2,1)S(1)}, u32[]{:S(2)}, u32[]{:S(2)}) collective-permute-start(bf16[4,192,128]{2,1,0:T(8,128)(2,1)S(1)} %get-tuple-element.138), channel_id=1, source_target_pairs={{0,16},{4,68},{8,24},{12,76},{16,0},{20,84},{24,8},{28,92},{32,48}... | collective-permute-start | bytes 589832 | tf_op jit(solution)/shard_map/ppermute | solution.py:630
  77.3 6.6 %collective-permute-start.22 = (bf16[4,192,128]{2,1,0:T(8,128)(2,1)S(1)}, bf16[4,192,128]{2,1,0:T(8,128)(2,1)S(1)}, u32[]{:S(2)}, u32[]{:S(2)}) collective-permute-start(bf16[4,192,128]{2,1,0:T(8,128)(2,1)S(1)} %get-tuple-element.137), channel_id=1, source_target_pairs={{0,8},{4,36},{8,16},{12,44},{16,24},{20,52},{24,0},{28,60},{32,40}... | collective-permute-start | bytes 589832 | tf_op jit(solution)/shard_map/ppermute | solution.py:630
  78.5 16.6 %collective-permute-start.23 = (bf16[4,192,128]{2,1,0:T(8,128)(2,1)S(1)}, bf16[4,192,128]{2,1,0:T(8,128)(2,1)S(1)}, u32[]{:S(2)}, u32[]{:S(2)}) collective-permute-start(bf16[4,192,128]{2,1,0:T(8,128)(2,1)S(1)} %get-tuple-element.136), channel_id=1, source_target_pairs={{0,24},{4,100},{8,0},{12,108},{16,8},{20,116},{24,16},{28,124},{32... | collective-permute-start | bytes 589832 | tf_op jit(solution)/shard_map/ppermute | solution.py:630
  80.7 27.7 %collective-permute-start.16 = (bf16[12,128,256]{2,1,0:T(8,128)(2,1)S(1)}, bf16[12,128,256]{2,1,0:T(8,128)(2,1)S(1)}, u32[]{:S(2)}, u32[]{:S(2)}) collective-permute-start(bf16[12,128,256]{2,1,0:T(8,128)(2,1)S(1)} %join_blocks.1.own0), channel_id=1, source_target_pairs={{0,16},{4,68},{8,24},{12,76},{16,0},{20,84},{24,8},{28,92},{32,48}... | collective-permute-start | bytes 2359304 | tf_op jit(solution)/shard_map/ppermute | solution.py:630
  82.5 25.9 %collective-permute-start.17 = (bf16[12,128,256]{2,1,0:T(8,128)(2,1)S(1)}, bf16[12,128,256]{2,1,0:T(8,128)(2,1)S(1)}, u32[]{:S(2)}, u32[]{:S(2)}) collective-permute-start(bf16[12,128,256]{2,1,0:T(8,128)(2,1)S(1)} %join_blocks.1.own0), channel_id=1, source_target_pairs={{0,8},{4,36},{8,16},{12,44},{16,24},{20,52},{24,0},{28,60},{32,40}... | collective-permute-start | bytes 2359304 | tf_op jit(solution)/shard_map/ppermute | solution.py:630
  83.4 25.0 %collective-permute-start.18 = (bf16[12,128,256]{2,1,0:T(8,128)(2,1)S(1)}, bf16[12,128,256]{2,1,0:T(8,128)(2,1)S(1)}, u32[]{:S(2)}, u32[]{:S(2)}) collective-permute-start(bf16[12,128,256]{2,1,0:T(8,128)(2,1)S(1)} %join_blocks.1.own0), channel_id=1, source_target_pairs={{0,24},{4,100},{8,0},{12,108},{16,8},{20,116},{24,16},{28,124},{32... | collective-permute-start | bytes 2359304 | tf_op jit(solution)/shard_map/ppermute | solution.py:630
  83.9 24.4 %collective-permute-start.19 = (bf16[12,128,256]{2,1,0:T(8,128)(2,1)S(1)}, bf16[12,128,256]{2,1,0:T(8,128)(2,1)}, u32[]{:S(2)}, u32[]{:S(2)}) collective-permute-start(bf16[12,128,256]{2,1,0:T(8,128)(2,1)S(1)} %join_blocks.1.own0), channel_id=1, source_target_pairs={{0,4},{4,0},{8,12},{12,8},{16,20},{20,16},{24,28},{28,24},{32,36},... | collective-permute-start | bytes 2359304 | tf_op jit(solution)/shard_map/ppermute | solution.py:634
  95.2 5.0 %collective-permute-start.24 = (bf16[192,128]{1,0:T(8,128)(2,1)S(1)}, bf16[192,128]{1,0:T(8,128)(2,1)S(1)}, u32[]{:S(2)}, u32[]{:S(2)}) collective-permute-start(bf16[192,128]{1,0:T(8,128)(2,1)S(1)} %get-tuple-element.141), channel_id=1, source_target_pairs={{0,64},{4,20},{8,72},{12,28},{16,80},{20,4},{24,88},{28,12},{32,96... | collective-permute-start | bytes 147464 | tf_op jit(solution)/shard_map/ppermute | solution.py:630
  100.3 5.0 %collective-permute-start.25 = (bf16[192,128]{1,0:T(8,128)(2,1)S(1)}, bf16[192,128]{1,0:T(8,128)(2,1)S(1)}, u32[]{:S(2)}, u32[]{:S(2)}) collective-permute-start(bf16[192,128]{1,0:T(8,128)(2,1)S(1)} %get-tuple-element.140), channel_id=1, source_target_pairs={{0,32},{4,12},{8,40},{12,20},{16,48},{20,28},{24,56},{28,4},{32,64... | collective-permute-start | bytes 147464 | tf_op jit(solution)/shard_map/ppermute | solution.py:630
  105.2 2.9 %collective-permute-start.26 = (bf16[192,128]{1,0:T(8,128)(2,1)S(1)}, bf16[192,128]{1,0:T(8,128)(2,1)S(1)}, u32[]{:S(2)}, u32[]{:S(2)}) collective-permute-start(bf16[192,128]{1,0:T(8,128)(2,1)S(1)} %get-tuple-element.139), channel_id=1, source_target_pairs={{0,96},{4,28},{8,104},{12,4},{16,112},{20,12},{24,120},{28,20},{32... | collective-permute-start | bytes 147464 | tf_op jit(solution)/shard_map/ppermute | solution.py:630
  108.4 8.0 %collective-permute-start.27 = (bf16[12,128,256]{2,1,0:T(8,128)(2,1)S(1)}, bf16[12,128,256]{2,1,0:T(8,128)(2,1)S(1)}, u32[]{:S(2)}, u32[]{:S(2)}) collective-permute-start(bf16[12,128,256]{2,1,0:T(8,128)(2,1)S(1)} %collective-permute-done.16.own2), channel_id=1, source_target_pairs={{0,4},{4,0},{8,12},{12,8},{16,20},{20,16},{24,28},{28,24},{32,36},... | collective-permute-start | bytes 2359304 | tf_op jit(solution)/shard_map/ppermute | solution.py:634
  108.5 8.0 %collective-permute-start.28 = (bf16[12,128,256]{2,1,0:T(8,128)(2,1)S(1)}, bf16[12,128,256]{2,1,0:T(8,128)(2,1)S(1)}, u32[]{:S(2)}, u32[]{:S(2)}) collective-permute-start(bf16[12,128,256]{2,1,0:T(8,128)(2,1)S(1)} %collective-permute-done.17.own3), channel_id=1, source_target_pairs={{0,4},{4,0},{8,12},{12,8},{16,20},{20,16},{24,28},{28,24},{32,36},... | collective-permute-start | bytes 2359304 | tf_op jit(solution)/shard_map/ppermute | solution.py:634
  109.0 7.5 %collective-permute-start.29 = (bf16[12,128,256]{2,1,0:T(8,128)(2,1)S(1)}, bf16[12,128,256]{2,1,0:T(8,128)(2,1)S(1)}, u32[]{:S(2)}, u32[]{:S(2)}) collective-permute-start(bf16[12,128,256]{2,1,0:T(8,128)(2,1)S(1)} %collective-permute-done.18.own1), channel_id=1, source_target_pairs={{0,4},{4,0},{8,12},{12,8},{16,20},{20,16},{24,28},{28,24},{32,36},... | collective-permute-start | bytes 2359304 | tf_op jit(solution)/shard_map/ppermute | solution.py:634
